TPU v7x, 32 devices: a whole 2x2x4 slice. The times are simulated.
32 devices in a mesh: grp: 4 (over z), row: 2 (over x), col: 4 (over y, core).
Axes of the slice: x: 2, y: 2, z: 4, core: 2. Of those that a mesh axis runs over, the one named last changes fastest.
Arguments:
- child_fronts: float32 [4, 4096, 4096], P('grp', 'row', 'col'), as said below
- parent_entries: float32 [16384, 4, 4096], P(('grp', 'row'), None, 'col'), as said below
- child_live: int32 [4], replicated, may hold values from 2 to 32, as said below
- quarters: int32 [4, 32], replicated, may hold values from 0 to 3, as said below
Outputs:
- parent_front: float32 [16384, 4, 4096], P(('grp', 'row'), None, 'col')
Inputs may be any that keep to these rules, and one draw needn't show every extreme that they name: `child_fronts`: every child front is symmetric and positive definite. `parent_entries`: symmetric and positive definite when read as a matrix of order 16384. `child_live`: one child has all 32 blocks in its structure in every draw. `quarters`: each child's blocks form aligned groups of 16 in a row (blocks 0 to 15, and so on); within one group no quarter is named more than 4 times, and some quarter exactly 4 times.
All inputs are finite; a program needn't handle non-finite values.
Results may differ from a plain program's by a relative error of at most 0.0003.
Values sent between devices are 32-bit elements; how exact they have to be, the bound alone decides.
No kernel may reach another device: no remote copies, remote signals or barrier semaphores. Data moves between devices by JAX's collectives and lax.ppermute only.
A program may use at most 256 MiB of HBM per device.

v0:
```python
import jax
import jax.numpy as jnp
from jax import lax
from jax.sharding import PartitionSpec as P

B = 128
KC = 1
KP = 3
FC = 4096


HIGHEST_MODE = lax.Precision.HIGHEST


def spread(value, axis, source):
    kept = jnp.where(lax.axis_index(axis) == source, value, 0).astype(value.dtype)
    return lax.psum(kept, axis)


def product_nt(left_side, right_side):
    return lax.dot_general(
        left_side,
        right_side,
        (((1,), (1,)), ((), ())),
        precision=HIGHEST_MODE,
        preferred_element_type=jnp.float32,
    )


def block_factors(pivot_block, column_strip, row_strip, row_ids, col_ids, first_index):
    factor = jnp.linalg.cholesky(pivot_block)
    column_part = lax.linalg.triangular_solve(
        factor, column_strip, left_side=False, lower=True, transpose_a=True
    )
    row_part = lax.linalg.triangular_solve(factor, row_strip, left_side=True, lower=True).T
    inside_ids = jnp.arange(pivot_block.shape[0])
    offset = row_ids[:, None] - first_index
    keep_rows = (offset >= pivot_block.shape[0]) | (offset >= 0) & (inside_ids[None, :] <= offset)
    keep_cols = col_ids[:, None] >= first_index
    return (jnp.where(keep_rows, column_part, 0.0), jnp.where(keep_cols, row_part, 0.0))


def child_update(local_front, block_step, row_ids, col_ids):
    rows_here, cols_here = local_front.shape
    first_index = block_step * B
    col_offset = first_index % cols_here
    row_offset = first_index % rows_here
    column_strip = spread(
        local_front[:, col_offset : col_offset + B], "col", first_index // cols_here
    )
    payload = jnp.concatenate(
        [local_front[row_offset : row_offset + B, :], column_strip[row_offset : row_offset + B, :]],
        axis=1,
    )
    payload = spread(payload, "row", first_index // rows_here)
    column_part, row_part = block_factors(
        payload[:, cols_here:], column_strip, payload[:, :cols_here], row_ids, col_ids, first_index
    )
    return local_front - product_nt(column_part, row_part)


def raw_strips(parent_front, block_step, cols_quarter):
    first_index = block_step * B
    col_offset = first_index % cols_quarter
    row_offset = first_index % parent_front.shape[0]
    return (
        parent_front[:, col_offset : col_offset + B],
        parent_front[row_offset : row_offset + B, :],
    )


def parent_factors(parent_front, column_raw, row_raw, block_step, row_ids, col_ids, cols_quarter):
    rows_here = parent_front.shape[0]
    first_index = block_step * B
    row_offset = first_index % rows_here
    column_strip = spread(column_raw, "col", first_index // cols_quarter)
    payload = jnp.concatenate([row_raw, column_strip[row_offset : row_offset + B, :]], axis=1)
    payload = spread(payload, ("grp", "row"), first_index // rows_here)
    strip_width = row_raw.shape[1]
    return block_factors(
        payload[:, strip_width:],
        column_strip,
        payload[:, :strip_width],
        row_ids,
        col_ids,
        first_index,
    )


def place_column(parent_front, column_part, block_step, col_pos, cols_quarter):
    first_index = block_step * B
    col_offset = first_index % cols_quarter
    is_owner = col_pos == first_index // cols_quarter
    current_values = lax.dynamic_slice_in_dim(parent_front, col_offset, B, 1)
    return lax.dynamic_update_slice_in_dim(
        parent_front, jnp.where(is_owner, column_part, current_values), col_offset, 1
    )


def slot_table(quarter_list, quarter_count, slot_count):
    list_size = quarter_list.shape[-1]
    order_ids = jnp.arange(list_size)
    earlier_same = (quarter_list[..., :, None] == quarter_list[..., None, :]) & (
        order_ids[None, :] < order_ids[:, None]
    )
    rank_ids = jnp.sum(earlier_same.astype(jnp.int32), axis=-1)
    to_quarter = quarter_list[..., None, None, :] == jnp.arange(quarter_count)[:, None, None]
    to_slot = rank_ids[..., None, None, :] == jnp.arange(slot_count)[None, :, None]
    return (to_quarter & to_slot).astype(jnp.float32)


def shards(child_fronts, parent_entries, child_live, quarters):
    local_front = child_fronts[0]
    rows_here, cols_here = local_front.shape
    groups = lax.axis_size("grp")
    group_id = lax.axis_index("grp")
    row_pos = lax.axis_index("row")
    col_pos = lax.axis_index("col")
    row_ids = row_pos * rows_here + jnp.arange(rows_here)
    col_ids = col_pos * cols_here + jnp.arange(cols_here)
    block_step = 0
    local_front = child_update(local_front, block_step, row_ids, col_ids)
    member = jnp.arange(groups) == group_id
    live_end = jnp.sum(jnp.where(member, child_live, 0)) * B
    live_rows = (row_ids >= KC * B) & (row_ids < live_end)
    live_cols = (col_ids >= KC * B) & (col_ids < live_end)
    contribution = jnp.where(live_rows[:, None] & live_cols[None, :], local_front, 0.0)
    row_blocks = rows_here // B
    col_blocks = cols_here // B
    row_quarters = lax.dynamic_slice_in_dim(quarters, row_pos * row_blocks, row_blocks, 1)
    col_quarters = lax.dynamic_slice_in_dim(quarters, col_pos * col_blocks, col_blocks, 1)
    col_lanes = jnp.repeat(col_quarters, B, axis=1)
    quarter_ids = jnp.arange(groups)
    col_select = (col_lanes[:, None, :] == quarter_ids[None, :, None]).astype(jnp.float32)
    slot_count = max(1, row_blocks // groups)
    own_quarters = jnp.sum(jnp.where(member[:, None], row_quarters, 0), axis=0)
    send_table = slot_table(own_quarters, groups, slot_count)
    outgoing = jnp.einsum(
        "dsb,bpw->dspw",
        send_table,
        contribution.reshape(row_blocks, B, cols_here),
        precision=HIGHEST_MODE,
    )
    incoming = lax.all_to_all(
        outgoing.reshape(groups, slot_count * B, cols_here),
        "grp",
        split_axis=0,
        concat_axis=0,
        tiled=True,
    )
    all_tables = slot_table(row_quarters, groups, slot_count)
    back_table = jnp.sum(jnp.where(member[None, :, None, None], all_tables, 0.0), axis=1)
    arrived = jnp.einsum(
        "gsb,gspw->gbpw",
        back_table,
        incoming.reshape(groups, slot_count, B, cols_here),
        precision=HIGHEST_MODE,
    )
    arrived = arrived.reshape(groups, rows_here, cols_here)
    added_part = jnp.sum(arrived[:, :, None, :] * col_select[:, None, :, :], axis=0)
    prow_count = parent_entries.shape[0]
    quarter_count = parent_entries.shape[1]
    parent_front = (parent_entries + added_part).reshape(prow_count, quarter_count * cols_here)
    prow_ids = (group_id * lax.axis_size("row") + row_pos) * prow_count + jnp.arange(prow_count)
    pcol_ids = (
        quarter_ids[:, None] * FC + col_pos * cols_here + jnp.arange(cols_here)[None, :]
    ).reshape(-1)
    for block_step in range(KP):
        column_raw, row_raw = raw_strips(parent_front, block_step, cols_here)
        column_part, row_part = parent_factors(
            parent_front, column_raw, row_raw, block_step, prow_ids, pcol_ids, cols_here
        )
        parent_front = parent_front - product_nt(column_part, row_part)
        parent_front = place_column(parent_front, column_part, block_step, col_pos, cols_here)
    upper_part = (prow_ids[:, None] < KP * B) & (pcol_ids[None, :] >= KP * B)
    parent_front = jnp.where(upper_part, 0.0, parent_front)
    return parent_front.reshape(prow_count, quarter_count, cols_here)


def solution(mesh):
    in_specs = (P("grp", "row", "col"), P(("grp", "row"), None, "col"), P(), P())
    out_specs = P(("grp", "row"), None, "col")
    return jax.shard_map(shards, mesh=mesh, in_specs=in_specs, out_specs=out_specs, check_vma=False)
```

profile of v0, /device:TPU:0, one launch (start us, length us, event | category | flops | bytes accessed | tf_op | source)
XLA Modules:
  0.0 1264.4 jit_solution(2288392207332268457)
XLA Ops:
  6.5 9.1 copy.36
  15.7 2.4 slice_select_fusion.6
  19.5 1.1 slice_bitcast_fusion
  20.6 36.7 %all-reduce.9.cloned.1.call-done = f32[2048,128]{0,1:T(8,128)} async-done(((f32[2048,128]{0,1:T(8,128)}), f32[2048,128]{0,1:T(8,128)}) %all-reduce.9.cloned.1.call-update) | async-done | bytes 1048592 | tf_op jit(solution)/shard_map/psum | solution.py:17
  58.1 0.9 maximum_select_fusion.3
  59.3 30.8 %all-reduce.11.cloned.1.call-done = f32[128,1152]{0,1:T(8,128)} async-done(((f32[128,1152]{0,1:T(8,128)}), f32[128,1152]{0,1:T(8,128)}) %all-reduce.11.cloned.1.call-update) | async-done | bytes 589840 | tf_op jit(solution)/shard_map/psum | solution.py:17
  91.1 0.9 fusion.38
  91.9 11.7 cholesky.74
  104.8 9.8 custom-call.17
  114.7 1.6 convolution_select_fusion.3
  116.3 2.4 fusion.7
  118.7 10.2 select_bitcast_fusion
  128.9 5.4 copy.61
  134.2 9.2 copy.40
  143.4 10.4 fusion
  153.8 8.3 copy.41
  162.1 5.7 all-to-all-start
  168.3 182.6 %all-to-all-done = f32[4,512,1024]{2,1,0:T(8,128)} async-done(((f32[4,512,1024]{2,1,0:T(8,128)}), f32[4,512,1024]{2,1,0:T(8,128)}, u32[]{:S(2)}, u32[]{:S(2)}) %all-to-all-start) | async-done | bytes 8388640 | tf_op jit(solution)/shard_map/all_to_all | solution.py:144
  350.9 38.6 %fusion.2 = f32[4,16,128,1024]{3,1,2,0:T(8,128)} fusion(f32[4,4,128,1024]{3,2,1,0:T(8,128)} %bitcast.14, f32[4,4,16]{2,1,0:T(4,128)S(1)} %select_reduce_fusion.4), kind=kOutput, calls=%fused_computation.8 | convolution fusion | flops 402653184 | bytes 41944064 | tf_op jit(solution)/shard_map/gsb,gspw->gbpw/dot_general | solution.py:153
  389.5 31.9 %copy.43 = f32[4,16,128,1024]{3,2,1,0:T(8,128)} copy(f32[4,16,128,1024]{3,1,2,0:T(8,128)} %fusion.2) | data formatting | bytes 67108864 | tf_op jit(solution)/shard_map/gsb,gspw->gbpw/dot_general | solution.py:153
  421.5 66.7 %multiply_reduce_fusion = f32[2048,4,1024]{2,0,1:T(8,128)} fusion(f32[4,4,1024]{2,1,0:T(4,128)S(1)} %fusion.39, f32[4,2048,1024]{2,1,0:T(8,128)} %bitcast.136), kind=kLoop, calls=%fused_computation | loop fusion | flops 58720256 | bytes 67174400 | tf_op jit(solution)/shard_map/reduce_sum | solution.py:160
  488.1 41.2 %copy_add_fusion = f32[2048,4,1024]{2,0,1:T(8,128)} fusion(f32[2048,4,1024]{2,0,1:T(8,128)} %multiply_reduce_fusion, f32[2048,4,1024]{2,1,0:T(4,128)} %param.10), kind=kLoop, calls=%fused_computation.1 | loop fusion | flops 8388608 | bytes 100663296 | tf_op jit(solution)/shard_map/add | solution.py:163
  529.3 33.7 %copy.45 = f32[2048,4,1024]{0,2,1:T(8,128)} copy(f32[2048,4,1024]{2,0,1:T(8,128)} %copy_add_fusion) | data formatting | bytes 67108864 | tf_op jit(solution)/shard_map/add | solution.py:163
  563.0 2.5 slice_select_fusion.5
  565.6 1.9 copy.46
  567.4 32.7 %all-reduce.13.cloned.1.call-done = f32[2048,128]{0,1:T(8,128)} async-done(((f32[2048,128]{0,1:T(8,128)}), f32[2048,128]{0,1:T(8,128)}) %all-reduce.13.cloned.1.call-update) | async-done | bytes 1048592 | tf_op jit(solution)/shard_map/psum | solution.py:17
  600.1 0.9 slice.104
  601.0 3.1 maximum_select_fusion
  604.7 103.5 %all-reduce.15.cloned.1.call-done = f32[128,4224]{0,1:T(8,128)} async-done(((f32[128,4224]{0,1:T(8,128)}), f32[128,4224]{0,1:T(8,128)}) %all-reduce.15.cloned.1.call-update) | async-done | bytes 2162704 | tf_op jit(solution)/shard_map/psum | solution.py:17
  709.2 0.9 fusion.35
  710.0 11.7 cholesky.85
  723.1 9.8 custom-call.18
  732.9 3.6 convolution_select_fusion.2
  736.5 1.2 fusion.6
  737.7 33.1 %convolution_subtract_fusion.2 = f32[2048,4096]{0,1:T(8,128)} fusion(f32[2048,4096]{0,1:T(8,128)} %bitcast.134, f32[2048,128]{0,1:T(8,128)S(1)} %fusion.6, f32[128,4096]{1,0:T(8,128)S(1)} %convolution_select_fusion.2), kind=kOutput, calls=%fused_computation.5 | convolution fusion | flops 12893290496 | bytes 70254592 | tf_op jit(solution)/shard_map/dot_general | solution.py:21
  770.8 2.3 fusion.13
  773.1 2.4 slice_select_fusion.3
  775.6 1.7 slice.107
  777.3 33.9 %all-reduce.17.cloned.1.call-done = f32[2048,128]{0,1:T(8,128)} async-done(((f32[2048,128]{0,1:T(8,128)}), f32[2048,128]{0,1:T(8,128)}) %all-reduce.17.cloned.1.call-update) | async-done | bytes 1048592 | tf_op jit(solution)/shard_map/psum | solution.py:17
  811.2 0.9 slice.109
  812.1 1.5 maximum_select_fusion.1
  813.8 104.9 %all-reduce.19.cloned.1.call-done = f32[128,4224]{0,1:T(8,128)} async-done(((f32[128,4224]{0,1:T(8,128)}), f32[128,4224]{0,1:T(8,128)}) %all-reduce.19.cloned.1.call-update) | async-done | bytes 2162704 | tf_op jit(solution)/shard_map/psum | solution.py:17
  919.6 0.9 fusion.32
  920.4 11.7 cholesky.96
  933.4 9.8 custom-call.20
  943.2 3.6 convolution_select_fusion.1
  946.7 1.2 fusion.5
  947.9 33.2 %convolution_subtract_fusion.1 = f32[2048,4096]{0,1:T(8,128)} fusion(f32[2048,4096]{0,1:T(8,128)} %fusion.13, f32[2048,128]{0,1:T(8,128)S(1)} %fusion.5, f32[128,4096]{1,0:T(8,128)S(1)} %convolution_select_fusion.1), kind=kOutput, calls=%fused_computation.4 | convolution fusion | flops 12893290496 | bytes 70254592 | tf_op jit(solution)/shard_map/dot_general | solution.py:21
  981.1 2.3 fusion.12
  983.4 2.4 slice_select_fusion.1
  985.9 1.7 slice.112
  987.6 33.9 %all-reduce.21.cloned.1.call-done = f32[2048,128]{0,1:T(8,128)} async-done(((f32[2048,128]{0,1:T(8,128)}), f32[2048,128]{0,1:T(8,128)}) %all-reduce.21.cloned.1.call-update) | async-done | bytes 1048592 | tf_op jit(solution)/shard_map/psum | solution.py:17
  1021.5 0.9 slice.114
  1022.5 1.5 maximum_select_fusion.2
  1024.1 105.0 %all-reduce.23.cloned.1.call-done = f32[128,4224]{0,1:T(8,128)} async-done(((f32[128,4224]{0,1:T(8,128)}), f32[128,4224]{0,1:T(8,128)}) %all-reduce.23.cloned.1.call-update) | async-done | bytes 2162704 | tf_op jit(solution)/shard_map/psum | solution.py:17
  1130.0 0.9 fusion.29
  1130.9 11.7 cholesky.107
  1143.8 9.8 custom-call.22
  1153.6 3.6 convolution_select_fusion
  1157.2 1.2 fusion.4
  1158.4 33.2 %convolution_subtract_fusion = f32[2048,4096]{0,1:T(8,128)} fusion(f32[2048,4096]{0,1:T(8,128)} %fusion.12, f32[2048,128]{0,1:T(8,128)S(1)} %fusion.4, f32[128,4096]{1,0:T(8,128)S(1)} %convolution_select_fusion), kind=kOutput, calls=%fused_computation.3 | convolution fusion | flops 12893290496 | bytes 70254592 | tf_op jit(solution)/shard_map/dot_general | solution.py:21
  1191.6 2.3 fusion.11
  1193.9 23.6 %and_select_fusion = f32[2048,4096]{0,1:T(8,128)} fusion(f32[2048,4096]{0,1:T(8,128)} %fusion.11, pred[2048]{0:T(1024)(128)(4,1)S(1)} %fusion.56, pred[4096]{0:T(1024)(128)(4,1)S(1)} %bitcast.142), kind=kLoop, calls=%fused_computation.2 | loop fusion | flops 16777216 | bytes 67115008 | tf_op jit(solution)/shard_map/jit(_where)/select_n | solution.py:176
  1217.5 39.6 %copy.53 = f32[2048,4,1024]{2,1,0:T(4,128)} copy(f32[2048,4,1024]{0,2,1:T(8,128)} %bitcast.135) | data formatting | bytes 67108864 | tf_op jit(solution)/shard_map/reshape | solution.py:177
  (79 shorter events, 12.0 us)
Async XLA Ops:
  6.5 50.7 %all-reduce.9.cloned.1.call-start = ((), (), s32[]{:S(2)}) async-start(), calls=%async_computation.1 | async-start | bytes 2097152 | tf_op jit(solution)/shard_map/psum | solution.py:17
  6.5 11.6 copy-start.4
  6.5 52.4 %copy-start.3 = (s32[4,32]{1,0:T(4,128)S(1)}, s32[4,32]{1,0:T(4,128)}, u32[]{:S(2)}) copy-start(s32[4,32]{1,0:T(4,128)} %param.12) | copy-start | bytes 1540
  18.1 72.0 %all-reduce.11.cloned.1.call-start = ((), (), s32[]{:S(2)}) async-start(), calls=%async_computation.2 | async-start | bytes 1179648 | tf_op jit(solution)/shard_map/psum | solution.py:17
  162.1 188.9 %all-to-all-start = ((f32[4,512,1024]{2,1,0:T(8,128)}), f32[4,512,1024]{2,1,0:T(8,128)}, u32[]{:S(2)}, u32[]{:S(2)}) async-start(f32[4,512,1024]{2,1,0:T(8,128)} %bitcast.138), calls=%async_computation | async-start | bytes 16777216 | tf_op jit(solution)/shard_map/all_to_all | solution.py:144
  167.7 432.3 %all-reduce.13.cloned.1.call-start = ((), (), s32[]{:S(2)}) async-start(), calls=%async_computation.3 | async-start | bytes 2097152 | tf_op jit(solution)/shard_map/psum | solution.py:17
  563.0 2.6 slice-start
  565.5 142.7 %all-reduce.15.cloned.1.call-start = ((), (), s32[]{:S(2)}) async-start(), calls=%async_computation.4 | async-start | bytes 4325376 | tf_op jit(solution)/shard_map/psum | solution.py:17
  600.1 136.4 %copy-start = (f32[2048,128]{0,1:T(8,128)S(1)}, f32[2048,128]{0,1:T(8,128)}, u32[]{:S(2)}) copy-start(f32[2048,128]{0,1:T(8,128)} %all-reduce.13.cloned.1.call-done) | copy-start | bytes 3145732
  604.1 207.1 %all-reduce.17.cloned.1.call-start = ((), (), s32[]{:S(2)}) async-start(), calls=%async_computation.5 | async-start | bytes 2097152 | tf_op jit(solution)/shard_map/psum | solution.py:17
  775.5 143.1 %all-reduce.19.cloned.1.call-start = ((), (), s32[]{:S(2)}) async-start(), calls=%async_computation.6 | async-start | bytes 4325376 | tf_op jit(solution)/shard_map/psum | solution.py:17
  811.2 135.5 %copy-start.2 = (f32[2048,128]{0,1:T(8,128)S(1)}, f32[2048,128]{0,1:T(8,128)}, u32[]{:S(2)}) copy-start(f32[2048,128]{0,1:T(8,128)} %all-reduce.17.cloned.1.call-done) | copy-start | bytes 3145732
  813.7 207.9 %all-reduce.21.cloned.1.call-start = ((), (), s32[]{:S(2)}) async-start(), calls=%async_computation.7 | async-start | bytes 2097152 | tf_op jit(solution)/shard_map/psum | solution.py:17
  985.8 143.3 %all-reduce.23.cloned.1.call-start = ((), (), s32[]{:S(2)}) async-start(), calls=%async_computation.8 | async-start | bytes 4325376 | tf_op jit(solution)/shard_map/psum | solution.py:17
  1021.5 135.7 %copy-start.1 = (f32[2048,128]{0,1:T(8,128)S(1)}, f32[2048,128]{0,1:T(8,128)}, u32[]{:S(2)}) copy-start(f32[2048,128]{0,1:T(8,128)} %all-reduce.21.cloned.1.call-done) | copy-start | bytes 3145732
Sparse Core Ops, SparseCore 0:
  18.2 38.9 all-reduce.8
  59.5 30.5 all-reduce.10
  565.6 34.4 all-reduce.12
  604.2 103.9 all-reduce.14
  775.6 35.5 all-reduce.16
  814.6 103.9 all-reduce.18
  985.9 35.5 all-reduce.20
  1025.1 103.9 all-reduce.22
where the time goes:
time: 1270 us; the launch traced here: 1260 us
  waiting for transfers between devices  664 us (52%)
  other arithmetic  251 us (20%)
  matrix products  177 us (14%)
  local copies, waits for them, and re-layouts  151 us (12%)
  between operations  15 us (1%)
    psum x8, waiting for transfers between devices, spread(): return lax.psum(kept, axis)  481 us
    all_to_all x1, waiting for transfers between devices, shards(): lax.all_to_all(outgoing.reshape(groups, slot_count * B, cols_here), 'grp'...  183 us
    dot_general x4, matrix products, product_nt(): lax.dot_general(left_side, right_side, (((1,), (1,)), ((), ())), precisio...  110 us
    reduce_sum x1, other arithmetic, shards(): jnp.sum(arrived[:, :, None, :] * col_select[:, None, :, :], axis=0)  66.7 us
    another operation x12, other arithmetic, block_factors(): factor = jnp.linalg.cholesky(pivot_block)  49.5 us
    another operation x8, other arithmetic, block_factors(): lax.linalg.triangular_solve(factor, column_strip, left_side=False, lower=...  41.6 us
    add x1, other arithmetic, shards(): parent_entries + added_part  41.2 us
    reshape x1, local copies, waits for them, and re-layouts, shards(): return parent_front.reshape(prow_count, quarter_count, cols_here)  39.6 us
  transfers between devices with their start and end apart: 9, of which 9 were waited for; matrix products, arithmetic and copies ran while one was open for 1% of the time, Pallas kernels for 0%

commit v1 on v0

v1 whole, which is shorter than its diff:
```python
import functools

import jax
import jax.numpy as jnp
from jax import lax
from jax.experimental import pallas as pl
from jax.experimental.pallas import tpu as pltpu
from jax.sharding import PartitionSpec as P

B = 128
KC = 1
KP = 3
FC = 4096
LEAD = KC * B
PIV = KP * B
HIGHEST = lax.Precision.HIGHEST
VMEM_LIMIT = 60 * 1024 * 1024


def dot_nn(a, b, precision=HIGHEST):
    return lax.dot_general(a, b, (((1,), (0,)), ((), ())), precision=precision, preferred_element_type=jnp.float32)


def dot_nt(a, b, precision=HIGHEST):
    return lax.dot_general(a, b, (((1,), (1,)), ((), ())), precision=precision, preferred_element_type=jnp.float32)


def dot_bf(a, b):
    return lax.dot_general(a, b, (((1,), (0,)), ((), ())), preferred_element_type=jnp.float32)


def split(x):
    hi = x.astype(jnp.bfloat16)
    lo = (x - hi.astype(jnp.float32)).astype(jnp.bfloat16)
    return hi, lo


def vmem():
    return pl.BlockSpec(memory_space=pltpu.VMEM)


def smem():
    return pl.BlockSpec(memory_space=pltpu.SMEM)


def invert_factor(block, aug):
    n = block.shape[0]
    rows = lax.broadcasted_iota(jnp.int32, (n, n), 0)
    cols = lax.broadcasted_iota(jnp.int32, (n, n), 1)
    row_ids = lax.broadcasted_iota(jnp.int32, (n, 1), 0)
    lane_ids = lax.broadcasted_iota(jnp.int32, (1, n), 1)
    aug[:, :n] = block
    aug[:, n:] = jnp.where(rows == cols, 1.0, 0.0).astype(jnp.float32)

    def step(k, pivots):
        pivot_row = aug[pl.ds(k, 1), :]
        pivot = jnp.sum(jnp.where(lane_ids == k, pivot_row[:, :n], 0.0), axis=1, keepdims=True)
        body = aug[...]
        column = jnp.sum(jnp.where(cols == k, body[:, :n], 0.0), axis=1, keepdims=True)
        factor = jnp.where(row_ids > k, column / pivot, 0.0)
        aug[...] = body - factor * pivot_row
        return jnp.where(row_ids == k, pivot, pivots)

    pivots = lax.fori_loop(0, n, step, jnp.ones((n, 1), jnp.float32))
    return aug[:, n:] / jnp.sqrt(pivots)


def child_kernel(pos, live, quarters, block, strip, prow, lead_rows, brow3, bcol3, panel, aug, brow):
    rows_here, cols_here = strip.shape[0], prow.shape[1]
    grp, row, col = pos[0], pos[1], pos[2]
    live_end = live[grp] * B
    inverse = invert_factor(block[...], aug)
    row_ids = row * rows_here + lax.broadcasted_iota(jnp.int32, (rows_here, 1), 0)
    col_ids = col * cols_here + lax.broadcasted_iota(jnp.int32, (1, cols_here), 1)
    live_rows = (row_ids >= LEAD) & (row_ids < live_end)
    live_cols = (col_ids >= LEAD) & (col_ids < live_end)
    brow[...] = jnp.where(live_rows, dot_nt(strip[...], inverse), 0.0)
    bcol = jnp.where(live_cols, dot_nn(inverse, prow[...]), 0.0)
    hi, lo = split(brow[...])
    brow3[:, :LEAD] = hi
    brow3[:, LEAD : 2 * LEAD] = hi
    brow3[:, 2 * LEAD :] = lo
    hi, lo = split(bcol)
    bcol3[:LEAD] = hi
    bcol3[LEAD : 2 * LEAD] = lo
    bcol3[2 * LEAD :] = hi
    for k in range(KC, KP):
        at = (k - KC) * B
        keep = live_cols & (k * B < live_end) & (quarters[grp, k] == 0)
        update = dot_nn(brow[k * B : (k + 1) * B, :], bcol)
        panel[at : at + B, :] = jnp.where(keep, lead_rows[at : at + B, :] - update, 0.0)


def outgoing_kernel(pos, live, quarters, front, brow3, bcol3, out, gathered, picked):
    rows_here, cols_here = front.shape
    row_blocks = rows_here // B
    slots = out.shape[1] // B
    grp, row, col = pos[0], pos[1], pos[2]
    live_end = live[grp] * B
    target = pl.program_id(0)

    def pick(b, count):
        hit = quarters[grp, row * row_blocks + b] == target

        @pl.when(hit & (count < slots))
        def _():
            picked[count] = b

        return count + hit.astype(jnp.int32)

    lax.fori_loop(0, row_blocks, pick, jnp.int32(0))
    for s in range(slots):
        at = pl.multiple_of(picked[s] * B, B)
        gathered[s * B : (s + 1) * B, :] = brow3[pl.ds(at, B), :]
    width = min(256, cols_here)
    for n in range(cols_here // width):
        cut = slice(n * width, (n + 1) * width)
        product = dot_bf(gathered[...], bcol3[:, cut])
        col_ids = col * cols_here + n * width + lax.broadcasted_iota(jnp.int32, (1, width), 1)
        live_cols = (col_ids >= LEAD) & (col_ids < live_end)
        for s in range(slots):
            at = pl.multiple_of(picked[s] * B, B)
            first = row * rows_here + at
            keep = live_cols & (first >= LEAD) & (first < live_end)
            value = front[pl.ds(at, B), cut] - product[s * B : (s + 1) * B]
            out[0, s * B : (s + 1) * B, cut] = jnp.where(keep, value, 0.0)


def head_kernel(head, inverse, work, factor, aug):
    work[...] = head[...]
    inverse[...] = jnp.zeros_like(inverse)
    for k in range(KP):
        kk = slice(k * B, (k + 1) * B)
        diag = invert_factor(work[kk, kk], aug)
        inverse[kk, kk] = diag
        for i in range(k + 1, KP):
            ii = slice(i * B, (i + 1) * B)
            factor[ii, kk] = dot_nt(work[ii, kk], diag)
        for i in range(k + 1, KP):
            for j in range(k + 1, i + 1):
                ii, jj = slice(i * B, (i + 1) * B), slice(j * B, (j + 1) * B)
                work[ii, jj] = work[ii, jj] - dot_nt(factor[ii, kk], factor[jj, kk])
        for j in range(k):
            jj = slice(j * B, (j + 1) * B)
            total = jnp.zeros((B, B), jnp.float32)
            for i in range(j, k):
                ii = slice(i * B, (i + 1) * B)
                total = total + dot_nn(factor[kk, ii], inverse[ii, jj])
            inverse[kk, jj] = -dot_nn(diag, total)


def columns_kernel(pos, quarters, inverse, entries, panels, lc3, mine, placed):
    groups, _, cols_here = panels.shape
    col_blocks = cols_here // B
    grp, col = pos[0], pos[2]
    quarter = pl.program_id(0)
    placed[...] = jnp.zeros_like(placed)
    for g in range(groups):
        for b in range(col_blocks):
            cut = slice(b * B, (b + 1) * B)

            @pl.when(quarters[g, col * col_blocks + b] == quarter)
            def _(g=g, cut=cut):
                placed[:, cut] += panels[g, :, cut]

    value = dot_nt(inverse[...], entries[...]) + dot_nn(inverse[:, LEAD:], placed[...])
    hi, lo = split(value)
    lc3[:PIV] = hi
    lc3[PIV : 2 * PIV] = lo
    lc3[2 * PIV :] = hi

    @pl.when(quarter == grp)
    def _():
        mine[...] = value


def rows_kernel(pos, across, lr, lr3):
    height = lr.shape[0]
    value = jnp.transpose(across[...])
    first = pos[3] + pl.program_id(0) * height
    row_ids = first + lax.broadcasted_iota(jnp.int32, (height, PIV), 0)
    inside = lax.broadcasted_iota(jnp.int32, (height, PIV), 1)
    value = jnp.where(inside <= row_ids, value, 0.0)
    lr[...] = value
    hi, lo = split(value)
    lr3[:, :PIV] = hi
    lr3[:, PIV : 2 * PIV] = hi
    lr3[:, 2 * PIV :] = lo


def final_kernel(pos, quarters, arrived, lr, lr3, lc3, entries, out, acc, slot_of):
    groups, _, cols_here = arrived.shape
    height = entries.shape[0]
    pair = entries.shape[1] // groups
    width = pair * B
    row_blocks = slot_of.shape[1]
    blocks = height // B
    grp, row, col, first_row = pos[0], pos[1], pos[2], pos[3]
    rb, p = pl.program_id(0), pl.program_id(1)

    @pl.when((rb == 0) & (p == 0))
    def _():
        for g in range(groups):

            def note(b, count, g=g):
                hit = quarters[g, row * row_blocks + b] == grp
                slot_of[g, b] = jnp.where(hit, count, -1)
                return count + hit.astype(jnp.int32)

            lax.fori_loop(0, row_blocks, note, jnp.int32(0))

    start = pl.multiple_of(p * width, width)
    left = lr3[...]
    for u in range(groups):
        product = dot_bf(left, lc3[:, pl.ds(pl.multiple_of(u * cols_here + start, width), width)])
        for h in range(pair):
            acc[h * groups + u] = -product[:, h * B : (h + 1) * B]

    for g in range(groups):
        for b in range(blocks):
            slot = slot_of[g, rb * blocks + b]

            @pl.when(slot >= 0)
            def _(g=g, b=b, slot=slot):
                at = pl.multiple_of(slot * B, B)
                for h in range(pair):
                    place = quarters[g, col * (cols_here // B) + p * pair + h]
                    value = arrived[g, pl.ds(at, B), pl.ds(pl.multiple_of(start + h * B, B), B)]
                    acc[h * groups + place, b * B : (b + 1) * B, :] += value

    step = 32
    first = first_row + rb * height

    def plain(i, carry):
        at = pl.multiple_of(i * step, step)
        value = jnp.swapaxes(acc[:, pl.ds(at, step), :], 0, 1)
        out[pl.ds(at, step)] = entries[pl.ds(at, step)] + value
        return carry

    begin_col = col * cols_here + start
    special = (first < PIV) | (begin_col < PIV)

    @pl.when(jnp.logical_not(special))
    def _():
        lax.fori_loop(0, height // step, plain, 0)

    @pl.when(special)
    def _():
        row_ids = first + lax.broadcasted_iota(jnp.int32, (height, 1), 0)
        for h in range(pair):
            for u in range(groups):
                here = begin_col + h * B
                is_pivot = (here < PIV) if u == 0 else False
                if u == 0:
                    strip = lr[:, pl.ds(pl.multiple_of(jnp.where(is_pivot, here, 0), B), B)]
                    other = jnp.where(row_ids < PIV, 0.0, acc[h * groups])
                    acc[h * groups] = jnp.where(is_pivot, strip, other)
                else:
                    acc[h * groups + u] = jnp.where(row_ids < PIV, 0.0, acc[h * groups + u])

        def masked(i, carry):
            at = pl.multiple_of(i * step, step)
            value = jnp.swapaxes(acc[:, pl.ds(at, step), :], 0, 1)
            shape = (step, pair * groups, B)
            ids = first + at + lax.broadcasted_iota(jnp.int32, shape, 0)
            which = lax.broadcasted_iota(jnp.int32, shape, 1)
            pivot_col = (which % groups == 0) & (begin_col + (which // groups) * B < PIV)
            keep = (ids >= PIV) & jnp.logical_not(pivot_col)
            out[pl.ds(at, step)] = jnp.where(keep, entries[pl.ds(at, step)], 0.0) + value
            return carry

        lax.fori_loop(0, height // step, masked, 0)


def params(**kw):
    return pltpu.CompilerParams(vmem_limit_bytes=VMEM_LIMIT, **kw)


def bcast(value, axis, size):
    here = lax.axis_index(axis)
    stride = size // 2
    while stride >= 1:
        pairs = [(i, i + stride) for i in range(0, size, 2 * stride)]
        moved = lax.ppermute(value, axis, pairs)
        value = jnp.where(here % (2 * stride) == stride, moved, value)
        stride //= 2
    return value


def shards(child_fronts, parent_entries, child_live, quarters):
    front = child_fronts[0]
    rows_here, cols_here = front.shape
    groups, rows_n, cols_n = (lax.axis_size(a) for a in ("grp", "row", "col"))
    grp, row, col = (lax.axis_index(a) for a in ("grp", "row", "col"))
    row_blocks = rows_here // B
    slots = row_blocks // groups
    spans = rows_here // cols_here
    first_row = (grp * rows_n + row) * rows_here
    ids = jnp.arange(8, dtype=jnp.int32)
    pos = jnp.where(ids == 0, grp, jnp.where(ids == 1, row, jnp.where(ids == 2, col, first_row)))
    pos = pos.astype(jnp.int32)
    f32, bf16 = jnp.float32, jnp.bfloat16
    shape = jax.ShapeDtypeStruct

    own = parent_entries[:, 0, : min(PIV, cols_here)]
    for other in range(1, -(-PIV // cols_here)):
        wide = min(cols_here, PIV - other * cols_here)
        own = jnp.concatenate([own, lax.ppermute(parent_entries[:, 0, :wide], "col", [(other, 0)])], axis=1)
    part = cols_here // rows_n
    piece = jnp.zeros((part, PIV), f32)
    for h in range(spans):
        for r in range(rows_n):
            at = h * cols_here + r * part
            pairs = [(s * cols_n, r * cols_n + s * spans + h) for s in range(rows_n)]
            piece = piece + lax.ppermute(own[at : at + part], ("row", "col"), pairs)
    entries_c = lax.all_gather(piece, ("grp", "row"), tiled=True)

    strip = bcast(front[:, :LEAD], "col", cols_n)
    corner = bcast(front[:LEAD, :LEAD], "col", cols_n)
    payload = bcast(jnp.concatenate([front[:LEAD], corner], axis=1), "row", rows_n)
    brow3, bcol3, panel = pl.pallas_call(
        child_kernel,
        out_shape=(
            shape((rows_here, 3 * LEAD), bf16),
            shape((3 * LEAD, cols_here), bf16),
            shape((PIV - LEAD, cols_here), f32),
        ),
        in_specs=[smem(), smem(), smem(), vmem(), vmem(), vmem(), vmem()],
        out_specs=(vmem(), vmem(), vmem()),
        scratch_shapes=[pltpu.VMEM((LEAD, 2 * LEAD), f32), pltpu.VMEM((rows_here, LEAD), f32)],
        compiler_params=params(),
        name="child",
    )(pos, child_live, quarters, payload[:, cols_here:], strip, payload[:, :cols_here], front[LEAD:PIV])

    head = jnp.zeros((PIV, PIV), f32)
    for other in range(-(-PIV // cols_here)):
        wide = min(cols_here, PIV - other * cols_here)
        mine = (row == 0) & (col == other)
        at = other * cols_here
        which = lax.dynamic_slice_in_dim(quarters, grp, 1, 0)[0, at // B : (at + wide) // B]
        keep = mine & (jnp.repeat(which, B) == 0)
        first = jnp.where(mine & (grp == 0), parent_entries[:PIV, 0, :wide], 0.0)
        added = jnp.where(keep[None, :], panel[:, :wide], 0.0)
        head = head.at[:, at : at + wide].add(first + jnp.pad(added, ((LEAD, 0), (0, 0))))
    head = lax.psum(head, ("grp", "row", "col"))

    share = (PIV - LEAD) // rows_n
    panel_piece = jnp.where(row == 0, panel[:share], 0.0)
    for r in range(1, rows_n):
        panel_piece = panel_piece + lax.ppermute(panel[r * share : (r + 1) * share], "row", [(0, r)])
    panels = lax.all_gather(panel_piece, ("grp", "row"), tiled=True).reshape(groups, PIV - LEAD, cols_here)

    outgoing = pl.pallas_call(
        outgoing_kernel,
        grid=(groups,),
        out_shape=shape((groups, slots * B, cols_here), f32),
        in_specs=[smem(), smem(), smem(), vmem(), vmem(), vmem()],
        out_specs=pl.BlockSpec((1, slots * B, cols_here), lambda d: (d, 0, 0)),
        scratch_shapes=[pltpu.VMEM((slots * B, 3 * LEAD), bf16), pltpu.SMEM((slots,), jnp.int32)],
        compiler_params=params(),
        name="outgoing",
    )(pos, child_live, quarters, front, brow3, bcol3)
    arrived = lax.all_to_all(outgoing, "grp", split_axis=0, concat_axis=0, tiled=True)

    inverse = pl.pallas_call(
        head_kernel,
        out_shape=shape((PIV, PIV), f32),
        in_specs=[vmem()],
        out_specs=vmem(),
        scratch_shapes=[pltpu.VMEM((PIV, PIV), f32), pltpu.VMEM((PIV, PIV), f32), pltpu.VMEM((B, 2 * B), f32)],
        compiler_params=params(),
        cost_estimate=pl.CostEstimate(flops=10**9, bytes_accessed=10**8, transcendentals=0),
        name="head",
    )(head)

    lc3, mine = pl.pallas_call(
        columns_kernel,
        grid=(groups,),
        out_shape=(shape((3 * PIV, groups * cols_here), bf16), shape((PIV, cols_here), f32)),
        in_specs=[
            smem(),
            smem(),
            vmem(),
            pl.BlockSpec((cols_here, PIV), lambda u: (u, 0)),
            vmem(),
        ],
        out_specs=(pl.BlockSpec((3 * PIV, cols_here), lambda u: (0, u)), vmem()),
        scratch_shapes=[pltpu.VMEM((PIV - LEAD, cols_here), f32)],
        compiler_params=params(),
        cost_estimate=pl.CostEstimate(flops=10**10, bytes_accessed=3 * 10**7, transcendentals=0),
        name="columns",
    )(pos, quarters, inverse, entries_c, panels)

    y_n = cols_n // spans
    y_here = (col // spans - row) % y_n
    stride = y_n // 2
    while stride >= 1:
        pairs = []
        for r in range(rows_n):
            for y in range(0, y_n, 2 * stride):
                for k in range(spans):
                    source, target = (r + y) % y_n * spans + k, (r + y + stride) % y_n * spans + k
                    pairs.append((r * cols_n + source, r * cols_n + target))
        moved = lax.ppermute(mine, ("row", "col"), pairs)
        mine = jnp.where(y_here % (2 * stride) == stride, moved, mine)
        stride //= 2
    parts = [mine]
    for k in range(1, spans):
        pairs = [(y * spans + i, y * spans + (i + k) % spans) for y in range(y_n) for i in range(spans)]
        parts.append(lax.ppermute(mine, "col", pairs))
    inner = col % spans
    across = jnp.concatenate(
        [
            functools.reduce(lambda a, k: jnp.where((inner - s) % spans == k, parts[k], a), range(1, spans), parts[0])
            for s in range(spans)
        ],
        axis=1,
    )
    tall = min(256, rows_here)
    lr, lr3 = pl.pallas_call(
        rows_kernel,
        grid=(rows_here // tall,),
        out_shape=(shape((rows_here, PIV), f32), shape((rows_here, 3 * PIV), bf16)),
        in_specs=[smem(), pl.BlockSpec((PIV, tall), lambda i: (0, i))],
        out_specs=(pl.BlockSpec((tall, PIV), lambda i: (i, 0)), pl.BlockSpec((tall, 3 * PIV), lambda i: (i, 0))),
        compiler_params=params(),
        name="rows",
    )(pos, across)

    lanes = cols_here // B
    pair = 2
    tall = min(512, rows_here)
    view = parent_entries.reshape(rows_here, groups, lanes, B).transpose(0, 2, 1, 3).reshape(rows_here, lanes * groups, B)
    result = pl.pallas_call(
        final_kernel,
        grid=(rows_here // tall, lanes // pair),
        out_shape=shape((rows_here, lanes * groups, B), f32),
        in_specs=[
            smem(),
            smem(),
            vmem(),
            pl.BlockSpec((tall, PIV), lambda i, p: (i, 0)),
            pl.BlockSpec((tall, 3 * PIV), lambda i, p: (i, 0)),
            vmem(),
            pl.BlockSpec((tall, pair * groups, B), lambda i, p: (i, p, 0)),
        ],
        out_specs=pl.BlockSpec((tall, pair * groups, B), lambda i, p: (i, p, 0)),
        scratch_shapes=[pltpu.VMEM((pair * groups, tall, B), f32), pltpu.SMEM((groups, row_blocks), jnp.int32)],
        compiler_params=params(),
        name="final",
    )(pos, quarters, arrived, lr, lr3, lc3, view)
    return result.reshape(rows_here, lanes, groups, B).transpose(0, 2, 1, 3).reshape(rows_here, groups, cols_here)


def solution(mesh):
    in_specs = (P("grp", "row", "col"), P(("grp", "row"), None, "col"), P(), P())
    out_specs = P(("grp", "row"), None, "col")
    return jax.shard_map(shards, mesh=mesh, in_specs=in_specs, out_specs=out_specs, check_vma=False)
```

time: 1270 us -> 621 us (0.49)
  waiting for transfers between devices: 664 us -> 380 us
  other arithmetic: 251 us -> 12.5 us
  matrix products: 177 us -> 0 us
  Pallas kernels: 0 us -> 159 us
  local copies, waits for them, and re-layouts: 151 us -> 17.1 us
  starting transfers between devices: 6.36 us -> 36.5 us
    all_to_all x1, waiting for transfers between devices: 183 us -> 0.01 us  [shards(): lax.all_to_all(outgoing, 'grp', split_axis=0, concat_axis=0, tiled=True)]
    psum x8 -> x1, waiting for transfers between devices: 481 us -> 310 us  [shards(): head = lax.psum(head, ('grp', 'row', 'col'))]
    dot_general x6 -> x0, matrix products: 159 us -> none  [the longest x4 110 us: product_nt(): lax.dot_general(left_side, right_side, (((1,), (1,)), ((), ())), precisio...]
    pallas_call x0 -> x6, Pallas kernels: none -> 159 us  [the longest x1 53.1 us: shards(): pl.pallas_call(final_kernel, grid=(rows_here // tall, lanes // pair), out...]
    another operation x20 -> x0, other arithmetic: 91 us -> none  [the longest x12 49.5 us: block_factors(): factor = jnp.linalg.cholesky(pivot_block)]
    ppermute x0 -> x12, waiting for transfers between devices: none -> 70.3 us  [the longest x1 34.2 us: shards(): moved = lax.ppermute(mine, ('row', 'col'), pairs)]
    reduce_sum x6 -> x0, other arithmetic: 67.9 us -> none  [the longest x1 66.7 us: shards(): jnp.sum(arrived[:, :, None, :] * col_select[:, None, :, :], axis=0)]
    reshape x2 -> x0, local copies, waits for them, and re-layouts: 48.8 us -> none  [the longest x1 39.6 us: shards(): return parent_front.reshape(prow_count, quarter_count, cols_here)]
  transfers between devices with their start and end apart: 9 -> 16, of which waited for: 9 -> 9; matrix products, arithmetic and copies ran while one was open for 1% -> 4% of each run, Pallas kernels for 0% -> 14%
where the time goes in v1:
time: 621 us; the launch traced here: 620 us
  waiting for transfers between devices  380 us (61%)
  Pallas kernels  159 us (26%)
  starting transfers between devices  36.5 us (6%)
  local copies, waits for them, and re-layouts  17.1 us (3%)
  between operations  15.2 us (2%)
  other arithmetic  12.5 us (2%)
    psum x1, waiting for transfers between devices, shards(): head = lax.psum(head, ('grp', 'row', 'col'))  310 us
    pallas_call x1, Pallas kernels, shards(): pl.pallas_call(final_kernel, grid=(rows_here // tall, lanes // pair), out...  53.1 us
    pallas_call x1, Pallas kernels, shards(): pl.pallas_call(head_kernel, out_shape=shape((PIV, PIV), f32), in_specs=[v...  45.4 us
    ppermute x1, waiting for transfers between devices, shards(): moved = lax.ppermute(mine, ('row', 'col'), pairs)  34.2 us
    pallas_call x1, Pallas kernels, shards(): pl.pallas_call(columns_kernel, grid=(groups,), out_shape=(shape((3 * PIV,...  23.3 us
    pallas_call x1, Pallas kernels, shards(): pl.pallas_call(child_kernel, out_shape=(shape((rows_here, 3 * LEAD), bf16...  19.2 us
    ppermute x4, waiting for transfers between devices, shards(): piece = piece + lax.ppermute(own[at:at + part], ('row', 'col'), pairs)  17.6 us
    ppermute x5, starting transfers between devices, bcast(): moved = lax.ppermute(value, axis, pairs)  13.1 us
  transfers between devices with their start and end apart: 16, of which 9 were waited for; matrix products, arithmetic and copies ran while one was open for 4% of the time, Pallas kernels for 14%

profile of v1, /device:TPU:0, one launch (start us, length us, event | category | flops | bytes accessed | tf_op | source)
XLA Modules:
  0.0 619.8 jit_solution(14803174372352075657)
XLA Ops:
  7.4 0.8 slice.103
  8.2 4.9 collective-permute-start
  13.1 1.3 slice.105
  14.4 1.4 collective-permute-start.3
  15.8 1.1 slice_bitcast_fusion.1
  16.9 0.7 constant_dynamic-slice_fusion
  17.6 0.0 collective-permute-done
  17.6 0.8 broadcast_select_fusion.6
  18.4 1.3 collective-permute-start.1
  19.8 0.8 collective-permute-done.1
  20.6 0.9 pad_maximum_fusion.1
  21.5 4.2 collective-permute-start.2
  25.7 2.3 collective-permute-done.3
  28.0 1.3 broadcast_select_fusion.3
  29.3 1.4 collective-permute-start.4
  30.7 0.6 compare_select_fusion.2.pos
  31.3 2.1 slice.90
  33.4 0.1 broadcast_bitcast_fusion
  33.4 2.3 slice_bitcast_fusion.lead_rows
  35.8 2.5 collective-permute-done.2
  38.3 0.1 broadcast_select_fusion.5
  38.3 0.6 slice.104.block
  39.0 0.8 slice.106.prow
  39.8 0.0 collective-permute-done.4
  39.8 1.1 broadcast_select_fusion.4.strip
  40.9 19.2 %child.1 = (bf16[2048,384]{1,0:T(8,128)(2,1)}, bf16[384,1024]{1,0:T(8,128)(2,1)}, f32[256,1024]{1,0:T(8,128)}) custom-call(s32[8]{0:T(128)} %compare_select_fusion.2.pos, s32[4]{0:T(128)} %live.3, s32[4,32]{1,0:T(4,128)} %quarters.7, f32[128,128]{1,0:T(8,128)} %slice.104.block, f32[2048,128]{1,0:T(8,128)} %broadcast_select_fusion.4.strip, ...), custom_call_target="tpu_custom_call" | custom-call | tf_op jit(solution)/shard_map/child/pallas_call | solution.py:321
  60.1 1.2 slice.102
  61.3 5.5 collective-permute-start.9
  66.8 1.0 slice_select_fusion
  67.8 0.9 fusion.1
  68.7 0.0 all-reduce.3.cloned.1.call-update
  68.8 0.0 all-gather.5.cloned.1.call-start
  68.8 9.4 %collective-permute-done.9 = f32[128,1024]{1,0:T(8,128)S(1)} collective-permute-done((f32[128,1024]{1,0:T(8,128)S(1)}, f32[128,1024]{1,0:T(8,128)S(1)}, u32[]{:S(2)}, u32[]{:S(2)}) %collective-permute-start.9) | collective-permute-done | bytes 524320 | tf_op jit(solution)/shard_map/ppermute | solution.py:350
  78.2 0.8 select_add_fusion
  79.1 0.0 all-gather.5.cloned.1.call-update
  79.1 0.0 all-gather.3.cloned.1.call-start
  79.1 5.9 fusion.2
  85.0 0.1 copy.26
  85.1 2.5 collective-permute-start.8
  87.6 0.1 copy.29
  87.7 0.7 collective-permute-start.5
  88.4 0.1 copy.27
  88.4 1.3 collective-permute-start.7
  89.8 0.1 copy.28
  89.8 3.9 collective-permute-start.6
  93.8 8.9 %collective-permute-done.8 = f32[512,384]{1,0:T(8,128)S(1)} collective-permute-done((f32[512,384]{1,0:T(8,128)S(1)}, f32[512,384]{1,0:T(8,128)S(1)}, u32[]{:S(2)}, u32[]{:S(2)}) %collective-permute-start.8) | collective-permute-done | bytes 786464 | tf_op jit(solution)/shard_map/ppermute | solution.py:315
  102.7 8.8 %collective-permute-done.6 = f32[512,384]{1,0:T(8,128)S(1)} collective-permute-done((f32[512,384]{1,0:T(8,128)S(1)}, f32[512,384]{1,0:T(8,128)S(1)}, u32[]{:S(2)}, u32[]{:S(2)}) %collective-permute-start.6) | collective-permute-done | bytes 786464 | tf_op jit(solution)/shard_map/ppermute | solution.py:315
  111.4 1.0 add_add_fusion
  112.5 0.0 all-gather.3.cloned.1.call-update
  112.5 10.1 %outgoing.1 = f32[4,512,1024]{2,1,0:T(8,128)} custom-call(s32[8]{0:T(128)} %compare_select_fusion.2.pos, s32[4]{0:T(128)} %live.3, s32[4,32]{1,0:T(4,128)} %quarters.7, f32[2048,1024]{1,0:T(8,128)} %bitcast.41, bf16[2048,384]{1,0:T(8,128)(2,1)} %get-tuple-element.32.brow3, bf16[384,1024]{1,0:T(8,128)(2,1)} %get-tuple-element.33.bcol3), custom_call_target="tpu_custom_call" | custom-call | tf_op jit(solution)/shard_map/outgoing/pallas_call | solution.py:353
  122.5 5.8 all-to-all-start
  128.3 309.6 %all-reduce.3.cloned.1.call-done.head = f32[384,384]{1,0:T(8,128)} async-done(((f32[384,384]{1,0:T(8,128)}), f32[384,384]{1,0:T(8,128)}) %all-reduce.3.cloned.1.call-update) | async-done | bytes 589840 | tf_op jit(solution)/shard_map/psum | solution.py:345
  437.9 45.4 %head.1.inverse = f32[384,384]{1,0:T(8,128)} custom-call(f32[384,384]{1,0:T(8,128)} %all-reduce.3.cloned.1.call-done.head), custom_call_target="tpu_custom_call" | custom-call | flops 1000000000 | bytes 100000000 | tf_op jit(solution)/shard_map/head/pallas_call | solution.py:365
  483.4 23.3 %columns.1 = (bf16[1152,4096]{1,0:T(8,128)(2,1)}, f32[384,1024]{1,0:T(8,128)}) custom-call(s32[8]{0:T(128)} %compare_select_fusion.2.pos, s32[4,32]{1,0:T(4,128)} %quarters.7, f32[384,384]{1,0:T(8,128)} %head.1.inverse, f32[4096,384]{1,0:T(8,128)} %all-gather.3.cloned.1.call-done.entries, f32[4,256,1024]{2,1,0:T(8,128)} %bitcast.46), custom_call_target="tpu_custom_call" | custom-call | flops 10000000000 | bytes 30000000 | tf_op jit(solution)/shard_map/columns/pallas_call | solution.py:376
  506.7 3.5 collective-permute-start.10
  510.2 34.2 %collective-permute-done.10 = f32[384,1024]{1,0:T(8,128)S(1)} collective-permute-done((f32[384,1024]{1,0:T(8,128)}, f32[384,1024]{1,0:T(8,128)S(1)}, u32[]{:S(2)}, u32[]{:S(2)}) %collective-permute-start.10) | collective-permute-done | bytes 1572896 | tf_op jit(solution)/shard_map/ppermute | solution.py:404
  544.4 1.7 broadcast_select_fusion.1
  546.0 0.1 collective-permute-start.11
  546.2 3.4 collective-permute-done.11
  549.5 0.3 broadcast_select_fusion.2
  549.8 2.0 pad_maximum_fusion.across
  551.8 7.5 %rows.1 = (f32[2048,384]{1,0:T(8,128)}, bf16[2048,1152]{1,0:T(8,128)(2,1)}) custom-call(s32[8]{0:T(128)} %compare_select_fusion.2.pos, f32[384,2048]{1,0:T(8,128)} %pad_maximum_fusion.across), custom_call_target="tpu_custom_call" | custom-call | tf_op jit(solution)/shard_map/rows/pallas_call | solution.py:420
  559.3 0.0 all-to-all-done.arrived
  559.3 53.1 %final.1 = f32[2048,32,128]{2,1,0:T(8,128)} custom-call(s32[8]{0:T(128)} %compare_select_fusion.2.pos, s32[4,32]{1,0:T(4,128)} %quarters.7, f32[4,512,1024]{2,1,0:T(8,128)} %all-to-all-done.arrived, f32[2048,384]{1,0:T(8,128)} %get-tuple-element.36.lr, bf16[2048,1152]{1,0:T(8,128)(2,1)} %get-tuple-element.37.lr3, bf16[1152,4096]{1,0:T(8,128)(2,1)} %get-tuple-element.38.lc3, ...), custom_call_target="tpu_custom_call" | custom-call | tf_op jit(solution)/shard_map/final/pallas_call | solution.py:434
  (9 shorter events, 0.0 us)
Async XLA Ops:
  7.4 430.6 %all-reduce.3.cloned.1.call-start = ((), (), s32[]{:S(2)}) async-start(), calls=%async_computation.1 | async-start | bytes 1179648 | tf_op jit(solution)/shard_map/psum | solution.py:345
  8.2 9.4 %collective-permute-start = (f32[128,128]{1,0:T(8,128)S(1)}, f32[128,128]{1,0:T(8,128)S(1)}, u32[]{:S(2)}, u32[]{:S(2)}) collective-permute-start(f32[128,128]{1,0:T(8,128)S(1)} %slice.103), channel_id=1, source_target_pairs={{0,2},{4,6},{8,10},{12,14},{16,18},{20,22},{24,26},{28,30}} | collective-permute-start | bytes 196616 | tf_op jit(solution)/shard_map/ppermute | solution.py:284
  14.4 13.6 %collective-permute-start.3 = (f32[2048,128]{1,0:T(8,128)S(1)}, f32[2048,128]{1,0:T(8,128)S(1)}, u32[]{:S(2)}, u32[]{:S(2)}) collective-permute-start(f32[2048,128]{1,0:T(8,128)S(1)} %slice.105), channel_id=1, source_target_pairs={{0,2},{4,6},{8,10},{12,14},{16,18},{20,22},{24,26},{28,30}} | collective-permute-start | bytes 3145736 | tf_op jit(solution)/shard_map/ppermute | solution.py:284
  18.4 2.2 collective-permute-start.1
  21.5 16.8 %collective-permute-start.2 = (f32[128,1152]{1,0:T(8,128)}, f32[128,1152]{1,0:T(8,128)}, u32[]{:S(2)}, u32[]{:S(2)}) collective-permute-start(f32[128,1152]{1,0:T(8,128)} %pad_maximum_fusion.1), channel_id=1, source_target_pairs={{0,4},{1,5},{2,6},{3,7},{8,12},{9,13},{10,14},{11,15},{16,20},{17,... | collective-permute-start | bytes 1769480 | tf_op jit(solution)/shard_map/ppermute | solution.py:284
  29.3 10.5 %collective-permute-start.4 = (f32[2048,128]{1,0:T(8,128)S(1)}, f32[2048,128]{1,0:T(8,128)S(1)}, u32[]{:S(2)}, u32[]{:S(2)}) collective-permute-start(f32[2048,128]{1,0:T(8,128)S(1)} %broadcast_select_fusion.3), channel_id=1, source_target_pairs={{0,1},{2,3},{4,5},{6,7},{8,9},{10,11},{12,13},{14,15},{16,17},{18,... | collective-permute-start | bytes 3145736 | tf_op jit(solution)/shard_map/ppermute | solution.py:284
  60.1 18.1 %copy-start = (f32[256,1024]{1,0:T(8,128)S(1)}, f32[256,1024]{1,0:T(8,128)}, u32[]{:S(2)}) copy-start(f32[256,1024]{1,0:T(8,128)} %get-tuple-element.34) | copy-start | bytes 3145732
  61.3 16.9 %collective-permute-start.9 = (f32[128,1024]{1,0:T(8,128)S(1)}, f32[128,1024]{1,0:T(8,128)S(1)}, u32[]{:S(2)}, u32[]{:S(2)}) collective-permute-start(f32[128,1024]{1,0:T(8,128)S(1)} %slice.102), channel_id=1, source_target_pairs={{0,4},{1,5},{2,6},{3,7},{8,12},{9,13},{10,14},{11,15},{16,20},{17,... | collective-permute-start | bytes 1572872 | tf_op jit(solution)/shard_map/ppermute | solution.py:350
  68.8 414.6 %all-gather.5.cloned.1.call-start = ((), (), s32[]{:S(2)}) async-start(), calls=%async_computation.3 | async-start | bytes 4718592 | tf_op jit(solution)/shard_map/all_gather | solution.py:351
  79.1 404.3 %all-gather.3.cloned.1.call-start = ((), (), s32[]{:S(2)}) async-start(), calls=%async_computation.2 | async-start | bytes 7077888 | tf_op jit(solution)/shard_map/all_gather | solution.py:316
  85.1 17.5 %collective-permute-start.8 = (f32[512,384]{1,0:T(8,128)S(1)}, f32[512,384]{1,0:T(8,128)S(1)}, u32[]{:S(2)}, u32[]{:S(2)}) collective-permute-start(f32[512,384]{1,0:T(8,128)S(1)} %bitcast.42), channel_id=1, source_target_pairs={{0,5},{4,7},{8,13},{12,15},{16,21},{20,23},{24,29},{28,31}} | collective-permute-start | bytes 2359304 | tf_op jit(solution)/shard_map/ppermute | solution.py:315
  87.7 15.0 %collective-permute-start.5 = (f32[512,384]{1,0:T(8,128)S(1)}, f32[512,384]{1,0:T(8,128)S(1)}, u32[]{:S(2)}, u32[]{:S(2)}) collective-permute-start(f32[512,384]{1,0:T(8,128)S(1)} %bitcast.43), channel_id=1, source_target_pairs={{0,0},{4,2},{8,8},{12,10},{16,16},{20,18},{24,24},{28,26}} | collective-permute-start | bytes 2359304 | tf_op jit(solution)/shard_map/ppermute | solution.py:315
  88.4 14.2 %collective-permute-start.7 = (f32[512,384]{1,0:T(8,128)S(1)}, f32[512,384]{1,0:T(8,128)S(1)}, u32[]{:S(2)}, u32[]{:S(2)}) collective-permute-start(f32[512,384]{1,0:T(8,128)S(1)} %bitcast.44), channel_id=1, source_target_pairs={{0,1},{4,3},{8,9},{12,11},{16,17},{20,19},{24,25},{28,27}} | collective-permute-start | bytes 2359304 | tf_op jit(solution)/shard_map/ppermute | solution.py:315
  89.8 21.6 %collective-permute-start.6 = (f32[512,384]{1,0:T(8,128)S(1)}, f32[512,384]{1,0:T(8,128)S(1)}, u32[]{:S(2)}, u32[]{:S(2)}) collective-permute-start(f32[512,384]{1,0:T(8,128)S(1)} %bitcast.45), channel_id=1, source_target_pairs={{0,4},{4,6},{8,12},{12,14},{16,20},{20,22},{24,28},{28,30}} | collective-permute-start | bytes 2359304 | tf_op jit(solution)/shard_map/ppermute | solution.py:315
  122.5 436.7 %all-to-all-start = ((f32[4,512,1024]{2,1,0:T(8,128)}), f32[4,512,1024]{2,1,0:T(8,128)}, u32[]{:S(2)}, u32[]{:S(2)}) async-start(f32[4,512,1024]{2,1,0:T(8,128)} %outgoing.1), calls=%async_computation | async-start | bytes 16777216 | tf_op jit(solution)/shard_map/all_to_all | solution.py:363
  506.7 37.7 %collective-permute-start.10 = (f32[384,1024]{1,0:T(8,128)}, f32[384,1024]{1,0:T(8,128)S(1)}, u32[]{:S(2)}, u32[]{:S(2)}) collective-permute-start(f32[384,1024]{1,0:T(8,128)} %get-tuple-element.35), channel_id=1, source_target_pairs={{0,2},{1,3},{6,4},{7,5},{8,10},{9,11},{14,12},{15,13},{16,18},{17,... | collective-permute-start | bytes 4718600 | tf_op jit(solution)/shard_map/ppermute | solution.py:404
  546.0 3.5 collective-permute-start.11
Sparse Core Ops, SparseCore 0:
  68.9 369.0 all-reduce.2
Sparse Core Ops, SparseCore 1:
  79.2 129.9 all-gather.4
  211.2 193.7 all-gather.2

commit v2 on v1

--- a/solution.py
+++ b/solution.py
@@ -52,17 +52,42 @@
     aug[:, :n] = block
     aug[:, n:] = jnp.where(rows == cols, 1.0, 0.0).astype(jnp.float32)
 
-    def step(k, pivots):
-        pivot_row = aug[pl.ds(k, 1), :]
-        pivot = jnp.sum(jnp.where(lane_ids == k, pivot_row[:, :n], 0.0), axis=1, keepdims=True)
+    many = 4
+
+    def step(i, pivots):
+        k = i * many
+        rows_k = [aug[pl.ds(k + j, 1), :] for j in range(many)]
         body = aug[...]
-        column = jnp.sum(jnp.where(cols == k, body[:, :n], 0.0), axis=1, keepdims=True)
-        factor = jnp.where(row_ids > k, column / pivot, 0.0)
-        aug[...] = body - factor * pivot_row
-        return jnp.where(row_ids == k, pivot, pivots)
-
-    pivots = lax.fori_loop(0, n, step, jnp.ones((n, 1), jnp.float32))
+        columns = [jnp.sum(jnp.where(cols == k + j, body[:, :n], 0.0), axis=1, keepdims=True) for j in range(many)]
+        small = [
+            [jnp.sum(jnp.where(lane_ids == k + b, rows_k[a][:, :n], 0.0), axis=1, keepdims=True) for b in range(many)]
+            for a in range(many)
+        ]
+        factors = []
+        for a in range(many):
+            scale = 1.0 / small[a][a]
+            for b in range(a + 1, many):
+                ratio = small[a][b] * scale
+                rows_k[b] = rows_k[b] - ratio * rows_k[a]
+                columns[b] = columns[b] - columns[a] * ratio
+                for c in range(b, many):
+                    small[b][c] = small[b][c] - ratio * small[a][c]
+            factors.append(jnp.where(row_ids >= k + many, columns[a] * scale, 0.0))
+            pivots = jnp.where(row_ids == k + a, small[a][a], pivots)
+        for a in range(many):
+            body = body - factors[a] * rows_k[a]
+        aug[...] = body
+        for a in range(1, many):
+            aug[pl.ds(k + a, 1), :] = rows_k[a]
+        return pivots
+
+    pivots = lax.fori_loop(0, n // many, step, jnp.ones((n, 1), jnp.float32))
     return aug[:, n:] / jnp.sqrt(pivots)
+
+
+def extract_kernel(groups, view, out):
+    for h in range(out.shape[1] // B):
+        out[:, h * B : (h + 1) * B] = view[:, h * groups, :]
 
 
 def child_kernel(pos, live, quarters, block, strip, prow, lead_rows, brow3, bcol3, panel, aug, brow):
@@ -149,34 +174,56 @@
             inverse[kk, jj] = -dot_nn(diag, total)
 
 
-def columns_kernel(pos, quarters, inverse, entries, panels, lc3, mine, placed):
-    groups, _, cols_here = panels.shape
-    col_blocks = cols_here // B
-    grp, col = pos[0], pos[2]
-    quarter = pl.program_id(0)
+def place_pieces(pos, quarters, pieces, panels, quarter, entries, placed):
+    groups = quarters.shape[0]
+    rows_n = len(pieces) // groups
+    part, share = pieces[0].shape[0], panels[0].shape[0]
+    col_blocks = placed.shape[1] // B
+    grp, row, col = pos[0], pos[1], pos[2]
     placed[...] = jnp.zeros_like(placed)
-    for g in range(groups):
+    for s in range(groups):
+        source = lax.rem(grp + groups - s, groups)
+
+        @pl.when(source == quarter)
+        def _(s=s):
+            for t in range(rows_n):
+                at = pl.multiple_of(lax.rem(row + rows_n - t, rows_n) * part, part)
+                entries[pl.ds(at, part), :] = pieces[s * rows_n + t][...]
+
         for b in range(col_blocks):
             cut = slice(b * B, (b + 1) * B)
 
-            @pl.when(quarters[g, col * col_blocks + b] == quarter)
-            def _(g=g, cut=cut):
-                placed[:, cut] += panels[g, :, cut]
-
+            @pl.when(quarters[source, col * col_blocks + b] == quarter)
+            def _(s=s, cut=cut):
+                for t in range(rows_n):
+                    at = pl.multiple_of(lax.rem(row + rows_n - t, rows_n) * share, share)
+                    placed[pl.ds(at, share), cut] += panels[s * rows_n + t][:, cut]
+
+
+def columns_kernel(pos, quarters, inverse, *refs):
+    lc3, entries, placed = refs[-3:]
+    count = (len(refs) - 3) // 2
+    place_pieces(pos, quarters, refs[:count], refs[count : 2 * count], pl.program_id(0), entries, placed)
     value = dot_nt(inverse[...], entries[...]) + dot_nn(inverse[:, LEAD:], placed[...])
     hi, lo = split(value)
     lc3[:PIV] = hi
     lc3[PIV : 2 * PIV] = lo
     lc3[2 * PIV :] = hi
 
-    @pl.when(quarter == grp)
-    def _():
-        mine[...] = value
-
-
-def rows_kernel(pos, across, lr, lr3):
+
+def mine_kernel(pos, quarters, *refs):
+    mine, entries, placed = refs[-3:]
+    count = (len(refs) - 3) // 2
+    place_pieces(pos, quarters, refs[:count], refs[count : 2 * count], pos[0], entries, placed)
+    for k in range(KP):
+        kk = slice(k * B, (k + 1) * B)
+        value = jnp.transpose(entries[:, kk])
+        mine[kk] = value if k < KC else value + placed[(k - KC) * B : (k - KC + 1) * B]
+
+
+def rows_kernel(pos, inverse, across, lr, lr3):
     height = lr.shape[0]
-    value = jnp.transpose(across[...])
+    value = jnp.transpose(dot_nn(inverse[...], across[...]))
     first = pos[3] + pl.program_id(0) * height
     row_ids = first + lax.broadcasted_iota(jnp.int32, (height, PIV), 0)
     inside = lax.broadcasted_iota(jnp.int32, (height, PIV), 1)
@@ -276,6 +323,10 @@
     return pltpu.CompilerParams(vmem_limit_bytes=VMEM_LIMIT, **kw)
 
 
+def cost(us):
+    return pl.CostEstimate(flops=10**6, bytes_accessed=us * 3_500_000, transcendentals=0)
+
+
 def bcast(value, axis, size):
     here = lax.axis_index(axis)
     stride = size // 2
@@ -285,6 +336,22 @@
         value = jnp.where(here % (2 * stride) == stride, moved, value)
         stride //= 2
     return value
+
+
+def ring_shift(value, axis, size, by):
+    return lax.ppermute(value, axis, [(i, (i + by) % size) for i in range(size)])
+
+
+def step_up(value, groups):
+    return lax.ppermute(value, "grp", [(i, i + 1) for i in range(groups - 1)])
+
+
+def step_down(value, groups):
+    return lax.ppermute(value, "grp", [(i + 1, i) for i in range(groups - 1)])
+
+
+def across_rows(planes, rows_n):
+    return [v if t == 0 else ring_shift(v, "row", rows_n, t) for v in planes for t in range(rows_n)]
 
 
 def shards(child_fronts, parent_entries, child_live, quarters):
@@ -302,22 +369,42 @@
     f32, bf16 = jnp.float32, jnp.bfloat16
     shape = jax.ShapeDtypeStruct
 
-    own = parent_entries[:, 0, : min(PIV, cols_here)]
+    lanes = cols_here // B
+    view = parent_entries.reshape(rows_here, groups, lanes, B).transpose(0, 2, 1, 3).reshape(rows_here, lanes * groups, B)
+    wide = min(PIV, cols_here)
+    tall = min(512, rows_here)
+    deep = -(-wide // B * groups // 8) * 8
+    own = pl.pallas_call(
+        functools.partial(extract_kernel, groups),
+        grid=(rows_here // tall,),
+        out_shape=shape((rows_here, wide), f32),
+        in_specs=[pl.BlockSpec((tall, deep, B), lambda i: (i, 0, 0))],
+        out_specs=pl.BlockSpec((tall, wide), lambda i: (i, 0)),
+        compiler_params=params(),
+        cost_estimate=cost(6),
+        name="extract",
+    )(view)
+    first_own = own
     for other in range(1, -(-PIV // cols_here)):
         wide = min(cols_here, PIV - other * cols_here)
-        own = jnp.concatenate([own, lax.ppermute(parent_entries[:, 0, :wide], "col", [(other, 0)])], axis=1)
+        own = jnp.concatenate([own, lax.ppermute(first_own[:, :wide], "col", [(other, 0)])], axis=1)
     part = cols_here // rows_n
-    piece = jnp.zeros((part, PIV), f32)
+    pieces = []
     for h in range(spans):
         for r in range(rows_n):
-            at = h * cols_here + r * part
+            at = (h * rows_n + r) * part
             pairs = [(s * cols_n, r * cols_n + s * spans + h) for s in range(rows_n)]
-            piece = piece + lax.ppermute(own[at : at + part], ("row", "col"), pairs)
-    entries_c = lax.all_gather(piece, ("grp", "row"), tiled=True)
+            pieces.append(lax.ppermute(own[at : at + part], ("row", "col"), pairs))
+    piece = functools.reduce(lambda a, b: a + b, pieces)
+    up = [piece, step_up(piece, groups)] + [None] * (groups - 2)
+    down = [piece, step_down(piece, groups)] + [None] * (groups - 2)
 
     strip = bcast(front[:, :LEAD], "col", cols_n)
     corner = bcast(front[:LEAD, :LEAD], "col", cols_n)
     payload = bcast(jnp.concatenate([front[:LEAD], corner], axis=1), "row", rows_n)
+    strip, payload, up[1], down[1] = lax.optimization_barrier((strip, payload, up[1], down[1]))
+    for k in range(2, groups):
+        up[k], down[k] = step_up(up[k - 1], groups), step_down(down[k - 1], groups)
     brow3, bcol3, panel = pl.pallas_call(
         child_kernel,
         out_shape=(
@@ -329,26 +416,14 @@
         out_specs=(vmem(), vmem(), vmem()),
         scratch_shapes=[pltpu.VMEM((LEAD, 2 * LEAD), f32), pltpu.VMEM((rows_here, LEAD), f32)],
         compiler_params=params(),
+        cost_estimate=cost(20),
         name="child",
     )(pos, child_live, quarters, payload[:, cols_here:], strip, payload[:, :cols_here], front[LEAD:PIV])
-
-    head = jnp.zeros((PIV, PIV), f32)
-    for other in range(-(-PIV // cols_here)):
-        wide = min(cols_here, PIV - other * cols_here)
-        mine = (row == 0) & (col == other)
-        at = other * cols_here
-        which = lax.dynamic_slice_in_dim(quarters, grp, 1, 0)[0, at // B : (at + wide) // B]
-        keep = mine & (jnp.repeat(which, B) == 0)
-        first = jnp.where(mine & (grp == 0), parent_entries[:PIV, 0, :wide], 0.0)
-        added = jnp.where(keep[None, :], panel[:, :wide], 0.0)
-        head = head.at[:, at : at + wide].add(first + jnp.pad(added, ((LEAD, 0), (0, 0))))
-    head = lax.psum(head, ("grp", "row", "col"))
 
     share = (PIV - LEAD) // rows_n
     panel_piece = jnp.where(row == 0, panel[:share], 0.0)
     for r in range(1, rows_n):
         panel_piece = panel_piece + lax.ppermute(panel[r * share : (r + 1) * share], "row", [(0, r)])
-    panels = lax.all_gather(panel_piece, ("grp", "row"), tiled=True).reshape(groups, PIV - LEAD, cols_here)
 
     outgoing = pl.pallas_call(
         outgoing_kernel,
@@ -358,39 +433,53 @@
         out_specs=pl.BlockSpec((1, slots * B, cols_here), lambda d: (d, 0, 0)),
         scratch_shapes=[pltpu.VMEM((slots * B, 3 * LEAD), bf16), pltpu.SMEM((slots,), jnp.int32)],
         compiler_params=params(),
+        cost_estimate=cost(10),
         name="outgoing",
     )(pos, child_live, quarters, front, brow3, bcol3)
+
+    planes = [panel_piece] + [ring_shift(panel_piece, "grp", groups, s) for s in range(1, groups)]
+    outgoing, up[1:], down[1:], planes[1:] = lax.optimization_barrier((outgoing, up[1:], down[1:], planes[1:]))
     arrived = lax.all_to_all(outgoing, "grp", split_axis=0, concat_axis=0, tiled=True)
-
-    inverse = pl.pallas_call(
-        head_kernel,
-        out_shape=shape((PIV, PIV), f32),
-        in_specs=[vmem()],
+    merged = [piece] + [jnp.where(grp >= s, up[s], down[groups - s]) for s in range(1, groups)]
+    entries_c = across_rows(merged, rows_n)
+    panels = across_rows(planes, rows_n)
+
+    wide = min(PIV, cols_here)
+    needed = min(part, wide)
+    zero = jnp.zeros((), f32)
+    own_rows, added = [], []
+    for at in range(rows_n):
+        total, extra = zero, zero
+        for s in range(groups):
+            start = col * (cols_here // B)
+            which = lax.dynamic_slice(quarters, ((grp - s) % groups, start), (1, wide // B))
+            lanes_in = jnp.repeat(which == 0, B, axis=1)
+            for t in range(rows_n):
+                here = (row - t) % rows_n == at
+                if at * part < wide:
+                    total = total + jnp.where(here & (grp == s), entries_c[s * rows_n + t][:needed], 0.0)
+                extra = extra + jnp.where(here & lanes_in, panels[s * rows_n + t][:, :wide], 0.0)
+        if at * part < wide:
+            own_rows.append(total)
+        added.append(extra)
+    own_rows = jnp.concatenate(own_rows, axis=0)[:wide]
+    head = own_rows + jnp.pad(jnp.concatenate(added, axis=0).T, ((0, 0), (LEAD, 0)))
+    heads = [head]
+    for other in range(1, -(-PIV // cols_here)):
+        wide = min(cols_here, PIV - other * cols_here)
+        heads.append(lax.ppermute(head[:wide], "col", [(other, 0)]))
+    head = bcast(jnp.concatenate(heads, axis=0) if len(heads) > 1 else head, "col", cols_n)
+
+    mine = pl.pallas_call(
+        mine_kernel,
+        out_shape=shape((PIV, cols_here), f32),
+        in_specs=[smem(), smem()] + [vmem()] * (len(entries_c) + len(panels)),
         out_specs=vmem(),
-        scratch_shapes=[pltpu.VMEM((PIV, PIV), f32), pltpu.VMEM((PIV, PIV), f32), pltpu.VMEM((B, 2 * B), f32)],
-        compiler_params=params(),
-        cost_estimate=pl.CostEstimate(flops=10**9, bytes_accessed=10**8, transcendentals=0),
-        name="head",
-    )(head)
-
-    lc3, mine = pl.pallas_call(
-        columns_kernel,
-        grid=(groups,),
-        out_shape=(shape((3 * PIV, groups * cols_here), bf16), shape((PIV, cols_here), f32)),
-        in_specs=[
-            smem(),
-            smem(),
-            vmem(),
-            pl.BlockSpec((cols_here, PIV), lambda u: (u, 0)),
-            vmem(),
-        ],
-        out_specs=(pl.BlockSpec((3 * PIV, cols_here), lambda u: (0, u)), vmem()),
-        scratch_shapes=[pltpu.VMEM((PIV - LEAD, cols_here), f32)],
-        compiler_params=params(),
-        cost_estimate=pl.CostEstimate(flops=10**10, bytes_accessed=3 * 10**7, transcendentals=0),
-        name="columns",
-    )(pos, quarters, inverse, entries_c, panels)
-
+        scratch_shapes=[pltpu.VMEM((cols_here, PIV), f32), pltpu.VMEM((PIV - LEAD, cols_here), f32)],
+        compiler_params=params(),
+        cost_estimate=cost(6),
+        name="mine",
+    )(pos, quarters, *entries_c, *panels)
     y_n = cols_n // spans
     y_here = (col // spans - row) % y_n
     stride = y_n // 2
@@ -416,21 +505,43 @@
         ],
         axis=1,
     )
+    inverse = pl.pallas_call(
+        head_kernel,
+        out_shape=shape((PIV, PIV), f32),
+        in_specs=[vmem()],
+        out_specs=vmem(),
+        scratch_shapes=[pltpu.VMEM((PIV, PIV), f32), pltpu.VMEM((PIV, PIV), f32), pltpu.VMEM((B, 2 * B), f32)],
+        compiler_params=params(),
+        cost_estimate=cost(25),
+        name="head",
+    )(head)
+
+    lc3 = pl.pallas_call(
+        columns_kernel,
+        grid=(groups,),
+        out_shape=shape((3 * PIV, groups * cols_here), bf16),
+        in_specs=[smem(), smem(), vmem()] + [vmem()] * (len(entries_c) + len(panels)),
+        out_specs=pl.BlockSpec((3 * PIV, cols_here), lambda u: (0, u)),
+        scratch_shapes=[pltpu.VMEM((cols_here, PIV), f32), pltpu.VMEM((PIV - LEAD, cols_here), f32)],
+        compiler_params=params(),
+        cost_estimate=cost(23),
+        name="columns",
+    )(pos, quarters, inverse, *entries_c, *panels)
+
     tall = min(256, rows_here)
     lr, lr3 = pl.pallas_call(
         rows_kernel,
         grid=(rows_here // tall,),
         out_shape=(shape((rows_here, PIV), f32), shape((rows_here, 3 * PIV), bf16)),
-        in_specs=[smem(), pl.BlockSpec((PIV, tall), lambda i: (0, i))],
+        in_specs=[smem(), vmem(), pl.BlockSpec((PIV, tall), lambda i: (0, i))],
         out_specs=(pl.BlockSpec((tall, PIV), lambda i: (i, 0)), pl.BlockSpec((tall, 3 * PIV), lambda i: (i, 0))),
         compiler_params=params(),
+        cost_estimate=cost(12),
         name="rows",
-    )(pos, across)
-
-    lanes = cols_here // B
+    )(pos, inverse, across)
+
     pair = 2
     tall = min(512, rows_here)
-    view = parent_entries.reshape(rows_here, groups, lanes, B).transpose(0, 2, 1, 3).reshape(rows_here, lanes * groups, B)
     result = pl.pallas_call(
         final_kernel,
         grid=(rows_here // tall, lanes // pair),

time: 621 us -> 431 us (0.69)
  waiting for transfers between devices: 380 us -> 146 us
  starting transfers between devices: 36.5 us -> 73.6 us
  local copies, waits for them, and re-layouts: 17.1 us -> 33.8 us
  between operations: 15.2 us -> 0.45 us
  other arithmetic: 12.5 us -> 22.3 us
  Pallas kernels: 159 us -> 152 us
    psum x1 -> x0, waiting for transfers between devices: 310 us -> none  [shards(): head = lax.psum(head, ('grp', 'row', 'col'))]
    ppermute x4 -> x21, waiting for transfers between devices: 17.6 us -> 129 us  [the longest x11 106 us: ring_shift(): lax.ppermute(value, axis, [(i, (i + by) % size) for i in range(size)])]
    ppermute x4 -> x21, starting transfers between devices: 8.46 us -> 44.8 us  [the longest x3 15.5 us: step_up(): return lax.ppermute(value, 'grp', [(i, i + 1) for i in range(groups - 1)])]
    ppermute x1, waiting for transfers between devices: 34.2 us -> 10.2 us  [shards(): moved = lax.ppermute(mine, ('row', 'col'), pairs)]
    pallas_call x1, Pallas kernels: 45.4 us -> 26.1 us  [shards(): pl.pallas_call(head_kernel, out_shape=shape((PIV, PIV), f32), in_specs=[v...]
    pallas_call x1 -> x3, Pallas kernels: 23.3 us -> 39.2 us  [the longest x1 24.5 us: shards(): pl.pallas_call(columns_kernel, grid=(groups,), out_shape=shape((3 * PIV,...]
    ppermute x1, waiting for transfers between devices: 9.41 us -> 0.16 us  [shards(): lax.ppermute(panel[r * share:(r + 1) * share], 'row', [(0, r)])]
    ppermute x0 -> x4, local copies, waits for them, and re-layouts: none -> 9.24 us  [ring_shift(): lax.ppermute(value, axis, [(i, (i + by) % size) for i in range(size)])]
  transfers between devices with their start and end apart: 16 -> 32, of which waited for: 9 -> 15; matrix products, arithmetic and copies ran while one was open for 4% -> 13% of each run, Pallas kernels for 14% -> 23%
where the time goes in v2:
time: 431 us; the launch traced here: 428 us
  Pallas kernels  152 us (35%)
  waiting for transfers between devices  146 us (34%)
  starting transfers between devices  73.6 us (17%)
  local copies, waits for them, and re-layouts  33.8 us (8%)
  other arithmetic  22.3 us (5%)
    ppermute x11, waiting for transfers between devices, ring_shift(): lax.ppermute(value, axis, [(i, (i + by) % size) for i in range(size)])  106 us
    pallas_call x1, Pallas kernels, shards(): pl.pallas_call(final_kernel, grid=(rows_here // tall, lanes // pair), out...  53.2 us
    pallas_call x1, Pallas kernels, shards(): pl.pallas_call(head_kernel, out_shape=shape((PIV, PIV), f32), in_specs=[v...  26.1 us
    pallas_call x1, Pallas kernels, shards(): pl.pallas_call(columns_kernel, grid=(groups,), out_shape=shape((3 * PIV,...  24.5 us
    ppermute x7, starting transfers between devices, bcast(): moved = lax.ppermute(value, axis, pairs)  15.6 us
    ppermute x3, starting transfers between devices, step_up(): return lax.ppermute(value, 'grp', [(i, i + 1) for i in range(groups - 1)])  15.5 us
    ppermute x4, starting transfers between devices, shards(): pieces.append(lax.ppermute(own[at:at + part], ('row', 'col'), pairs))  14 us
    pallas_call x1, Pallas kernels, shards(): pl.pallas_call(child_kernel, out_shape=(shape((rows_here, 3 * LEAD), bf16...  12.9 us
  transfers between devices with their start and end apart: 32, of which 15 were waited for; matrix products, arithmetic and copies ran while one was open for 13% of the time, Pallas kernels for 23%

profile of v2, /device:TPU:0, one launch (start us, length us, event | category | flops | bytes accessed | tf_op | source)
XLA Modules:
  0.0 428.1 jit_solution(4830694422831773107)
XLA Ops:
  0.8 4.9 %collective-permute-start.2 = (f32[128,128]{1,0:T(8,128)S(1)}, f32[128,128]{1,0:T(8,128)S(1)}, u32[]{:S(2)}, u32[]{:S(2)}) collective-permute-start(f32[128,128]{1,0:T(8,128)S(1)} %slice.129), channel_id=1, source_target_pairs={{0,2},{4,6},{8,10},{12,14},{16,18},{20,22},{24,26},{28,30}} | collective-permute-start | bytes 196616 | tf_op jit(solution)/shard_map/ppermute | solution.py:335
  5.7 2.3 slice.128
  8.0 2.3 collective-permute-start
  10.3 8.1 %extract.1 = f32[2048,384]{1,0:T(8,128)} custom-call(f32[2048,32,128]{2,1,0:T(8,128)} %bitcast.81), custom_call_target="tpu_custom_call" | custom-call | flops 1000000 | bytes 21000000 | tf_op jit(solution)/shard_map/extract/pallas_call | solution.py:377
  18.4 3.0 fusion.8
  21.3 2.3 copy.31
  23.6 2.2 collective-permute-start.8
  27.0 7.4 %collective-permute-start.5 = (f32[512,384]{0,1:T(8,128)}, f32[512,384]{0,1:T(8,128)}, u32[]{:S(2)}, u32[]{:S(2)}) collective-permute-start(f32[512,384]{0,1:T(8,128)} %copy.28), channel_id=1, source_target_pairs={{0,0},{4,2},{8,8},{12,10},{16,16},{20,18},{24,24},{28,26}} | collective-permute-start | bytes 2359304 | tf_op jit(solution)/shard_map/ppermute | solution.py:397
  34.7 2.2 collective-permute-start.7
  37.7 1.3 collective-permute-start.3
  41.3 2.2 collective-permute-start.6
  44.4 2.1 collective-permute-start.4
  46.5 1.3 broadcast_select_fusion.3
  47.8 2.3 collective-permute-start.1
  50.7 7.9 %collective-permute-done.6 = f32[512,384]{0,1:T(8,128)} collective-permute-done((f32[512,384]{0,1:T(8,128)}, f32[512,384]{0,1:T(8,128)}, u32[]{:S(2)}, u32[]{:S(2)}) %collective-permute-start.6) | collective-permute-done | bytes 786464 | tf_op jit(solution)/shard_map/ppermute | solution.py:397
  58.7 2.2 add_add_fusion
  60.9 1.3 collective-permute-start.10
  62.2 5.5 %collective-permute-start.9 = (f32[512,384]{0,1:T(8,128)S(1)}, f32[512,384]{0,1:T(8,128)}, u32[]{:S(2)}, u32[]{:S(2)}) collective-permute-start(f32[512,384]{0,1:T(8,128)S(1)} %add_add_fusion), channel_id=1, source_target_pairs={{0,8},{8,16},{16,24},{1,9},{9,17},{17,25},{2,10},{10,18},{18,26},{... | collective-permute-start | bytes 2359304 | tf_op jit(solution)/shard_map/ppermute | solution.py:346
  68.8 7.6 %collective-permute-done.10 = f32[512,384]{0,1:T(8,128)} collective-permute-done((f32[512,384]{0,1:T(8,128)S(1)}, f32[512,384]{0,1:T(8,128)}, u32[]{:S(2)}, u32[]{:S(2)}) %collective-permute-start.10) | collective-permute-done | bytes 786464 | tf_op jit(solution)/shard_map/ppermute | solution.py:350
  76.5 7.0 %collective-permute-done.9 = f32[512,384]{0,1:T(8,128)} collective-permute-done((f32[512,384]{0,1:T(8,128)S(1)}, f32[512,384]{0,1:T(8,128)}, u32[]{:S(2)}, u32[]{:S(2)}) %collective-permute-start.9) | collective-permute-done | bytes 786464 | tf_op jit(solution)/shard_map/ppermute | solution.py:346
  83.4 4.5 %collective-permute-start.11 = (f32[512,384]{0,1:T(8,128)}, f32[512,384]{0,1:T(8,128)S(1)}, u32[]{:S(2)}, u32[]{:S(2)}) collective-permute-start(f32[512,384]{0,1:T(8,128)} %collective-permute-done.9), channel_id=1, source_target_pairs={{0,8},{8,16},{16,24},{1,9},{9,17},{17,25},{2,10},{10,18},{18,26},{... | collective-permute-start | bytes 2359304 | tf_op jit(solution)/shard_map/ppermute | solution.py:346
  88.0 1.3 collective-permute-start.13
  89.3 2.3 slice_bitcast_fusion.lead_rows
  93.1 12.9 %child.1 = (bf16[2048,384]{1,0:T(8,128)(2,1)}, bf16[384,1024]{1,0:T(8,128)(2,1)}, f32[256,1024]{1,0:T(8,128)}) custom-call(s32[8]{0:T(128)} %compare_select_fusion.2.pos, s32[4]{0:T(128)} %live.3, s32[4,32]{1,0:T(4,128)} %quarters.9, f32[128,128]{1,0:T(8,128)} %slice.106.block, f32[2048,128]{1,0:T(8,128)} %broadcast_select_fusion.4.strip, ...), custom_call_target="tpu_custom_call" | custom-call | flops 1000000 | bytes 70000000 | tf_op jit(solution)/shard_map/child/pallas_call | solution.py:408
  106.0 1.9 slice.111
  107.9 2.5 collective-permute-start.15
  110.4 5.5 %collective-permute-start.12 = (f32[512,384]{0,1:T(8,128)S(1)}, f32[512,384]{0,1:T(8,128)}, u32[]{:S(2)}, u32[]{:S(2)}) collective-permute-start(f32[512,384]{0,1:T(8,128)S(1)} %collective-permute-done.11), channel_id=1, source_target_pairs={{0,8},{8,16},{16,24},{1,9},{9,17},{17,25},{2,10},{10,18},{18,26},{... | collective-permute-start | bytes 2359304 | tf_op jit(solution)/shard_map/ppermute | solution.py:346
  115.9 1.3 collective-permute-start.14
  117.3 1.9 select_add_fusion.refs_8_
  119.3 4.7 %collective-permute-start.18 = (f32[128,1024]{1,0:T(8,128)}, f32[128,1024]{1,0:T(8,128)}, u32[]{:S(2)}, u32[]{:S(2)}) collective-permute-start(f32[128,1024]{1,0:T(8,128)} %select_add_fusion.refs_8_), channel_id=1, source_target_pairs={{0,24},{8,0},{16,8},{24,16},{1,25},{9,1},{17,9},{25,17},{2,26},{10... | collective-permute-start | bytes 1572872 | tf_op jit(solution)/shard_map/ppermute | solution.py:342
  124.9 9.5 %outgoing.1 = f32[4,512,1024]{2,1,0:T(8,128)} custom-call(s32[8]{0:T(128)} %compare_select_fusion.2.pos, s32[4]{0:T(128)} %live.3, s32[4,32]{1,0:T(4,128)} %quarters.9, f32[2048,1024]{1,0:T(8,128)} %bitcast.87, bf16[2048,384]{1,0:T(8,128)(2,1)} %get-tuple-element.26.brow3, bf16[384,1024]{1,0:T(8,128)(2,1)} %get-tuple-element.27.bcol3), custom_call_target="tpu_custom_call" | custom-call | flops 1000000 | bytes 35000000 | tf_op jit(solution)/shard_map/outgoing/pallas_call | solution.py:428
  134.4 10.8 %collective-permute-done.18.refs_14_ = f32[128,1024]{1,0:T(8,128)} collective-permute-done((f32[128,1024]{1,0:T(8,128)}, f32[128,1024]{1,0:T(8,128)}, u32[]{:S(2)}, u32[]{:S(2)}) %collective-permute-start.18) | collective-permute-done | bytes 524320 | tf_op jit(solution)/shard_map/ppermute | solution.py:342
  145.2 48.1 %collective-permute-done.17.refs_12_ = f32[128,1024]{1,0:T(8,128)} collective-permute-done((f32[128,1024]{1,0:T(8,128)}, f32[128,1024]{1,0:T(8,128)}, u32[]{:S(2)}, u32[]{:S(2)}) %collective-permute-start.17) | collective-permute-done | bytes 524320 | tf_op jit(solution)/shard_map/ppermute | solution.py:342
  193.3 5.6 %all-to-all-start = ((f32[4,512,1024]{2,1,0:T(8,128)}), f32[4,512,1024]{2,1,0:T(8,128)}, u32[]{:S(2)}, u32[]{:S(2)}) async-start(f32[4,512,1024]{2,1,0:T(8,128)} %outgoing.1), calls=%async_computation | async-start | bytes 16777216 | tf_op jit(solution)/shard_map/all_to_all | solution.py:442
  199.6 1.3 broadcast_select_fusion.5
  200.9 2.1 collective-permute-start.22
  204.5 1.3 broadcast_select_fusion.7
  205.8 2.1 collective-permute-start.20
  207.9 12.2 %collective-permute-done.19 = f32[512,384]{0,1:T(8,128)} collective-permute-done((f32[512,384]{0,1:T(8,128)S(1)}, f32[512,384]{0,1:T(8,128)}, u32[]{:S(2)}, u32[]{:S(2)}) %collective-permute-start.19) | collective-permute-done | bytes 786464 | tf_op jit(solution)/shard_map/ppermute | solution.py:342
  220.1 11.4 %collective-permute-done.22 = f32[512,384]{0,1:T(8,128)} collective-permute-done((f32[512,384]{0,1:T(8,128)S(1)}, f32[512,384]{0,1:T(8,128)}, u32[]{:S(2)}, u32[]{:S(2)}) %collective-permute-start.22) | collective-permute-done | bytes 786464 | tf_op jit(solution)/shard_map/ppermute | solution.py:342
  232.3 7.7 %collective-permute-done.21 = f32[512,384]{0,1:T(8,128)} collective-permute-done((f32[512,384]{0,1:T(8,128)S(1)}, f32[512,384]{0,1:T(8,128)}, u32[]{:S(2)}, u32[]{:S(2)}) %collective-permute-start.21) | collective-permute-done | bytes 786464 | tf_op jit(solution)/shard_map/ppermute | solution.py:342
  242.1 2.3 copy.12.refs_1_
  248.0 2.4 copy.18.refs_7_
  250.3 2.3 copy.16.refs_5_
  252.6 2.3 copy.14.refs_3_
  254.9 4.7 %collective-permute-done.24.refs_11_ = f32[128,1024]{1,0:T(8,128)} collective-permute-done((f32[128,1024]{1,0:T(8,128)}, f32[128,1024]{1,0:T(8,128)}, u32[]{:S(2)}, u32[]{:S(2)}) %collective-permute-start.24) | collective-permute-done | bytes 524320 | tf_op jit(solution)/shard_map/ppermute | solution.py:342
  259.6 5.6 %collective-permute-done.25.refs_13_ = f32[128,1024]{1,0:T(8,128)} collective-permute-done((f32[128,1024]{1,0:T(8,128)}, f32[128,1024]{1,0:T(8,128)}, u32[]{:S(2)}, u32[]{:S(2)}) %collective-permute-start.25) | collective-permute-done | bytes 524320 | tf_op jit(solution)/shard_map/ppermute | solution.py:342
  265.2 5.6 %collective-permute-done.26.refs_15_ = f32[128,1024]{1,0:T(8,128)} collective-permute-done((f32[128,1024]{1,0:T(8,128)}, f32[128,1024]{1,0:T(8,128)}, u32[]{:S(2)}, u32[]{:S(2)}) %collective-permute-start.26) | collective-permute-done | bytes 524320 | tf_op jit(solution)/shard_map/ppermute | solution.py:342
  270.8 6.6 %mine.1 = f32[384,1024]{1,0:T(8,128)} custom-call(s32[8]{0:T(128)} %compare_select_fusion.2.pos, s32[4,32]{1,0:T(4,128)} %quarters.9, f32[512,384]{1,0:T(8,128)} %copy.11.refs_0_, f32[512,384]{1,0:T(8,128)} %copy.12.refs_1_, f32[512,384]{1,0:T(8,128)} %copy.13.refs_2_, f32[512,384]{1,0:T(8,128)} %copy.14.refs_3_, f32[512,384]{1,0:T(8,128)} %copy.15.refs_4_, ...), custom_call_target="tpu_custom_call" | custom-call | flops 1000000 | bytes 21000000 | tf_op jit(solution)/shard_map/mine/pallas_call | solution.py:473
  277.5 5.0 %collective-permute-start.29 = (f32[384,1024]{1,0:T(8,128)}, f32[384,1024]{1,0:T(8,128)}, u32[]{:S(2)}, u32[]{:S(2)}) collective-permute-start(f32[384,1024]{1,0:T(8,128)} %mine.1), channel_id=1, source_target_pairs={{0,2},{1,3},{6,4},{7,5},{8,10},{9,11},{14,12},{15,13},{16,18},{17,... | collective-permute-start | bytes 4718600 | tf_op jit(solution)/shard_map/ppermute | solution.py:493
  282.7 1.6 select_add_fusion.1
  284.3 1.6 select_add_fusion.2
  285.9 2.1 fusion.1
  288.1 1.3 collective-permute-start.27
  289.4 10.2 %collective-permute-done.29 = f32[384,1024]{1,0:T(8,128)} collective-permute-done((f32[384,1024]{1,0:T(8,128)}, f32[384,1024]{1,0:T(8,128)}, u32[]{:S(2)}, u32[]{:S(2)}) %collective-permute-start.29) | collective-permute-done | bytes 1572896 | tf_op jit(solution)/shard_map/ppermute | solution.py:493
  299.9 5.9 %collective-permute-done.27 = f32[384,384]{0,1:T(8,128)S(1)} collective-permute-done((f32[384,384]{0,1:T(8,128)S(1)}, f32[384,384]{0,1:T(8,128)S(1)}, u32[]{:S(2)}, u32[]{:S(2)}) %collective-permute-start.27) | collective-permute-done | bytes 589856 | tf_op jit(solution)/shard_map/ppermute | solution.py:335
  305.9 1.3 collective-permute-start.28
  307.2 1.5 collective-permute-done.28
  309.9 26.1 %head.1.inverse = f32[384,384]{1,0:T(8,128)} custom-call(f32[384,384]{1,0:T(8,128)} %copy.10.head), custom_call_target="tpu_custom_call" | custom-call | flops 1000000 | bytes 87500000 | tf_op jit(solution)/shard_map/head/pallas_call | solution.py:508
  336.0 24.5 %columns.1.lc3 = bf16[1152,4096]{1,0:T(8,128)(2,1)} custom-call(s32[8]{0:T(128)} %compare_select_fusion.2.pos, s32[4,32]{1,0:T(4,128)} %quarters.9, f32[384,384]{1,0:T(8,128)} %head.1.inverse, f32[512,384]{1,0:T(8,128)} %copy.11.refs_0_, f32[512,384]{1,0:T(8,128)} %copy.12.refs_1_, f32[512,384]{1,0:T(8,128)} %copy.13.refs_2_, f32[512,384]{1,0:T(8,128)} %copy.14.refs_3_, ...), custom_call_target="tpu_custom_call" | custom-call | flops 1000000 | bytes 80500000 | tf_op jit(solution)/shard_map/columns/pallas_call | solution.py:519
  360.5 1.8 broadcast_select_fusion.2
  362.3 2.0 pad_maximum_fusion.across
  364.3 10.7 %rows.1 = (f32[2048,384]{1,0:T(8,128)}, bf16[2048,1152]{1,0:T(8,128)(2,1)}) custom-call(s32[8]{0:T(128)} %compare_select_fusion.2.pos, f32[384,384]{1,0:T(8,128)} %head.1.inverse, f32[384,2048]{1,0:T(8,128)} %pad_maximum_fusion.across), custom_call_target="tpu_custom_call" | custom-call | flops 1000000 | bytes 42000000 | tf_op jit(solution)/shard_map/rows/pallas_call | solution.py:532
  375.0 53.2 %final.1 = f32[2048,32,128]{2,1,0:T(8,128)} custom-call(s32[8]{0:T(128)} %compare_select_fusion.2.pos, s32[4,32]{1,0:T(4,128)} %quarters.9, f32[4,512,1024]{2,1,0:T(8,128)} %all-to-all-done.arrived, f32[2048,384]{1,0:T(8,128)} %get-tuple-element.41.lr, bf16[2048,1152]{1,0:T(8,128)(2,1)} %get-tuple-element.42.lr3, bf16[1152,4096]{1,0:T(8,128)(2,1)} %columns.1.lc3, ...), custom_call_target="tpu_custom_call" | custom-call | tf_op jit(solution)/shard_map/final/pallas_call | solution.py:545
  (77 shorter events, 21.1 us)
Async XLA Ops:
  0.8 36.0 %collective-permute-start.2 = (f32[128,128]{1,0:T(8,128)S(1)}, f32[128,128]{1,0:T(8,128)S(1)}, u32[]{:S(2)}, u32[]{:S(2)}) collective-permute-start(f32[128,128]{1,0:T(8,128)S(1)} %slice.129), channel_id=1, source_target_pairs={{0,2},{4,6},{8,10},{12,14},{16,18},{20,22},{24,26},{28,30}} | collective-permute-start | bytes 196616 | tf_op jit(solution)/shard_map/ppermute | solution.py:335
  8.0 36.3 %collective-permute-start = (f32[2048,128]{1,0:T(8,128)}, f32[2048,128]{1,0:T(8,128)}, u32[]{:S(2)}, u32[]{:S(2)}) collective-permute-start(f32[2048,128]{1,0:T(8,128)} %slice.128), channel_id=1, source_target_pairs={{0,2},{4,6},{8,10},{12,14},{16,18},{20,22},{24,26},{28,30}} | collective-permute-start | bytes 3145736 | tf_op jit(solution)/shard_map/ppermute | solution.py:335
  23.6 24.2 %collective-permute-start.8 = (f32[512,384]{0,1:T(8,128)}, f32[512,384]{0,1:T(8,128)}, u32[]{:S(2)}, u32[]{:S(2)}) collective-permute-start(f32[512,384]{0,1:T(8,128)} %copy.31), channel_id=1, source_target_pairs={{0,5},{4,7},{8,13},{12,15},{16,21},{20,23},{24,29},{28,31}} | collective-permute-start | bytes 2359304 | tf_op jit(solution)/shard_map/ppermute | solution.py:397
  27.0 23.8 %collective-permute-start.5 = (f32[512,384]{0,1:T(8,128)}, f32[512,384]{0,1:T(8,128)}, u32[]{:S(2)}, u32[]{:S(2)}) collective-permute-start(f32[512,384]{0,1:T(8,128)} %copy.28), channel_id=1, source_target_pairs={{0,0},{4,2},{8,8},{12,10},{16,16},{20,18},{24,24},{28,26}} | collective-permute-start | bytes 2359304 | tf_op jit(solution)/shard_map/ppermute | solution.py:397
  34.7 16.1 %collective-permute-start.7 = (f32[512,384]{0,1:T(8,128)S(1)}, f32[512,384]{0,1:T(8,128)}, u32[]{:S(2)}, u32[]{:S(2)}) collective-permute-start(f32[512,384]{0,1:T(8,128)S(1)} %copy.30), channel_id=1, source_target_pairs={{0,1},{4,3},{8,9},{12,11},{16,17},{20,19},{24,25},{28,27}} | collective-permute-start | bytes 2359304 | tf_op jit(solution)/shard_map/ppermute | solution.py:397
  37.7 3.6 collective-permute-start.3
  41.3 17.4 %collective-permute-start.6 = (f32[512,384]{0,1:T(8,128)}, f32[512,384]{0,1:T(8,128)}, u32[]{:S(2)}, u32[]{:S(2)}) collective-permute-start(f32[512,384]{0,1:T(8,128)} %copy.29), channel_id=1, source_target_pairs={{0,4},{4,6},{8,12},{12,14},{16,20},{20,22},{24,28},{28,30}} | collective-permute-start | bytes 2359304 | tf_op jit(solution)/shard_map/ppermute | solution.py:397
  44.4 23.3 %collective-permute-start.4 = (f32[128,1152]{1,0:T(8,128)}, f32[128,1152]{1,0:T(8,128)}, u32[]{:S(2)}, u32[]{:S(2)}) collective-permute-start(f32[128,1152]{1,0:T(8,128)} %pad_maximum_fusion.1), channel_id=1, source_target_pairs={{0,4},{1,5},{2,6},{3,7},{8,12},{9,13},{10,14},{11,15},{16,20},{17,... | collective-permute-start | bytes 1769480 | tf_op jit(solution)/shard_map/ppermute | solution.py:335
  47.8 19.9 %collective-permute-start.1 = (f32[2048,128]{1,0:T(8,128)S(1)}, f32[2048,128]{1,0:T(8,128)}, u32[]{:S(2)}, u32[]{:S(2)}) collective-permute-start(f32[2048,128]{1,0:T(8,128)S(1)} %broadcast_select_fusion.3), channel_id=1, source_target_pairs={{0,1},{2,3},{4,5},{6,7},{8,9},{10,11},{12,13},{14,15},{16,17},{18,... | collective-permute-start | bytes 3145736 | tf_op jit(solution)/shard_map/ppermute | solution.py:335
  60.9 15.6 %collective-permute-start.10 = (f32[512,384]{0,1:T(8,128)S(1)}, f32[512,384]{0,1:T(8,128)}, u32[]{:S(2)}, u32[]{:S(2)}) collective-permute-start(f32[512,384]{0,1:T(8,128)S(1)} %add_add_fusion), channel_id=1, source_target_pairs={{8,0},{16,8},{24,16},{9,1},{17,9},{25,17},{10,2},{18,10},{26,18},{... | collective-permute-start | bytes 2359304 | tf_op jit(solution)/shard_map/ppermute | solution.py:350
  62.2 21.3 %collective-permute-start.9 = (f32[512,384]{0,1:T(8,128)S(1)}, f32[512,384]{0,1:T(8,128)}, u32[]{:S(2)}, u32[]{:S(2)}) collective-permute-start(f32[512,384]{0,1:T(8,128)S(1)} %add_add_fusion), channel_id=1, source_target_pairs={{0,8},{8,16},{16,24},{1,9},{9,17},{17,25},{2,10},{10,18},{18,26},{... | collective-permute-start | bytes 2359304 | tf_op jit(solution)/shard_map/ppermute | solution.py:346
  83.4 26.9 %collective-permute-start.11 = (f32[512,384]{0,1:T(8,128)}, f32[512,384]{0,1:T(8,128)S(1)}, u32[]{:S(2)}, u32[]{:S(2)}) collective-permute-start(f32[512,384]{0,1:T(8,128)} %collective-permute-done.9), channel_id=1, source_target_pairs={{0,8},{8,16},{16,24},{1,9},{9,17},{17,25},{2,10},{10,18},{18,26},{... | collective-permute-start | bytes 2359304 | tf_op jit(solution)/shard_map/ppermute | solution.py:346
  88.0 27.9 %collective-permute-start.13 = (f32[512,384]{0,1:T(8,128)}, f32[512,384]{0,1:T(8,128)S(1)}, u32[]{:S(2)}, u32[]{:S(2)}) collective-permute-start(f32[512,384]{0,1:T(8,128)} %collective-permute-done.10), channel_id=1, source_target_pairs={{8,0},{16,8},{24,16},{9,1},{17,9},{25,17},{10,2},{18,10},{26,18},{... | collective-permute-start | bytes 2359304 | tf_op jit(solution)/shard_map/ppermute | solution.py:350
  107.9 9.5 %collective-permute-start.15 = (f32[128,1024]{1,0:T(8,128)}, f32[128,1024]{1,0:T(8,128)S(1)}, u32[]{:S(2)}, u32[]{:S(2)}) collective-permute-start(f32[128,1024]{1,0:T(8,128)} %slice.111), channel_id=1, source_target_pairs={{0,4},{1,5},{2,6},{3,7},{8,12},{9,13},{10,14},{11,15},{16,20},{17,... | collective-permute-start | bytes 1572872 | tf_op jit(solution)/shard_map/ppermute | solution.py:426
  110.4 24.0 %copy-start.1 = (f32[512,384]{0,1:T(8,128)}, f32[512,384]{0,1:T(8,128)S(1)}, u32[]{:S(2)}) copy-start(f32[512,384]{0,1:T(8,128)S(1)} %collective-permute-done.11) | copy-start | bytes 2359300
  110.4 82.9 %collective-permute-start.12 = (f32[512,384]{0,1:T(8,128)S(1)}, f32[512,384]{0,1:T(8,128)}, u32[]{:S(2)}, u32[]{:S(2)}) collective-permute-start(f32[512,384]{0,1:T(8,128)S(1)} %collective-permute-done.11), channel_id=1, source_target_pairs={{0,8},{8,16},{16,24},{1,9},{9,17},{17,25},{2,10},{10,18},{18,26},{... | collective-permute-start | bytes 2359304 | tf_op jit(solution)/shard_map/ppermute | solution.py:346
  115.9 18.5 %copy-start.3 = (f32[512,384]{0,1:T(8,128)}, f32[512,384]{0,1:T(8,128)S(1)}, u32[]{:S(2)}) copy-start(f32[512,384]{0,1:T(8,128)S(1)} %collective-permute-done.13) | copy-start | bytes 2359300
  115.9 77.4 %collective-permute-start.14 = (f32[512,384]{0,1:T(8,128)S(1)}, f32[512,384]{0,1:T(8,128)}, u32[]{:S(2)}, u32[]{:S(2)}) collective-permute-start(f32[512,384]{0,1:T(8,128)S(1)} %collective-permute-done.13), channel_id=1, source_target_pairs={{8,0},{16,8},{24,16},{9,1},{17,9},{25,17},{10,2},{18,10},{26,18},{... | collective-permute-start | bytes 2359304 | tf_op jit(solution)/shard_map/ppermute | solution.py:350
  119.3 25.9 %collective-permute-start.18 = (f32[128,1024]{1,0:T(8,128)}, f32[128,1024]{1,0:T(8,128)}, u32[]{:S(2)}, u32[]{:S(2)}) collective-permute-start(f32[128,1024]{1,0:T(8,128)} %select_add_fusion.refs_8_), channel_id=1, source_target_pairs={{0,24},{8,0},{16,8},{24,16},{1,25},{9,1},{17,9},{25,17},{2,26},{10... | collective-permute-start | bytes 1572872 | tf_op jit(solution)/shard_map/ppermute | solution.py:342
  123.9 69.3 %collective-permute-start.17 = (f32[128,1024]{1,0:T(8,128)}, f32[128,1024]{1,0:T(8,128)}, u32[]{:S(2)}, u32[]{:S(2)}) collective-permute-start(f32[128,1024]{1,0:T(8,128)} %select_add_fusion.refs_8_), channel_id=1, source_target_pairs={{0,16},{8,24},{16,0},{24,8},{1,17},{9,25},{17,1},{25,9},{2,18},{10... | collective-permute-start | bytes 1572872 | tf_op jit(solution)/shard_map/ppermute | solution.py:342
  123.9 69.3 %collective-permute-start.16 = (f32[128,1024]{1,0:T(8,128)}, f32[128,1024]{1,0:T(8,128)}, u32[]{:S(2)}, u32[]{:S(2)}) collective-permute-start(f32[128,1024]{1,0:T(8,128)} %select_add_fusion.refs_8_), channel_id=1, source_target_pairs={{0,8},{8,16},{16,24},{24,0},{1,9},{9,17},{17,25},{25,1},{2,10},{10... | collective-permute-start | bytes 1572872 | tf_op jit(solution)/shard_map/ppermute | solution.py:342
  134.4 64.6 %copy-start.4 = (s32[4,32]{1,0:T(4,128)S(1)}, s32[4,32]{1,0:T(4,128)}, u32[]{:S(2)}) copy-start(s32[4,32]{1,0:T(4,128)} %quarters.9) | copy-start | bytes 1540
  145.2 57.8 %copy-start.2 = (f32[512,384]{0,1:T(8,128)S(1)}, f32[512,384]{0,1:T(8,128)}, u32[]{:S(2)}) copy-start(f32[512,384]{0,1:T(8,128)} %copy-done.1) | copy-start | bytes 2359300
  193.3 181.7 %all-to-all-start = ((f32[4,512,1024]{2,1,0:T(8,128)}), f32[4,512,1024]{2,1,0:T(8,128)}, u32[]{:S(2)}, u32[]{:S(2)}) async-start(f32[4,512,1024]{2,1,0:T(8,128)} %outgoing.1), calls=%async_computation | async-start | bytes 16777216 | tf_op jit(solution)/shard_map/all_to_all | solution.py:442
  199.5 20.6 %collective-permute-start.19 = (f32[512,384]{0,1:T(8,128)S(1)}, f32[512,384]{0,1:T(8,128)}, u32[]{:S(2)}, u32[]{:S(2)}) collective-permute-start(f32[512,384]{0,1:T(8,128)S(1)} %add_add_fusion), channel_id=1, source_target_pairs={{0,4},{4,0},{1,5},{5,1},{2,6},{6,2},{3,7},{7,3},{8,12},{12,8},{9,1... | collective-permute-start | bytes 2359304 | tf_op jit(solution)/shard_map/ppermute | solution.py:342
  200.9 30.6 %collective-permute-start.22 = (f32[512,384]{0,1:T(8,128)S(1)}, f32[512,384]{0,1:T(8,128)}, u32[]{:S(2)}, u32[]{:S(2)}) collective-permute-start(f32[512,384]{0,1:T(8,128)S(1)} %broadcast_select_fusion.5), channel_id=1, source_target_pairs={{0,4},{4,0},{1,5},{5,1},{2,6},{6,2},{3,7},{7,3},{8,12},{12,8},{9,1... | collective-permute-start | bytes 2359304 | tf_op jit(solution)/shard_map/ppermute | solution.py:342
  204.2 35.7 %collective-permute-start.21 = (f32[512,384]{0,1:T(8,128)S(1)}, f32[512,384]{0,1:T(8,128)}, u32[]{:S(2)}, u32[]{:S(2)}) collective-permute-start(f32[512,384]{0,1:T(8,128)S(1)} %broadcast_select_fusion.6), channel_id=1, source_target_pairs={{0,4},{4,0},{1,5},{5,1},{2,6},{6,2},{3,7},{7,3},{8,12},{12,8},{9,1... | collective-permute-start | bytes 2359304 | tf_op jit(solution)/shard_map/ppermute | solution.py:342
  205.8 46.9 %collective-permute-start.20 = (f32[512,384]{0,1:T(8,128)S(1)}, f32[512,384]{0,1:T(8,128)}, u32[]{:S(2)}, u32[]{:S(2)}) collective-permute-start(f32[512,384]{0,1:T(8,128)S(1)} %broadcast_select_fusion.7), channel_id=1, source_target_pairs={{0,4},{4,0},{1,5},{5,1},{2,6},{6,2},{3,7},{7,3},{8,12},{12,8},{9,1... | collective-permute-start | bytes 2359304 | tf_op jit(solution)/shard_map/ppermute | solution.py:342
  207.9 47.0 %collective-permute-start.23 = (f32[128,1024]{1,0:T(8,128)}, f32[128,1024]{1,0:T(8,128)}, u32[]{:S(2)}, u32[]{:S(2)}) collective-permute-start(f32[128,1024]{1,0:T(8,128)} %select_add_fusion.refs_8_), channel_id=1, source_target_pairs={{0,4},{4,0},{1,5},{5,1},{2,6},{6,2},{3,7},{7,3},{8,12},{12,8},{9,1... | collective-permute-start | bytes 1572872 | tf_op jit(solution)/shard_map/ppermute | solution.py:342
  220.1 39.5 %collective-permute-start.24 = (f32[128,1024]{1,0:T(8,128)}, f32[128,1024]{1,0:T(8,128)}, u32[]{:S(2)}, u32[]{:S(2)}) collective-permute-start(f32[128,1024]{1,0:T(8,128)} %collective-permute-done.16.refs_10_), channel_id=1, source_target_pairs={{0,4},{4,0},{1,5},{5,1},{2,6},{6,2},{3,7},{7,3},{8,12},{12,8},{9,1... | collective-permute-start | bytes 1572872 | tf_op jit(solution)/shard_map/ppermute | solution.py:342
  231.5 33.7 %collective-permute-start.25 = (f32[128,1024]{1,0:T(8,128)}, f32[128,1024]{1,0:T(8,128)}, u32[]{:S(2)}, u32[]{:S(2)}) collective-permute-start(f32[128,1024]{1,0:T(8,128)} %collective-permute-done.17.refs_12_), channel_id=1, source_target_pairs={{0,4},{4,0},{1,5},{5,1},{2,6},{6,2},{3,7},{7,3},{8,12},{12,8},{9,1... | collective-permute-start | bytes 1572872 | tf_op jit(solution)/shard_map/ppermute | solution.py:342
  240.0 30.9 %collective-permute-start.26 = (f32[128,1024]{1,0:T(8,128)}, f32[128,1024]{1,0:T(8,128)}, u32[]{:S(2)}, u32[]{:S(2)}) collective-permute-start(f32[128,1024]{1,0:T(8,128)} %collective-permute-done.18.refs_14_), channel_id=1, source_target_pairs={{0,4},{4,0},{1,5},{5,1},{2,6},{6,2},{3,7},{7,3},{8,12},{12,8},{9,1... | collective-permute-start | bytes 1572872 | tf_op jit(solution)/shard_map/ppermute | solution.py:342
  277.5 22.1 %collective-permute-start.29 = (f32[384,1024]{1,0:T(8,128)}, f32[384,1024]{1,0:T(8,128)}, u32[]{:S(2)}, u32[]{:S(2)}) collective-permute-start(f32[384,1024]{1,0:T(8,128)} %mine.1), channel_id=1, source_target_pairs={{0,2},{1,3},{6,4},{7,5},{8,10},{9,11},{14,12},{15,13},{16,18},{17,... | collective-permute-start | bytes 4718600 | tf_op jit(solution)/shard_map/ppermute | solution.py:493
  285.9 13.7 %copy-start = (f32[384,1024]{1,0:T(8,128)S(1)}, f32[384,1024]{1,0:T(8,128)}, u32[]{:S(2)}) copy-start(f32[384,1024]{1,0:T(8,128)} %mine.1) | copy-start | bytes 4718596
  288.1 17.7 %collective-permute-start.27 = (f32[384,384]{0,1:T(8,128)S(1)}, f32[384,384]{0,1:T(8,128)S(1)}, u32[]{:S(2)}, u32[]{:S(2)}) collective-permute-start(f32[384,384]{0,1:T(8,128)S(1)} %fusion.1), channel_id=1, source_target_pairs={{0,2},{4,6},{8,10},{12,14},{16,18},{20,22},{24,26},{28,30}} | collective-permute-start | bytes 1769480 | tf_op jit(solution)/shard_map/ppermute | solution.py:335
  299.8 60.7 %collective-permute-start.30 = (f32[384,1024]{1,0:T(8,128)S(1)}, f32[384,1024]{1,0:T(8,128)}, u32[]{:S(2)}, u32[]{:S(2)}) collective-permute-start(f32[384,1024]{1,0:T(8,128)S(1)} %broadcast_select_fusion.1), channel_id=1, source_target_pairs={{0,1},{1,0},{2,3},{3,2},{4,5},{5,4},{6,7},{7,6},{8,9},{9,8},{10,11... | collective-permute-start | bytes 4718600 | tf_op jit(solution)/shard_map/ppermute | solution.py:499
  305.9 2.9 collective-permute-start.28

commit v3 on v2

--- a/solution.py
+++ b/solution.py
@@ -85,41 +85,51 @@
     return aug[:, n:] / jnp.sqrt(pivots)
 
 
-def extract_kernel(groups, view, out):
-    for h in range(out.shape[1] // B):
-        out[:, h * B : (h + 1) * B] = view[:, h * groups, :]
-
-
-def child_kernel(pos, live, quarters, block, strip, prow, lead_rows, brow3, bcol3, panel, aug, brow):
+def extract_kernel(groups, view, *outs):
+    for i, out in enumerate(outs):
+
+        @pl.when(pl.program_id(0) == i)
+        def _(out=out):
+            for h in range(out.shape[1] // B):
+                out[:, h * B : (h + 1) * B] = view[:, h * groups, :]
+
+
+def child_kernel(pos, live, quarters, corner, strip, prow, lead, brow3, bcol3, panel, aug, below):
     rows_here, cols_here = strip.shape[0], prow.shape[1]
+    share = lead.shape[0]
     grp, row, col = pos[0], pos[1], pos[2]
     live_end = live[grp] * B
-    inverse = invert_factor(block[...], aug)
+    inverse = invert_factor(corner[:LEAD], aug)
     row_ids = row * rows_here + lax.broadcasted_iota(jnp.int32, (rows_here, 1), 0)
     col_ids = col * cols_here + lax.broadcasted_iota(jnp.int32, (1, cols_here), 1)
     live_rows = (row_ids >= LEAD) & (row_ids < live_end)
     live_cols = (col_ids >= LEAD) & (col_ids < live_end)
-    brow[...] = jnp.where(live_rows, dot_nt(strip[...], inverse), 0.0)
     bcol = jnp.where(live_cols, dot_nn(inverse, prow[...]), 0.0)
-    hi, lo = split(brow[...])
-    brow3[:, :LEAD] = hi
-    brow3[:, LEAD : 2 * LEAD] = hi
-    brow3[:, 2 * LEAD :] = lo
+    below[...] = dot_nt(corner[LEAD:], inverse)
+    tall = min(share, B)
+    for i in range(0, share, tall):
+        at = pl.multiple_of(row * share + i, tall)
+        k = KC + lax.div(at, B)
+        keep = live_cols & (k * B < live_end) & (quarters[grp, k] == 0)
+        update = dot_nn(below[pl.ds(at, tall), :], bcol)
+        value = jnp.where(keep, lead[i : i + tall, :] - update, 0.0)
+        for g in range(panel.shape[0]):
+            panel[g, i : i + tall, :] = value
     hi, lo = split(bcol)
     bcol3[:LEAD] = hi
     bcol3[LEAD : 2 * LEAD] = lo
     bcol3[2 * LEAD :] = hi
-    for k in range(KC, KP):
-        at = (k - KC) * B
-        keep = live_cols & (k * B < live_end) & (quarters[grp, k] == 0)
-        update = dot_nn(brow[k * B : (k + 1) * B, :], bcol)
-        panel[at : at + B, :] = jnp.where(keep, lead_rows[at : at + B, :] - update, 0.0)
-
-
-def outgoing_kernel(pos, live, quarters, front, brow3, bcol3, out, gathered, picked):
+    hi, lo = split(jnp.where(live_rows, dot_nt(strip[...], inverse), 0.0))
+    brow3[:, :LEAD] = hi
+    brow3[:, LEAD : 2 * LEAD] = hi
+    brow3[:, 2 * LEAD :] = lo
+
+
+def outgoing_kernel(pos, live, quarters, front, brow3, bcol3, *refs):
+    *outs, gathered, picked = refs
     rows_here, cols_here = front.shape
     row_blocks = rows_here // B
-    slots = out.shape[1] // B
+    slots = gathered.shape[0] // B
     grp, row, col = pos[0], pos[1], pos[2]
     live_end = live[grp] * B
     target = pl.program_id(0)
@@ -137,7 +147,7 @@
     for s in range(slots):
         at = pl.multiple_of(picked[s] * B, B)
         gathered[s * B : (s + 1) * B, :] = brow3[pl.ds(at, B), :]
-    width = min(256, cols_here)
+    width = min(256, cols_here // len(outs))
     for n in range(cols_here // width):
         cut = slice(n * width, (n + 1) * width)
         product = dot_bf(gathered[...], bcol3[:, cut])
@@ -148,7 +158,8 @@
             first = row * rows_here + at
             keep = live_cols & (first >= LEAD) & (first < live_end)
             value = front[pl.ds(at, B), cut] - product[s * B : (s + 1) * B]
-            out[0, s * B : (s + 1) * B, cut] = jnp.where(keep, value, 0.0)
+            which, inner = divmod(n * width, cols_here // len(outs))
+            outs[which][0, s * B : (s + 1) * B, inner : inner + width] = jnp.where(keep, value, 0.0)
 
 
 def head_kernel(head, inverse, work, factor, aug):
@@ -174,36 +185,38 @@
             inverse[kk, jj] = -dot_nn(diag, total)
 
 
-def place_pieces(pos, quarters, pieces, panels, quarter, entries, placed):
+def place_pieces(pos, quarters, refs, quarter, entries, placed):
     groups = quarters.shape[0]
-    rows_n = len(pieces) // groups
-    part, share = pieces[0].shape[0], panels[0].shape[0]
+    own, own_panels, *others = refs
+    pieces, panels = others[: len(others) // 2], others[len(others) // 2 :]
+    rows_n = len(pieces) // groups + 1
+    part, share = own.shape[1], own_panels.shape[1]
     col_blocks = placed.shape[1] // B
-    grp, row, col = pos[0], pos[1], pos[2]
+    row, col = pos[1], pos[2]
     placed[...] = jnp.zeros_like(placed)
     for s in range(groups):
-        source = lax.rem(grp + groups - s, groups)
-
-        @pl.when(source == quarter)
-        def _(s=s):
+        mine = [own.at[s]] + list(pieces[s * (rows_n - 1) : (s + 1) * (rows_n - 1)])
+        added = [own_panels.at[s]] + list(panels[s * (rows_n - 1) : (s + 1) * (rows_n - 1)])
+
+        @pl.when(quarter == s)
+        def _(mine=mine):
             for t in range(rows_n):
                 at = pl.multiple_of(lax.rem(row + rows_n - t, rows_n) * part, part)
-                entries[pl.ds(at, part), :] = pieces[s * rows_n + t][...]
+                entries[pl.ds(at, part), :] = mine[t][...]
 
         for b in range(col_blocks):
             cut = slice(b * B, (b + 1) * B)
 
-            @pl.when(quarters[source, col * col_blocks + b] == quarter)
-            def _(s=s, cut=cut):
+            @pl.when(quarters[s, col * col_blocks + b] == quarter)
+            def _(added=added, cut=cut):
                 for t in range(rows_n):
                     at = pl.multiple_of(lax.rem(row + rows_n - t, rows_n) * share, share)
-                    placed[pl.ds(at, share), cut] += panels[s * rows_n + t][:, cut]
+                    placed[pl.ds(at, share), cut] += added[t][:, cut]
 
 
 def columns_kernel(pos, quarters, inverse, *refs):
     lc3, entries, placed = refs[-3:]
-    count = (len(refs) - 3) // 2
-    place_pieces(pos, quarters, refs[:count], refs[count : 2 * count], pl.program_id(0), entries, placed)
+    place_pieces(pos, quarters, refs[:-3], pl.program_id(0), entries, placed)
     value = dot_nt(inverse[...], entries[...]) + dot_nn(inverse[:, LEAD:], placed[...])
     hi, lo = split(value)
     lc3[:PIV] = hi
@@ -213,8 +226,7 @@
 
 def mine_kernel(pos, quarters, *refs):
     mine, entries, placed = refs[-3:]
-    count = (len(refs) - 3) // 2
-    place_pieces(pos, quarters, refs[:count], refs[count : 2 * count], pos[0], entries, placed)
+    place_pieces(pos, quarters, refs[:-3], pos[0], entries, placed)
     for k in range(KP):
         kk = slice(k * B, (k + 1) * B)
         value = jnp.transpose(entries[:, kk])
@@ -235,8 +247,10 @@
     lr3[:, 2 * PIV :] = lo
 
 
-def final_kernel(pos, quarters, arrived, lr, lr3, lc3, entries, out, acc, slot_of):
-    groups, _, cols_here = arrived.shape
+def final_kernel(offset, pos, quarters, arrived, lr, lr3, lc3, entries, *refs):
+    out, acc, slot_of = refs[-3:]
+    groups = quarters.shape[0]
+    cols_here = lc3.shape[1] // groups
     height = entries.shape[0]
     pair = entries.shape[1] // groups
     width = pair * B
@@ -256,7 +270,8 @@
 
             lax.fori_loop(0, row_blocks, note, jnp.int32(0))
 
-    start = pl.multiple_of(p * width, width)
+    inner = pl.multiple_of(p * width, width)
+    start = pl.multiple_of((p + offset) * width, width)
     left = lr3[...]
     for u in range(groups):
         product = dot_bf(left, lc3[:, pl.ds(pl.multiple_of(u * cols_here + start, width), width)])
@@ -271,8 +286,8 @@
             def _(g=g, b=b, slot=slot):
                 at = pl.multiple_of(slot * B, B)
                 for h in range(pair):
-                    place = quarters[g, col * (cols_here // B) + p * pair + h]
-                    value = arrived[g, pl.ds(at, B), pl.ds(pl.multiple_of(start + h * B, B), B)]
+                    place = quarters[g, col * (cols_here // B) + (p + offset) * pair + h]
+                    value = arrived[g, pl.ds(at, B), pl.ds(pl.multiple_of(inner + h * B, B), B)]
                     acc[h * groups + place, b * B : (b + 1) * B, :] += value
 
     step = 32
@@ -342,16 +357,13 @@
     return lax.ppermute(value, axis, [(i, (i + by) % size) for i in range(size)])
 
 
-def step_up(value, groups):
-    return lax.ppermute(value, "grp", [(i, i + 1) for i in range(groups - 1)])
-
-
-def step_down(value, groups):
-    return lax.ppermute(value, "grp", [(i + 1, i) for i in range(groups - 1)])
+def planes_of(value, groups):
+    return lax.all_to_all(jnp.broadcast_to(value[None], (groups,) + value.shape), "grp", split_axis=0, concat_axis=0)
 
 
 def across_rows(planes, rows_n):
-    return [v if t == 0 else ring_shift(v, "row", rows_n, t) for v in planes for t in range(rows_n)]
+    groups = planes.shape[0]
+    return [ring_shift(planes[g], "row", rows_n, t) for g in range(groups) for t in range(1, rows_n)]
 
 
 def shards(child_fronts, parent_entries, child_live, quarters):
@@ -372,77 +384,79 @@
     lanes = cols_here // B
     view = parent_entries.reshape(rows_here, groups, lanes, B).transpose(0, 2, 1, 3).reshape(rows_here, lanes * groups, B)
     wide = min(PIV, cols_here)
-    tall = min(512, rows_here)
+    part = cols_here // rows_n
     deep = -(-wide // B * groups // 8) * 8
     own = pl.pallas_call(
         functools.partial(extract_kernel, groups),
-        grid=(rows_here // tall,),
-        out_shape=shape((rows_here, wide), f32),
-        in_specs=[pl.BlockSpec((tall, deep, B), lambda i: (i, 0, 0))],
-        out_specs=pl.BlockSpec((tall, wide), lambda i: (i, 0)),
+        grid=(spans * rows_n,),
+        out_shape=[shape((part, wide), f32)] * (spans * rows_n),
+        in_specs=[pl.BlockSpec((part, deep, B), lambda i: (i, 0, 0))],
+        out_specs=[vmem()] * (spans * rows_n),
         compiler_params=params(),
         cost_estimate=cost(6),
         name="extract",
     )(view)
-    first_own = own
-    for other in range(1, -(-PIV // cols_here)):
-        wide = min(cols_here, PIV - other * cols_here)
-        own = jnp.concatenate([own, lax.ppermute(first_own[:, :wide], "col", [(other, 0)])], axis=1)
-    part = cols_here // rows_n
+    if wide < PIV:
+        owners = range(1, -(-PIV // cols_here))
+        widths = [min(cols_here, PIV - o * cols_here) for o in owners]
+        moved = [[lax.ppermute(x[:, :w], "col", [(o, 0)]) for o, w in zip(owners, widths)] for x in own]
+        own = [jnp.concatenate([x] + more, axis=1) for x, more in zip(own, moved)]
     pieces = []
     for h in range(spans):
         for r in range(rows_n):
-            at = (h * rows_n + r) * part
             pairs = [(s * cols_n, r * cols_n + s * spans + h) for s in range(rows_n)]
-            pieces.append(lax.ppermute(own[at : at + part], ("row", "col"), pairs))
+            pieces.append(lax.ppermute(own[h * rows_n + r], ("row", "col"), pairs))
+    pieces, front = lax.optimization_barrier((pieces, front))
     piece = functools.reduce(lambda a, b: a + b, pieces)
-    up = [piece, step_up(piece, groups)] + [None] * (groups - 2)
-    down = [piece, step_down(piece, groups)] + [None] * (groups - 2)
-
+    entry_planes = planes_of(piece, groups)
+
+    share = (PIV - LEAD) // rows_n
+    lead = jnp.where(row == 0, front[LEAD : LEAD + share], 0.0)
+    for r in range(1, rows_n):
+        at = LEAD + r * share
+        lead = lead + lax.ppermute(front[at : at + share], "row", [(0, r)])
     strip = bcast(front[:, :LEAD], "col", cols_n)
-    corner = bcast(front[:LEAD, :LEAD], "col", cols_n)
-    payload = bcast(jnp.concatenate([front[:LEAD], corner], axis=1), "row", rows_n)
-    strip, payload, up[1], down[1] = lax.optimization_barrier((strip, payload, up[1], down[1]))
-    for k in range(2, groups):
-        up[k], down[k] = step_up(up[k - 1], groups), step_down(down[k - 1], groups)
+    prow = bcast(front[:LEAD], "row", rows_n)
+    corner = bcast(bcast(front[:PIV, :LEAD], "col", cols_n), "row", rows_n)
     brow3, bcol3, panel = pl.pallas_call(
         child_kernel,
         out_shape=(
             shape((rows_here, 3 * LEAD), bf16),
             shape((3 * LEAD, cols_here), bf16),
-            shape((PIV - LEAD, cols_here), f32),
+            shape((groups, share, cols_here), f32),
         ),
         in_specs=[smem(), smem(), smem(), vmem(), vmem(), vmem(), vmem()],
         out_specs=(vmem(), vmem(), vmem()),
-        scratch_shapes=[pltpu.VMEM((LEAD, 2 * LEAD), f32), pltpu.VMEM((rows_here, LEAD), f32)],
-        compiler_params=params(),
-        cost_estimate=cost(20),
+        scratch_shapes=[pltpu.VMEM((LEAD, 2 * LEAD), f32), pltpu.VMEM((PIV - LEAD, LEAD), f32)],
+        compiler_params=params(),
+        cost_estimate=cost(15),
         name="child",
-    )(pos, child_live, quarters, payload[:, cols_here:], strip, payload[:, :cols_here], front[LEAD:PIV])
-
-    share = (PIV - LEAD) // rows_n
-    panel_piece = jnp.where(row == 0, panel[:share], 0.0)
-    for r in range(1, rows_n):
-        panel_piece = panel_piece + lax.ppermute(panel[r * share : (r + 1) * share], "row", [(0, r)])
-
+    )(pos, child_live, quarters, corner, strip, prow, lead)
+
+    pair = lanes
+    chunks = 1
     outgoing = pl.pallas_call(
         outgoing_kernel,
         grid=(groups,),
-        out_shape=shape((groups, slots * B, cols_here), f32),
+        out_shape=[shape((groups, slots * B, cols_here // chunks), f32)] * chunks,
         in_specs=[smem(), smem(), smem(), vmem(), vmem(), vmem()],
-        out_specs=pl.BlockSpec((1, slots * B, cols_here), lambda d: (d, 0, 0)),
+        out_specs=[pl.BlockSpec((1, slots * B, cols_here // chunks), lambda d: (d, 0, 0))] * chunks,
         scratch_shapes=[pltpu.VMEM((slots * B, 3 * LEAD), bf16), pltpu.SMEM((slots,), jnp.int32)],
         compiler_params=params(),
         cost_estimate=cost(10),
         name="outgoing",
     )(pos, child_live, quarters, front, brow3, bcol3)
 
-    planes = [panel_piece] + [ring_shift(panel_piece, "grp", groups, s) for s in range(1, groups)]
-    outgoing, up[1:], down[1:], planes[1:] = lax.optimization_barrier((outgoing, up[1:], down[1:], planes[1:]))
-    arrived = lax.all_to_all(outgoing, "grp", split_axis=0, concat_axis=0, tiled=True)
-    merged = [piece] + [jnp.where(grp >= s, up[s], down[groups - s]) for s in range(1, groups)]
-    entries_c = across_rows(merged, rows_n)
+    entry_planes, panel = lax.optimization_barrier((entry_planes, panel))
+    planes = lax.all_to_all(panel, "grp", split_axis=0, concat_axis=0, tiled=True)
+    entries_c = across_rows(entry_planes, rows_n)
+    early = entries_c[: len(entries_c) // 2]
+    outgoing, planes, early = lax.optimization_barrier((outgoing, planes, early))
+    entries_c[: len(early)] = early
+    arrived = [lax.all_to_all(x, "grp", split_axis=0, concat_axis=0, tiled=True) for x in outgoing]
     panels = across_rows(planes, rows_n)
+
+    sources = [entry_planes, planes] + entries_c + panels
 
     wide = min(PIV, cols_here)
     needed = min(part, wide)
@@ -452,13 +466,15 @@
         total, extra = zero, zero
         for s in range(groups):
             start = col * (cols_here // B)
-            which = lax.dynamic_slice(quarters, ((grp - s) % groups, start), (1, wide // B))
+            which = lax.dynamic_slice(quarters, (s, start), (1, wide // B))
             lanes_in = jnp.repeat(which == 0, B, axis=1)
             for t in range(rows_n):
                 here = (row - t) % rows_n == at
-                if at * part < wide:
-                    total = total + jnp.where(here & (grp == s), entries_c[s * rows_n + t][:needed], 0.0)
-                extra = extra + jnp.where(here & lanes_in, panels[s * rows_n + t][:, :wide], 0.0)
+                if at * part < wide and s == 0:
+                    value = entries_c[t - 1] if t else entry_planes[0]
+                    total = total + jnp.where(here, value[:needed], 0.0)
+                value = panels[s * (rows_n - 1) + t - 1] if t else planes[s]
+                extra = extra + jnp.where(here & lanes_in, value[:, :wide], 0.0)
         if at * part < wide:
             own_rows.append(total)
         added.append(extra)
@@ -473,13 +489,25 @@
     mine = pl.pallas_call(
         mine_kernel,
         out_shape=shape((PIV, cols_here), f32),
-        in_specs=[smem(), smem()] + [vmem()] * (len(entries_c) + len(panels)),
+        in_specs=[smem(), smem()] + [vmem()] * len(sources),
         out_specs=vmem(),
         scratch_shapes=[pltpu.VMEM((cols_here, PIV), f32), pltpu.VMEM((PIV - LEAD, cols_here), f32)],
         compiler_params=params(),
         cost_estimate=cost(6),
         name="mine",
-    )(pos, quarters, *entries_c, *panels)
+    )(pos, quarters, *sources)
+    mine, head = lax.optimization_barrier((mine, head))
+    inverse = pl.pallas_call(
+        head_kernel,
+        out_shape=shape((PIV, PIV), f32),
+        in_specs=[vmem()],
+        out_specs=vmem(),
+        scratch_shapes=[pltpu.VMEM((PIV, PIV), f32), pltpu.VMEM((PIV, PIV), f32), pltpu.VMEM((B, 2 * B), f32)],
+        compiler_params=params(),
+        cost_estimate=cost(25),
+        name="head",
+    )(head)
+
     y_n = cols_n // spans
     y_here = (col // spans - row) % y_n
     stride = y_n // 2
@@ -491,6 +519,8 @@
                     source, target = (r + y) % y_n * spans + k, (r + y + stride) % y_n * spans + k
                     pairs.append((r * cols_n + source, r * cols_n + target))
         moved = lax.ppermute(mine, ("row", "col"), pairs)
+        if stride == 1:
+            moved, inverse = lax.optimization_barrier((moved, inverse))
         mine = jnp.where(y_here % (2 * stride) == stride, moved, mine)
         stride //= 2
     parts = [mine]
@@ -505,28 +535,17 @@
         ],
         axis=1,
     )
-    inverse = pl.pallas_call(
-        head_kernel,
-        out_shape=shape((PIV, PIV), f32),
-        in_specs=[vmem()],
-        out_specs=vmem(),
-        scratch_shapes=[pltpu.VMEM((PIV, PIV), f32), pltpu.VMEM((PIV, PIV), f32), pltpu.VMEM((B, 2 * B), f32)],
-        compiler_params=params(),
-        cost_estimate=cost(25),
-        name="head",
-    )(head)
-
     lc3 = pl.pallas_call(
         columns_kernel,
         grid=(groups,),
         out_shape=shape((3 * PIV, groups * cols_here), bf16),
-        in_specs=[smem(), smem(), vmem()] + [vmem()] * (len(entries_c) + len(panels)),
+        in_specs=[smem(), smem(), vmem()] + [vmem()] * len(sources),
         out_specs=pl.BlockSpec((3 * PIV, cols_here), lambda u: (0, u)),
         scratch_shapes=[pltpu.VMEM((cols_here, PIV), f32), pltpu.VMEM((PIV - LEAD, cols_here), f32)],
         compiler_params=params(),
         cost_estimate=cost(23),
         name="columns",
-    )(pos, quarters, inverse, *entries_c, *panels)
+    )(pos, quarters, inverse, *sources)
 
     tall = min(256, rows_here)
     lr, lr3 = pl.pallas_call(
@@ -540,26 +559,33 @@
         name="rows",
     )(pos, inverse, across)
 
-    pair = 2
-    tall = min(512, rows_here)
-    result = pl.pallas_call(
-        final_kernel,
-        grid=(rows_here // tall, lanes // pair),
-        out_shape=shape((rows_here, lanes * groups, B), f32),
-        in_specs=[
-            smem(),
-            smem(),
-            vmem(),
-            pl.BlockSpec((tall, PIV), lambda i, p: (i, 0)),
-            pl.BlockSpec((tall, 3 * PIV), lambda i, p: (i, 0)),
-            vmem(),
-            pl.BlockSpec((tall, pair * groups, B), lambda i, p: (i, p, 0)),
-        ],
-        out_specs=pl.BlockSpec((tall, pair * groups, B), lambda i, p: (i, p, 0)),
-        scratch_shapes=[pltpu.VMEM((pair * groups, tall, B), f32), pltpu.SMEM((groups, row_blocks), jnp.int32)],
-        compiler_params=params(),
-        name="final",
-    )(pos, quarters, arrived, lr, lr3, lc3, view)
+    tall = min(256, rows_here)
+    steps = lanes // pair // chunks
+    result = None
+    for n in range(chunks):
+        block = pl.BlockSpec((tall, pair * groups, B), lambda i, p, n=n: (i, p + n * steps, 0))
+        before = [] if result is None else [result]
+        result = pl.pallas_call(
+            functools.partial(final_kernel, n * steps),
+            grid=(rows_here // tall, steps),
+            out_shape=shape((rows_here, lanes * groups, B), f32),
+            in_specs=[
+                smem(),
+                smem(),
+                vmem(),
+                pl.BlockSpec((tall, PIV), lambda i, p: (i, 0)),
+                pl.BlockSpec((tall, 3 * PIV), lambda i, p: (i, 0)),
+                vmem(),
+                block,
+            ]
+            + [pl.BlockSpec(memory_space=pl.ANY)] * len(before),
+            out_specs=block,
+            scratch_shapes=[pltpu.VMEM((pair * groups, tall, B), f32), pltpu.SMEM((groups, row_blocks), jnp.int32)],
+            input_output_aliases={7: 0} if before else {},
+            compiler_params=params(),
+            cost_estimate=cost(50 // chunks),
+            name="final",
+        )(pos, quarters, arrived[n], lr, lr3, lc3, view, *before)
     return result.reshape(rows_here, lanes, groups, B).transpose(0, 2, 1, 3).reshape(rows_here, groups, cols_here)
 
 

time: 431 us -> 405 us (0.940); the launches traced: 428 us -> 397 us
  waiting for transfers between devices: 146 us -> 134 us
  other arithmetic: 22.3 us -> 15 us
  local copies, waits for them, and re-layouts: 33.8 us -> 26.9 us
    ppermute x11 -> x5, starting transfers between devices: 35.8 us -> 13.7 us  [the longest x4 11 us: shards(): pieces.append(lax.ppermute(own[h * rows_n + r], ('row', 'col'), pairs))]
    ppermute x11 -> x8, starting transfers between devices: 11.5 us -> 28.6 us  [ring_shift(): lax.ppermute(value, axis, [(i, (i + by) % size) for i in range(size)])]
    ppermute x11 -> x8, waiting for transfers between devices: 106 us -> 89.7 us  [ring_shift(): lax.ppermute(value, axis, [(i, (i + by) % size) for i in range(size)])]
    ppermute x7 -> x8, waiting for transfers between devices: 7.42 us -> 18 us  [bcast(): moved = lax.ppermute(value, axis, pairs)]
    all_to_all x1 -> x3, starting transfers between devices: 5.63 us -> 14.1 us  [the longest x1 5.59 us: shards(): lax.all_to_all(x, 'grp', split_axis=0, concat_axis=0, tiled=True)]
    slice x7 -> x2, local copies, waits for them, and re-layouts: 10.6 us -> 3.24 us  [the longest x1 2.3 us: shards(): lead = lead + lax.ppermute(front[at:at + share], 'row', [(0, r)])]
    ppermute x11 -> x5, waiting for transfers between devices: 22.7 us -> 15.5 us  [the longest x4 15.5 us: shards(): pieces.append(lax.ppermute(own[h * rows_n + r], ('row', 'col'), pairs))]
    optimization_barrier x0 -> x4, local copies, waits for them, and re-layouts: none -> 6.92 us  [the longest x2 3.49 us: shards(): lax.optimization_barrier((outgoing, planes, early))]
  transfers between devices with their start and end apart: 32 -> 26, of which waited for: 15 -> 18; matrix products, arithmetic and copies ran while one was open for 13% -> 9% of each run, Pallas kernels for 23% -> 23%
where the time goes in v3:
time: 405 us; the launch traced here: 397 us
  Pallas kernels  148 us (37%)
  waiting for transfers between devices  134 us (33%)
  starting transfers between devices  73.4 us (18%)
  local copies, waits for them, and re-layouts  26.9 us (7%)
  other arithmetic  15 us (4%)
    ppermute x8, waiting for transfers between devices, ring_shift(): lax.ppermute(value, axis, [(i, (i + by) % size) for i in range(size)])  89.7 us
    pallas_call x1, Pallas kernels, shards(): pl.pallas_call(functools.partial(final_kernel, n * steps), grid=(rows_her...  49.3 us
    ppermute x8, starting transfers between devices, ring_shift(): lax.ppermute(value, axis, [(i, (i + by) % size) for i in range(size)])  28.6 us
    pallas_call x1, Pallas kernels, shards(): pl.pallas_call(head_kernel, out_shape=shape((PIV, PIV), f32), in_specs=[v...  26.1 us
    pallas_call x1, Pallas kernels, shards(): pl.pallas_call(columns_kernel, grid=(groups,), out_shape=shape((3 * PIV,...  24.4 us
    ppermute x8, waiting for transfers between devices, bcast(): moved = lax.ppermute(value, axis, pairs)  18 us
    ppermute x4, waiting for transfers between devices, shards(): pieces.append(lax.ppermute(own[h * rows_n + r], ('row', 'col'), pairs))  15.5 us
    ppermute x8, starting transfers between devices, bcast(): moved = lax.ppermute(value, axis, pairs)  14.6 us
  transfers between devices with their start and end apart: 26, of which 18 were waited for; matrix products, arithmetic and copies ran while one was open for 9% of the time, Pallas kernels for 23%

profile of v3, /device:TPU:0, one launch (start us, length us, event | category | flops | bytes accessed | tf_op | source)
XLA Modules:
  0.0 397.2 jit_solution(4687661297762669287)
XLA Ops:
  0.0 8.5 %extract.1 = (f32[512,384]{1,0:T(8,128)}, f32[512,384]{1,0:T(8,128)}, f32[512,384]{1,0:T(8,128)}, f32[512,384]{1,0:T(8,128)}) custom-call(f32[2048,32,128]{2,1,0:T(8,128)} %bitcast.97), custom_call_target="tpu_custom_call" | custom-call | flops 1000000 | bytes 21000000 | tf_op jit(solution)/shard_map/extract/pallas_call | solution.py:389
  8.5 1.8 collective-permute-start
  10.3 6.6 %collective-permute-start.1 = (f32[512,384]{1,0:T(8,128)}, f32[512,384]{1,0:T(8,128)S(1)}, u32[]{:S(2)}, u32[]{:S(2)}) collective-permute-start(f32[512,384]{1,0:T(8,128)} %get-tuple-element.30), channel_id=1, source_target_pairs={{0,4},{4,6},{8,12},{12,14},{16,20},{20,22},{24,28},{28,30}} | collective-permute-start | bytes 2359304 | tf_op jit(solution)/shard_map/ppermute | solution.py:408
  16.9 1.3 collective-permute-start.2
  18.2 1.3 collective-permute-start.3
  19.6 7.1 %collective-permute-done.1 = f32[512,384]{1,0:T(8,128)S(1)} collective-permute-done((f32[512,384]{1,0:T(8,128)}, f32[512,384]{1,0:T(8,128)S(1)}, u32[]{:S(2)}, u32[]{:S(2)}) %collective-permute-start.1) | collective-permute-done | bytes 786464 | tf_op jit(solution)/shard_map/ppermute | solution.py:408
  26.6 8.4 %collective-permute-done.3 = f32[512,384]{1,0:T(8,128)S(1)} collective-permute-done((f32[512,384]{1,0:T(8,128)}, f32[512,384]{1,0:T(8,128)S(1)}, u32[]{:S(2)}, u32[]{:S(2)}) %collective-permute-start.3) | collective-permute-done | bytes 786464 | tf_op jit(solution)/shard_map/ppermute | solution.py:408
  35.5 2.1 broadcast_in_dim.179
  37.6 4.9 %all-to-all-start = ((f32[4,512,384]{1,2,0:T(8,128)}), f32[4,512,384]{1,2,0:T(8,128)S(1)}, u32[]{:S(2)}, u32[]{:S(2)}) async-start(f32[4,512,384]{1,2,0:T(8,128)} %broadcast_in_dim.179), calls=%async_computation | async-start | bytes 6291456 | tf_op jit(solution)/shard_map/all_to_all | solution.py:361
  42.4 2.3 slice.89
  44.7 2.3 collective-permute-start.7
  47.0 0.9 slice.88
  47.9 1.3 collective-permute-start.4
  49.2 2.3 fusion.1
  51.5 2.7 collective-permute-start.10
  54.2 2.1 collective-permute-start.9
  56.3 2.3 collective-permute-done.7
  58.6 2.3 broadcast_select_fusion.3
  60.9 2.3 collective-permute-start.8
  63.2 0.9 broadcast_select_fusion.8
  64.2 1.3 collective-permute-start.5
  66.5 1.9 collective-permute-start.6
  68.5 8.8 %collective-permute-done.9 = f32[128,1024]{1,0:T(8,128)} collective-permute-done((f32[128,1024]{1,0:T(8,128)}, f32[128,1024]{1,0:T(8,128)}, u32[]{:S(2)}, u32[]{:S(2)}) %collective-permute-start.9) | collective-permute-done | bytes 524320 | tf_op jit(solution)/shard_map/ppermute | solution.py:350
  77.3 2.6 select_add_fusion
  79.9 1.2 collective-permute-done.6
  81.8 2.3 broadcast_select_fusion.4.strip
  84.1 12.5 %child.1 = (bf16[2048,384]{1,0:T(8,128)(2,1)}, bf16[384,1024]{1,0:T(8,128)(2,1)}, f32[4,128,1024]{2,1,0:T(8,128)}) custom-call(s32[8]{0:T(128)} %compare_select_fusion.2.pos, s32[4]{0:T(128)} %live.3, s32[4,32]{1,0:T(4,128)} %quarters.9, f32[384,128]{1,0:T(8,128)} %broadcast_select_fusion.10.corner, f32[2048,128]{1,0:T(8,128)} %broadcast_select_fusion.4.strip, ...), custom_call_target="tpu_custom_call" | custom-call | flops 1000000 | bytes 52500000 | tf_op jit(solution)/shard_map/child/pallas_call | solution.py:421
  96.6 2.2 all-to-all-done
  98.9 1.6 copy-done.1
  100.5 3.6 all-to-all-start.1
  104.1 3.5 slice_bitcast_fusion
  107.6 14.7 %collective-permute-start.12 = (f32[512,384]{0,1:T(8,128)}, f32[512,384]{0,1:T(8,128)}, u32[]{:S(2)}, u32[]{:S(2)}) collective-permute-start(f32[512,384]{0,1:T(8,128)} %get-tuple-element.69), channel_id=1, source_target_pairs={{0,4},{4,0},{1,5},{5,1},{2,6},{6,2},{3,7},{7,3},{8,12},{12,8},{9,1... | collective-permute-start | bytes 2359304 | tf_op jit(solution)/shard_map/ppermute | solution.py:357
  122.4 9.5 %outgoing.1 = f32[4,512,1024]{2,1,0:T(8,128)} custom-call(s32[8]{0:T(128)} %compare_select_fusion.2.pos, s32[4]{0:T(128)} %live.3, s32[4,32]{1,0:T(4,128)} %quarters.9, f32[2048,1024]{1,0:T(8,128)} %bitcast.105, bf16[2048,384]{1,0:T(8,128)(2,1)} %get-tuple-element.34.brow3, bf16[384,1024]{1,0:T(8,128)(2,1)} %get-tuple-element.35.bcol3), custom_call_target="tpu_custom_call" | custom-call | flops 1000000 | bytes 35000000 | tf_op jit(solution)/shard_map/outgoing/pallas_call | solution.py:438
  131.9 9.1 %collective-permute-done.12 = f32[512,384]{0,1:T(8,128)} collective-permute-done((f32[512,384]{0,1:T(8,128)}, f32[512,384]{0,1:T(8,128)}, u32[]{:S(2)}, u32[]{:S(2)}) %collective-permute-start.12) | collective-permute-done | bytes 786464 | tf_op jit(solution)/shard_map/ppermute | solution.py:357
  141.0 16.7 %collective-permute-done.11 = f32[512,384]{0,1:T(8,128)S(1)} collective-permute-done((f32[512,384]{0,1:T(8,128)}, f32[512,384]{0,1:T(8,128)S(1)}, u32[]{:S(2)}, u32[]{:S(2)}) %collective-permute-start.11) | collective-permute-done | bytes 786464 | tf_op jit(solution)/shard_map/ppermute | solution.py:357
  158.7 5.6 %all-to-all-start.2 = ((f32[4,512,1024]{2,1,0:T(8,128)}), f32[4,512,1024]{2,1,0:T(8,128)}, u32[]{:S(2)}, u32[]{:S(2)}) async-start(f32[4,512,1024]{2,1,0:T(8,128)} %outgoing.1), calls=%async_computation.2 | async-start | bytes 16777216 | tf_op jit(solution)/shard_map/all_to_all | solution.py:456
  165.5 9.6 %collective-permute-start.18 = (f32[128,1024]{1,0:T(8,128)S(1)}, f32[128,1024]{1,0:T(8,128)S(1)}, u32[]{:S(2)}, u32[]{:S(2)}) collective-permute-start(f32[128,1024]{1,0:T(8,128)S(1)} %get-tuple-element.71), channel_id=1, source_target_pairs={{0,4},{4,0},{1,5},{5,1},{2,6},{6,2},{3,7},{7,3},{8,12},{12,8},{9,1... | collective-permute-start | bytes 1572872 | tf_op jit(solution)/shard_map/ppermute | solution.py:357
  175.2 1.9 collective-permute-start.16
  177.4 10.4 %collective-permute-done.18.refs_9_ = f32[128,1024]{1,0:T(8,128)S(1)} collective-permute-done((f32[128,1024]{1,0:T(8,128)S(1)}, f32[128,1024]{1,0:T(8,128)S(1)}, u32[]{:S(2)}, u32[]{:S(2)}) %collective-permute-start.18) | collective-permute-done | bytes 524320 | tf_op jit(solution)/shard_map/ppermute | solution.py:357
  187.9 11.2 %collective-permute-done.17.refs_8_ = f32[128,1024]{1,0:T(8,128)S(1)} collective-permute-done((f32[128,1024]{1,0:T(8,128)S(1)}, f32[128,1024]{1,0:T(8,128)S(1)}, u32[]{:S(2)}, u32[]{:S(2)}) %collective-permute-start.17) | collective-permute-done | bytes 524320 | tf_op jit(solution)/shard_map/ppermute | solution.py:357
  199.1 11.2 %collective-permute-done.16.refs_7_ = f32[128,1024]{1,0:T(8,128)S(1)} collective-permute-done((f32[128,1024]{1,0:T(8,128)S(1)}, f32[128,1024]{1,0:T(8,128)S(1)}, u32[]{:S(2)}, u32[]{:S(2)}) %collective-permute-start.16) | collective-permute-done | bytes 524320 | tf_op jit(solution)/shard_map/ppermute | solution.py:357
  210.3 10.4 %collective-permute-done.15.refs_6_ = f32[128,1024]{1,0:T(8,128)S(1)} collective-permute-done((f32[128,1024]{1,0:T(8,128)S(1)}, f32[128,1024]{1,0:T(8,128)S(1)}, u32[]{:S(2)}, u32[]{:S(2)}) %collective-permute-start.15) | collective-permute-done | bytes 524320 | tf_op jit(solution)/shard_map/ppermute | solution.py:357
  221.6 1.3 collective-permute-start.19
  222.9 1.8 collective-permute-start.14
  225.0 5.3 %collective-permute-done.19 = f32[384,384]{0,1:T(8,128)S(1)} collective-permute-done((f32[384,384]{0,1:T(8,128)S(1)}, f32[384,384]{0,1:T(8,128)S(1)}, u32[]{:S(2)}, u32[]{:S(2)}) %collective-permute-start.19) | collective-permute-done | bytes 589856 | tf_op jit(solution)/shard_map/ppermute | solution.py:350
  231.1 2.1 collective-permute-start.20
  233.2 2.4 copy.7.refs_0_
  235.6 8.1 %collective-permute-done.14 = f32[512,384]{0,1:T(8,128)} collective-permute-done((f32[512,384]{0,1:T(8,128)}, f32[512,384]{0,1:T(8,128)}, u32[]{:S(2)}, u32[]{:S(2)}) %collective-permute-start.14) | collective-permute-done | bytes 786464 | tf_op jit(solution)/shard_map/ppermute | solution.py:357
  243.7 2.3 copy.11.refs_5_
  246.0 12.4 %collective-permute-done.13 = f32[512,384]{0,1:T(8,128)} collective-permute-done((f32[512,384]{0,1:T(8,128)}, f32[512,384]{0,1:T(8,128)}, u32[]{:S(2)}, u32[]{:S(2)}) %collective-permute-start.13) | collective-permute-done | bytes 786464 | tf_op jit(solution)/shard_map/ppermute | solution.py:357
  258.4 2.4 copy.10.refs_4_
  260.7 1.2 copy.8.refs_2_
  262.0 2.3 copy.9.refs_3_
  264.2 6.6 %mine.1 = f32[384,1024]{1,0:T(8,128)} custom-call(s32[8]{0:T(128)} %compare_select_fusion.2.pos, s32[4,32]{1,0:T(4,128)} %quarters.9, f32[4,512,384]{2,1,0:T(8,128)} %copy.7.refs_0_, f32[4,128,1024]{2,1,0:T(8,128)} %copy-done, f32[512,384]{1,0:T(8,128)} %copy.8.refs_2_, f32[512,384]{1,0:T(8,128)} %copy.9.refs_3_, f32[512,384]{1,0:T(8,128)} %copy.10.refs_4_, ...), custom_call_target="tpu_custom_call" | custom-call | flops 1000000 | bytes 21000000 | tf_op jit(solution)/shard_map/mine/pallas_call | solution.py:489
  270.8 1.3 broadcast_select_fusion.6
  272.1 2.4 collective-permute-start.21
  274.5 1.1 copy.12.head
  275.6 26.1 %head.1.inverse = f32[384,384]{1,0:T(8,128)} custom-call(f32[384,384]{1,0:T(8,128)} %copy.12.head), custom_call_target="tpu_custom_call" | custom-call | flops 1000000 | bytes 87500000 | tf_op jit(solution)/shard_map/head/pallas_call | solution.py:500
  301.7 3.9 collective-permute-done.21
  306.0 24.4 %columns.1.lc3 = bf16[1152,4096]{1,0:T(8,128)(2,1)} custom-call(s32[8]{0:T(128)} %compare_select_fusion.2.pos, s32[4,32]{1,0:T(4,128)} %quarters.9, f32[384,384]{1,0:T(8,128)} %head.1.inverse, f32[4,512,384]{2,1,0:T(8,128)} %copy.7.refs_0_, f32[4,128,1024]{2,1,0:T(8,128)} %copy-done, f32[512,384]{1,0:T(8,128)} %copy.8.refs_2_, f32[512,384]{1,0:T(8,128)} %copy.9.refs_3_, ...), custom_call_target="tpu_custom_call" | custom-call | flops 1000000 | bytes 80500000 | tf_op jit(solution)/shard_map/columns/pallas_call | solution.py:538
  330.7 2.0 pad_maximum_fusion.across
  332.7 10.7 %rows.1 = (f32[2048,384]{1,0:T(8,128)}, bf16[2048,1152]{1,0:T(8,128)(2,1)}) custom-call(s32[8]{0:T(128)} %compare_select_fusion.2.pos, f32[384,384]{1,0:T(8,128)} %head.1.inverse, f32[384,2048]{1,0:T(8,128)} %pad_maximum_fusion.across), custom_call_target="tpu_custom_call" | custom-call | flops 1000000 | bytes 42000000 | tf_op jit(solution)/shard_map/rows/pallas_call | solution.py:551
  343.4 4.5 %all-to-all-done.2.arrived = f32[4,512,1024]{2,1,0:T(8,128)} async-done(((f32[4,512,1024]{2,1,0:T(8,128)}), f32[4,512,1024]{2,1,0:T(8,128)}, u32[]{:S(2)}, u32[]{:S(2)}) %all-to-all-start.2) | async-done | bytes 8388640 | tf_op jit(solution)/shard_map/all_to_all | solution.py:456
  347.9 49.3 %final.1 = f32[2048,32,128]{2,1,0:T(8,128)} custom-call(s32[8]{0:T(128)} %compare_select_fusion.2.pos, s32[4,32]{1,0:T(4,128)} %quarters.9, f32[4,512,1024]{2,1,0:T(8,128)} %all-to-all-done.2.arrived, f32[2048,384]{1,0:T(8,128)} %get-tuple-element.51.lr, bf16[2048,1152]{1,0:T(8,128)(2,1)} %get-tuple-element.52.lr3, bf16[1152,4096]{1,0:T(8,128)(2,1)} %columns.1.lc3, ...), custom_call_target="tpu_custom_call" | custom-call | flops 1000000 | bytes 175000000 | tf_op jit(solution)/shard_map/final/pallas_call | solution.py:568
  (67 shorter events, 7.2 us)
Async XLA Ops:
  8.5 11.1 %collective-permute-start = (f32[512,384]{1,0:T(8,128)}, f32[512,384]{1,0:T(8,128)S(1)}, u32[]{:S(2)}, u32[]{:S(2)}) collective-permute-start(f32[512,384]{1,0:T(8,128)} %get-tuple-element.29), channel_id=1, source_target_pairs={{0,0},{4,2},{8,8},{12,10},{16,16},{20,18},{24,24},{28,26}} | collective-permute-start | bytes 2359304 | tf_op jit(solution)/shard_map/ppermute | solution.py:408
  10.3 16.3 %collective-permute-start.1 = (f32[512,384]{1,0:T(8,128)}, f32[512,384]{1,0:T(8,128)S(1)}, u32[]{:S(2)}, u32[]{:S(2)}) collective-permute-start(f32[512,384]{1,0:T(8,128)} %get-tuple-element.30), channel_id=1, source_target_pairs={{0,4},{4,6},{8,12},{12,14},{16,20},{20,22},{24,28},{28,30}} | collective-permute-start | bytes 2359304 | tf_op jit(solution)/shard_map/ppermute | solution.py:408
  16.9 9.8 %collective-permute-start.2 = (f32[512,384]{1,0:T(8,128)}, f32[512,384]{1,0:T(8,128)S(1)}, u32[]{:S(2)}, u32[]{:S(2)}) collective-permute-start(f32[512,384]{1,0:T(8,128)} %get-tuple-element.31), channel_id=1, source_target_pairs={{0,1},{4,3},{8,9},{12,11},{16,17},{20,19},{24,25},{28,27}} | collective-permute-start | bytes 2359304 | tf_op jit(solution)/shard_map/ppermute | solution.py:408
  18.2 16.8 %collective-permute-start.3 = (f32[512,384]{1,0:T(8,128)}, f32[512,384]{1,0:T(8,128)S(1)}, u32[]{:S(2)}, u32[]{:S(2)}) collective-permute-start(f32[512,384]{1,0:T(8,128)} %get-tuple-element.32), channel_id=1, source_target_pairs={{0,5},{4,7},{8,13},{12,15},{16,21},{20,23},{24,29},{28,31}} | collective-permute-start | bytes 2359304 | tf_op jit(solution)/shard_map/ppermute | solution.py:408
  37.6 61.3 %all-to-all-start = ((f32[4,512,384]{1,2,0:T(8,128)}), f32[4,512,384]{1,2,0:T(8,128)S(1)}, u32[]{:S(2)}, u32[]{:S(2)}) async-start(f32[4,512,384]{1,2,0:T(8,128)} %broadcast_in_dim.179), calls=%async_computation | async-start | bytes 6291456 | tf_op jit(solution)/shard_map/all_to_all | solution.py:361
  44.7 13.9 %collective-permute-start.7 = (f32[2048,128]{1,0:T(8,128)}, f32[2048,128]{1,0:T(8,128)}, u32[]{:S(2)}, u32[]{:S(2)}) collective-permute-start(f32[2048,128]{1,0:T(8,128)} %slice.89), channel_id=1, source_target_pairs={{0,2},{4,6},{8,10},{12,14},{16,18},{20,22},{24,26},{28,30}} | collective-permute-start | bytes 3145736 | tf_op jit(solution)/shard_map/ppermute | solution.py:350
  47.9 15.3 %collective-permute-start.4 = (f32[384,128]{1,0:T(8,128)S(1)}, f32[384,128]{1,0:T(8,128)S(1)}, u32[]{:S(2)}, u32[]{:S(2)}) collective-permute-start(f32[384,128]{1,0:T(8,128)S(1)} %slice.88), channel_id=1, source_target_pairs={{0,2},{4,6},{8,10},{12,14},{16,18},{20,22},{24,26},{28,30}} | collective-permute-start | bytes 589832 | tf_op jit(solution)/shard_map/ppermute | solution.py:350
  51.5 17.0 %collective-permute-start.10 = (f32[128,1024]{1,0:T(8,128)}, f32[128,1024]{1,0:T(8,128)}, u32[]{:S(2)}, u32[]{:S(2)}) collective-permute-start(f32[128,1024]{1,0:T(8,128)} %get-tuple-element.63), channel_id=1, source_target_pairs={{0,4},{1,5},{2,6},{3,7},{8,12},{9,13},{10,14},{11,15},{16,20},{17,... | collective-permute-start | bytes 1572872 | tf_op jit(solution)/shard_map/ppermute | solution.py:417
  54.2 23.1 %collective-permute-start.9 = (f32[128,1024]{1,0:T(8,128)}, f32[128,1024]{1,0:T(8,128)}, u32[]{:S(2)}, u32[]{:S(2)}) collective-permute-start(f32[128,1024]{1,0:T(8,128)} %get-tuple-element.64), channel_id=1, source_target_pairs={{0,4},{1,5},{2,6},{3,7},{8,12},{9,13},{10,14},{11,15},{16,20},{17,... | collective-permute-start | bytes 1572872 | tf_op jit(solution)/shard_map/ppermute | solution.py:350
  60.9 20.9 %collective-permute-start.8 = (f32[2048,128]{1,0:T(8,128)}, f32[2048,128]{1,0:T(8,128)}, u32[]{:S(2)}, u32[]{:S(2)}) collective-permute-start(f32[2048,128]{1,0:T(8,128)} %broadcast_select_fusion.3), channel_id=1, source_target_pairs={{0,1},{2,3},{4,5},{6,7},{8,9},{10,11},{12,13},{14,15},{16,17},{18,... | collective-permute-start | bytes 3145736 | tf_op jit(solution)/shard_map/ppermute | solution.py:350
  64.2 2.4 collective-permute-start.5
  66.5 14.5 %collective-permute-start.6 = (f32[384,128]{1,0:T(8,128)S(1)}, f32[384,128]{1,0:T(8,128)S(1)}, u32[]{:S(2)}, u32[]{:S(2)}) collective-permute-start(f32[384,128]{1,0:T(8,128)S(1)} %broadcast_select_fusion.9), channel_id=1, source_target_pairs={{0,4},{1,5},{2,6},{3,7},{8,12},{9,13},{10,14},{11,15},{16,20},{17,... | collective-permute-start | bytes 589832 | tf_op jit(solution)/shard_map/ppermute | solution.py:350
  98.9 1.6 copy-start.1
  100.5 57.3 %all-to-all-start.1 = ((f32[4,128,1024]{2,1,0:T(8,128)}), f32[4,128,1024]{2,1,0:T(8,128)S(1)}, u32[]{:S(2)}, u32[]{:S(2)}) async-start(f32[4,128,1024]{2,1,0:T(8,128)} %get-tuple-element.41), calls=%async_computation.1 | async-start | bytes 4194304 | tf_op jit(solution)/shard_map/all_to_all | solution.py:451
  107.6 33.4 %collective-permute-start.12 = (f32[512,384]{0,1:T(8,128)}, f32[512,384]{0,1:T(8,128)}, u32[]{:S(2)}, u32[]{:S(2)}) collective-permute-start(f32[512,384]{0,1:T(8,128)} %get-tuple-element.69), channel_id=1, source_target_pairs={{0,4},{4,0},{1,5},{5,1},{2,6},{6,2},{3,7},{7,3},{8,12},{12,8},{9,1... | collective-permute-start | bytes 2359304 | tf_op jit(solution)/shard_map/ppermute | solution.py:357
  122.4 35.4 %collective-permute-start.11 = (f32[512,384]{0,1:T(8,128)}, f32[512,384]{0,1:T(8,128)S(1)}, u32[]{:S(2)}, u32[]{:S(2)}) collective-permute-start(f32[512,384]{0,1:T(8,128)} %get-tuple-element.70), channel_id=1, source_target_pairs={{0,4},{4,0},{1,5},{5,1},{2,6},{6,2},{3,7},{7,3},{8,12},{12,8},{9,1... | collective-permute-start | bytes 2359304 | tf_op jit(solution)/shard_map/ppermute | solution.py:357
  131.9 32.4 %copy-start.11 = (s32[4,32]{1,0:T(4,128)S(1)}, s32[4,32]{1,0:T(4,128)}, u32[]{:S(2)}) copy-start(s32[4,32]{1,0:T(4,128)} %quarters.9) | copy-start | bytes 1540
  157.8 0.9 copy-start.8
  157.8 7.4 %copy-start = (f32[4,128,1024]{2,1,0:T(8,128)}, f32[4,128,1024]{2,1,0:T(8,128)S(1)}, u32[]{:S(2)}) copy-start(f32[4,128,1024]{2,1,0:T(8,128)S(1)} %all-to-all-done.1.refs_1_) | copy-start | bytes 6291460
  158.7 189.2 %all-to-all-start.2 = ((f32[4,512,1024]{2,1,0:T(8,128)}), f32[4,512,1024]{2,1,0:T(8,128)}, u32[]{:S(2)}, u32[]{:S(2)}) async-start(f32[4,512,1024]{2,1,0:T(8,128)} %outgoing.1), calls=%async_computation.2 | async-start | bytes 16777216 | tf_op jit(solution)/shard_map/all_to_all | solution.py:456
  165.5 55.8 %copy-start.2 = (f32[4,512,384]{1,2,0:T(8,128)S(1)}, f32[4,512,384]{1,2,0:T(8,128)}, u32[]{:S(2)}) copy-start(f32[4,512,384]{1,2,0:T(8,128)} %copy-done.1) | copy-start | bytes 9437188
  165.5 55.8 %copy-start.9 = (f32[512,384]{0,1:T(8,128)S(1)}, f32[512,384]{0,1:T(8,128)}, u32[]{:S(2)}) copy-start(f32[512,384]{0,1:T(8,128)} %copy-done.8) | copy-start | bytes 2359300
  165.5 22.4 %collective-permute-start.18 = (f32[128,1024]{1,0:T(8,128)S(1)}, f32[128,1024]{1,0:T(8,128)S(1)}, u32[]{:S(2)}, u32[]{:S(2)}) collective-permute-start(f32[128,1024]{1,0:T(8,128)S(1)} %get-tuple-element.71), channel_id=1, source_target_pairs={{0,4},{4,0},{1,5},{5,1},{2,6},{6,2},{3,7},{7,3},{8,12},{12,8},{9,1... | collective-permute-start | bytes 1572872 | tf_op jit(solution)/shard_map/ppermute | solution.py:357
  175.1 24.0 %collective-permute-start.17 = (f32[128,1024]{1,0:T(8,128)S(1)}, f32[128,1024]{1,0:T(8,128)S(1)}, u32[]{:S(2)}, u32[]{:S(2)}) collective-permute-start(f32[128,1024]{1,0:T(8,128)S(1)} %get-tuple-element.72), channel_id=1, source_target_pairs={{0,4},{4,0},{1,5},{5,1},{2,6},{6,2},{3,7},{7,3},{8,12},{12,8},{9,1... | collective-permute-start | bytes 1572872 | tf_op jit(solution)/shard_map/ppermute | solution.py:357
  175.2 35.2 %collective-permute-start.16 = (f32[128,1024]{1,0:T(8,128)S(1)}, f32[128,1024]{1,0:T(8,128)S(1)}, u32[]{:S(2)}, u32[]{:S(2)}) collective-permute-start(f32[128,1024]{1,0:T(8,128)S(1)} %get-tuple-element.73), channel_id=1, source_target_pairs={{0,4},{4,0},{1,5},{5,1},{2,6},{6,2},{3,7},{7,3},{8,12},{12,8},{9,1... | collective-permute-start | bytes 1572872 | tf_op jit(solution)/shard_map/ppermute | solution.py:357
  177.1 43.7 %collective-permute-start.15 = (f32[128,1024]{1,0:T(8,128)S(1)}, f32[128,1024]{1,0:T(8,128)S(1)}, u32[]{:S(2)}, u32[]{:S(2)}) collective-permute-start(f32[128,1024]{1,0:T(8,128)S(1)} %get-tuple-element.74), channel_id=1, source_target_pairs={{0,4},{4,0},{1,5},{5,1},{2,6},{6,2},{3,7},{7,3},{8,12},{12,8},{9,1... | collective-permute-start | bytes 1572872 | tf_op jit(solution)/shard_map/ppermute | solution.py:357
  187.9 33.5 %copy-start.4 = (f32[128,1024]{1,0:T(8,128)}, f32[128,1024]{1,0:T(8,128)S(1)}, u32[]{:S(2)}) copy-start(f32[128,1024]{1,0:T(8,128)S(1)} %collective-permute-done.18.refs_9_) | copy-start | bytes 1572868
  199.1 22.3 %copy-start.5 = (f32[128,1024]{1,0:T(8,128)}, f32[128,1024]{1,0:T(8,128)S(1)}, u32[]{:S(2)}) copy-start(f32[128,1024]{1,0:T(8,128)S(1)} %collective-permute-done.17.refs_8_) | copy-start | bytes 1572868
  210.3 11.1 %copy-start.6 = (f32[128,1024]{1,0:T(8,128)}, f32[128,1024]{1,0:T(8,128)S(1)}, u32[]{:S(2)}) copy-start(f32[128,1024]{1,0:T(8,128)S(1)} %collective-permute-done.16.refs_7_) | copy-start | bytes 1572868
  220.8 0.8 copy-start.7
  221.6 8.7 %collective-permute-start.19 = (f32[384,384]{0,1:T(8,128)S(1)}, f32[384,384]{0,1:T(8,128)S(1)}, u32[]{:S(2)}, u32[]{:S(2)}) collective-permute-start(f32[384,384]{0,1:T(8,128)S(1)} %fusion), channel_id=1, source_target_pairs={{0,2},{4,6},{8,10},{12,14},{16,18},{20,22},{24,26},{28,30}} | collective-permute-start | bytes 1769480 | tf_op jit(solution)/shard_map/ppermute | solution.py:350
  222.9 20.8 %collective-permute-start.14 = (f32[512,384]{0,1:T(8,128)}, f32[512,384]{0,1:T(8,128)}, u32[]{:S(2)}, u32[]{:S(2)}) collective-permute-start(f32[512,384]{0,1:T(8,128)} %get-tuple-element.67), channel_id=1, source_target_pairs={{0,4},{4,0},{1,5},{5,1},{2,6},{6,2},{3,7},{7,3},{8,12},{12,8},{9,1... | collective-permute-start | bytes 2359304 | tf_op jit(solution)/shard_map/ppermute | solution.py:357
  224.7 33.7 %collective-permute-start.13 = (f32[512,384]{0,1:T(8,128)}, f32[512,384]{0,1:T(8,128)}, u32[]{:S(2)}, u32[]{:S(2)}) collective-permute-start(f32[512,384]{0,1:T(8,128)} %get-tuple-element.68), channel_id=1, source_target_pairs={{0,4},{4,0},{1,5},{5,1},{2,6},{6,2},{3,7},{7,3},{8,12},{12,8},{9,1... | collective-permute-start | bytes 2359304 | tf_op jit(solution)/shard_map/ppermute | solution.py:357
  231.1 39.7 %collective-permute-start.20 = (f32[384,384]{0,1:T(8,128)}, f32[384,384]{0,1:T(8,128)}, u32[]{:S(2)}, u32[]{:S(2)}) collective-permute-start(f32[384,384]{0,1:T(8,128)} %broadcast_select_fusion.5), channel_id=1, source_target_pairs={{0,1},{2,3},{4,5},{6,7},{8,9},{10,11},{12,13},{14,15},{16,17},{18,... | collective-permute-start | bytes 1769480 | tf_op jit(solution)/shard_map/ppermute | solution.py:350
  235.6 25.2 %copy-start.10 = (f32[512,384]{0,1:T(8,128)S(1)}, f32[512,384]{0,1:T(8,128)}, u32[]{:S(2)}) copy-start(f32[512,384]{0,1:T(8,128)} %copy-done.8) | copy-start | bytes 2359300
  270.8 34.8 %copy-start.3 = (f32[384,1024]{1,0:T(8,128)S(1)}, f32[384,1024]{1,0:T(8,128)}, u32[]{:S(2)}) copy-start(f32[384,1024]{1,0:T(8,128)} %mine.1) | copy-start | bytes 4718596
  272.1 33.5 %collective-permute-start.21 = (f32[384,1024]{1,0:T(8,128)}, f32[384,1024]{1,0:T(8,128)}, u32[]{:S(2)}, u32[]{:S(2)}) collective-permute-start(f32[384,1024]{1,0:T(8,128)} %mine.1), channel_id=1, source_target_pairs={{0,2},{1,3},{6,4},{7,5},{8,10},{9,11},{14,12},{15,13},{16,18},{17,... | collective-permute-start | bytes 4718600 | tf_op jit(solution)/shard_map/ppermute | solution.py:521
  305.8 24.6 %collective-permute-start.22 = (f32[384,1024]{1,0:T(8,128)S(1)}, f32[384,1024]{1,0:T(8,128)S(1)}, u32[]{:S(2)}, u32[]{:S(2)}) collective-permute-start(f32[384,1024]{1,0:T(8,128)S(1)} %broadcast_select_fusion.1), channel_id=1, source_target_pairs={{0,1},{1,0},{2,3},{3,2},{4,5},{5,4},{6,7},{7,6},{8,9},{9,8},{10,11... | collective-permute-start | bytes 4718600 | tf_op jit(solution)/shard_map/ppermute | solution.py:529

commit v4 on v3

--- a/solution.py
+++ b/solution.py
@@ -217,7 +217,8 @@
 def columns_kernel(pos, quarters, inverse, *refs):
     lc3, entries, placed = refs[-3:]
     place_pieces(pos, quarters, refs[:-3], pl.program_id(0), entries, placed)
-    value = dot_nt(inverse[...], entries[...]) + dot_nn(inverse[:, LEAD:], placed[...])
+    entries[:, LEAD:] += jnp.transpose(placed[...])
+    value = dot_nt(inverse[...], entries[...])
     hi, lo = split(value)
     lc3[:PIV] = hi
     lc3[PIV : 2 * PIV] = lo
@@ -247,8 +248,8 @@
     lr3[:, 2 * PIV :] = lo
 
 
-def final_kernel(offset, pos, quarters, arrived, lr, lr3, lc3, entries, *refs):
-    out, acc, slot_of = refs[-3:]
+def final_kernel(offset, pos, quarters, incoming, lr, lr3, lc3, entries, *refs):
+    out, acc, slot_of, arrived, ready = refs[-5:]
     groups = quarters.shape[0]
     cols_here = lc3.shape[1] // groups
     height = entries.shape[0]
@@ -259,8 +260,11 @@
     grp, row, col, first_row = pos[0], pos[1], pos[2], pos[3]
     rb, p = pl.program_id(0), pl.program_id(1)
 
+    load = pltpu.make_async_copy(incoming, arrived, ready)
+
     @pl.when((rb == 0) & (p == 0))
     def _():
+        load.start()
         for g in range(groups):
 
             def note(b, count, g=g):
@@ -277,6 +281,10 @@
         product = dot_bf(left, lc3[:, pl.ds(pl.multiple_of(u * cols_here + start, width), width)])
         for h in range(pair):
             acc[h * groups + u] = -product[:, h * B : (h + 1) * B]
+
+    @pl.when((rb == 0) & (p == 0))
+    def _():
+        load.wait()
 
     for g in range(groups):
         for b in range(blocks):
@@ -386,16 +394,19 @@
     wide = min(PIV, cols_here)
     part = cols_here // rows_n
     deep = -(-wide // B * groups // 8) * 8
-    own = pl.pallas_call(
-        functools.partial(extract_kernel, groups),
-        grid=(spans * rows_n,),
-        out_shape=[shape((part, wide), f32)] * (spans * rows_n),
-        in_specs=[pl.BlockSpec((part, deep, B), lambda i: (i, 0, 0))],
-        out_specs=[vmem()] * (spans * rows_n),
-        compiler_params=params(),
-        cost_estimate=cost(6),
-        name="extract",
-    )(view)
+    own = []
+    each = spans * rows_n // 2 or 1
+    for start in range(0, spans * rows_n, each):
+        own += pl.pallas_call(
+            functools.partial(extract_kernel, groups),
+            grid=(each,),
+            out_shape=[shape((part, wide), f32)] * each,
+            in_specs=[pl.BlockSpec((part, deep, B), lambda i, start=start: (i + start, 0, 0))],
+            out_specs=[vmem()] * each,
+            compiler_params=params(),
+            cost_estimate=cost(4),
+            name="extract",
+        )(view)
     if wide < PIV:
         owners = range(1, -(-PIV // cols_here))
         widths = [min(cols_here, PIV - o * cols_here) for o in owners]
@@ -572,7 +583,7 @@
             in_specs=[
                 smem(),
                 smem(),
-                vmem(),
+                pl.BlockSpec(memory_space=pl.ANY),
                 pl.BlockSpec((tall, PIV), lambda i, p: (i, 0)),
                 pl.BlockSpec((tall, 3 * PIV), lambda i, p: (i, 0)),
                 vmem(),
@@ -580,7 +591,12 @@
             ]
             + [pl.BlockSpec(memory_space=pl.ANY)] * len(before),
             out_specs=block,
-            scratch_shapes=[pltpu.VMEM((pair * groups, tall, B), f32), pltpu.SMEM((groups, row_blocks), jnp.int32)],
+            scratch_shapes=[
+                pltpu.VMEM((pair * groups, tall, B), f32),
+                pltpu.SMEM((groups, row_blocks), jnp.int32),
+                pltpu.VMEM(arrived[n].shape, f32),
+                pltpu.SemaphoreType.DMA(()),
+            ],
             input_output_aliases={7: 0} if before else {},
             compiler_params=params(),
             cost_estimate=cost(50 // chunks),

time: 405 us -> 385 us (0.951)
  waiting for transfers between devices: 134 us -> 114 us
  starting transfers between devices: 73.4 us -> 79.3 us
  Pallas kernels: 148 us -> 143 us
    ppermute x8, waiting for transfers between devices: 89.7 us -> 79.3 us  [ring_shift(): lax.ppermute(value, axis, [(i, (i + by) % size) for i in range(size)])]
    ppermute x8, waiting for transfers between devices: 18 us -> 8.21 us  [bcast(): moved = lax.ppermute(value, axis, pairs)]
    ppermute x8, starting transfers between devices: 28.6 us -> 20.6 us  [ring_shift(): lax.ppermute(value, axis, [(i, (i + by) % size) for i in range(size)])]
    ppermute x8, starting transfers between devices: 14.6 us -> 22.4 us  [bcast(): moved = lax.ppermute(value, axis, pairs)]
    ppermute x4, waiting for transfers between devices: 15.5 us -> 9.73 us  [shards(): pieces.append(lax.ppermute(own[h * rows_n + r], ('row', 'col'), pairs))]
    ppermute x1, starting transfers between devices: 2.43 us -> 7.12 us  [shards(): moved = lax.ppermute(mine, ('row', 'col'), pairs)]
    pallas_call x1, Pallas kernels: 24.4 us -> 19.8 us  [shards(): pl.pallas_call(columns_kernel, grid=(groups,), out_shape=shape((3 * PIV,...]
    pallas_call x1 -> x2, Pallas kernels: 8.51 us -> 10.2 us  [shards(): pl.pallas_call(functools.partial(extract_kernel, groups), grid=(each,), o...]
  transfers between devices with their start and end apart: 26 -> 26, of which waited for: 18 -> 17; matrix products, arithmetic and copies ran while one was open for 9% -> 10% of each run, Pallas kernels for 23% -> 24%
where the time goes in v4:
time: 385 us; the launch traced here: 377 us
  Pallas kernels  143 us (37%)
  waiting for transfers between devices  114 us (30%)
  starting transfers between devices  79.3 us (21%)
  local copies, waits for them, and re-layouts  26.1 us (7%)
  other arithmetic  15 us (4%)
    ppermute x8, waiting for transfers between devices, ring_shift(): lax.ppermute(value, axis, [(i, (i + by) % size) for i in range(size)])  79.3 us
    pallas_call x1, Pallas kernels, shards(): pl.pallas_call(functools.partial(final_kernel, n * steps), grid=(rows_her...  47.4 us
    pallas_call x1, Pallas kernels, shards(): pl.pallas_call(head_kernel, out_shape=shape((PIV, PIV), f32), in_specs=[v...  26.1 us
    ppermute x8, starting transfers between devices, bcast(): moved = lax.ppermute(value, axis, pairs)  22.4 us
    ppermute x8, starting transfers between devices, ring_shift(): lax.ppermute(value, axis, [(i, (i + by) % size) for i in range(size)])  20.6 us
    pallas_call x1, Pallas kernels, shards(): pl.pallas_call(columns_kernel, grid=(groups,), out_shape=shape((3 * PIV,...  19.8 us
    pallas_call x1, Pallas kernels, shards(): pl.pallas_call(child_kernel, out_shape=(shape((rows_here, 3 * LEAD), bf16...  12.5 us
    pallas_call x1, Pallas kernels, shards(): pl.pallas_call(rows_kernel, grid=(rows_here // tall,), out_shape=(shape((...  10.7 us
  transfers between devices with their start and end apart: 26, of which 17 were waited for; matrix products, arithmetic and copies ran while one was open for 10% of the time, Pallas kernels for 24%

profile of v4, /device:TPU:0, one launch (start us, length us, event | category | flops | bytes accessed | tf_op | source)
XLA Modules:
  0.0 377.5 jit_solution(11460634148265050523)
XLA Ops:
  0.0 5.1 %extract.3 = (f32[512,384]{1,0:T(8,128)}, f32[512,384]{1,0:T(8,128)}) custom-call(f32[2048,32,128]{2,1,0:T(8,128)} %bitcast.97), custom_call_target="tpu_custom_call" | custom-call | flops 1000000 | bytes 14000000 | tf_op jit(solution)/shard_map/extract/pallas_call | solution.py:400
  5.1 2.4 collective-permute-start.2
  7.5 2.6 collective-permute-start.3
  10.2 5.1 %extract.2 = (f32[512,384]{1,0:T(8,128)}, f32[512,384]{1,0:T(8,128)}) custom-call(f32[2048,32,128]{2,1,0:T(8,128)} %bitcast.98), custom_call_target="tpu_custom_call" | custom-call | flops 1000000 | bytes 14000000 | tf_op jit(solution)/shard_map/extract/pallas_call | solution.py:400
  15.3 1.8 collective-permute-start
  17.1 3.6 collective-permute-start.1
  20.7 9.7 %collective-permute-done.1 = f32[512,384]{1,0:T(8,128)S(1)} collective-permute-done((f32[512,384]{1,0:T(8,128)}, f32[512,384]{1,0:T(8,128)S(1)}, u32[]{:S(2)}, u32[]{:S(2)}) %collective-permute-start.1) | collective-permute-done | bytes 786464 | tf_op jit(solution)/shard_map/ppermute | solution.py:419
  30.9 2.1 broadcast_in_dim.179
  32.9 4.9 %all-to-all-start = ((f32[4,512,384]{1,2,0:T(8,128)}), f32[4,512,384]{1,2,0:T(8,128)S(1)}, u32[]{:S(2)}, u32[]{:S(2)}) async-start(f32[4,512,384]{1,2,0:T(8,128)} %broadcast_in_dim.179), calls=%async_computation | async-start | bytes 6291456 | tf_op jit(solution)/shard_map/all_to_all | solution.py:369
  37.8 2.3 slice.89
  40.1 3.4 collective-permute-start.7
  43.5 0.9 slice.88
  44.4 1.3 collective-permute-start.4
  45.7 2.3 fusion.1
  48.0 4.6 %collective-permute-start.10 = (f32[128,1024]{1,0:T(8,128)}, f32[128,1024]{1,0:T(8,128)}, u32[]{:S(2)}, u32[]{:S(2)}) collective-permute-start(f32[128,1024]{1,0:T(8,128)} %get-tuple-element.63), channel_id=1, source_target_pairs={{0,4},{1,5},{2,6},{3,7},{8,12},{9,13},{10,14},{11,15},{16,20},{17,... | collective-permute-start | bytes 1572872 | tf_op jit(solution)/shard_map/ppermute | solution.py:428
  52.6 2.1 collective-permute-start.9
  55.1 2.3 broadcast_select_fusion.3
  57.4 2.3 collective-permute-start.8
  59.7 0.9 broadcast_select_fusion.8
  60.7 1.3 collective-permute-start.5
  63.0 3.8 %collective-permute-start.6 = (f32[384,128]{1,0:T(8,128)S(1)}, f32[384,128]{1,0:T(8,128)S(1)}, u32[]{:S(2)}, u32[]{:S(2)}) collective-permute-start(f32[384,128]{1,0:T(8,128)S(1)} %broadcast_select_fusion.9), channel_id=1, source_target_pairs={{0,4},{1,5},{2,6},{3,7},{8,12},{9,13},{10,14},{11,15},{16,20},{17,... | collective-permute-start | bytes 589832 | tf_op jit(solution)/shard_map/ppermute | solution.py:358
  66.9 2.6 select_add_fusion
  69.5 2.0 collective-permute-done.6
  72.2 2.3 broadcast_select_fusion.4.strip
  74.6 12.5 %child.1 = (bf16[2048,384]{1,0:T(8,128)(2,1)}, bf16[384,1024]{1,0:T(8,128)(2,1)}, f32[4,128,1024]{2,1,0:T(8,128)}) custom-call(s32[8]{0:T(128)} %compare_select_fusion.2.pos, s32[4]{0:T(128)} %live.3, s32[4,32]{1,0:T(4,128)} %quarters.9, f32[384,128]{1,0:T(8,128)} %broadcast_select_fusion.10.corner, f32[2048,128]{1,0:T(8,128)} %broadcast_select_fusion.4.strip, ...), custom_call_target="tpu_custom_call" | custom-call | flops 1000000 | bytes 52500000 | tf_op jit(solution)/shard_map/child/pallas_call | solution.py:432
  87.1 6.1 %all-to-all-done = f32[4,512,384]{1,2,0:T(8,128)S(1)} async-done(((f32[4,512,384]{1,2,0:T(8,128)}), f32[4,512,384]{1,2,0:T(8,128)S(1)}, u32[]{:S(2)}, u32[]{:S(2)}) %all-to-all-start) | async-done | bytes 3145760 | tf_op jit(solution)/shard_map/all_to_all | solution.py:369
  93.2 1.6 copy-done.1
  94.8 3.6 all-to-all-start.1
  98.4 3.5 slice_bitcast_fusion
  102.0 7.1 %collective-permute-start.12 = (f32[512,384]{0,1:T(8,128)}, f32[512,384]{0,1:T(8,128)}, u32[]{:S(2)}, u32[]{:S(2)}) collective-permute-start(f32[512,384]{0,1:T(8,128)} %get-tuple-element.69), channel_id=1, source_target_pairs={{0,4},{4,0},{1,5},{5,1},{2,6},{6,2},{3,7},{7,3},{8,12},{12,8},{9,1... | collective-permute-start | bytes 2359304 | tf_op jit(solution)/shard_map/ppermute | solution.py:365
  109.1 9.5 %outgoing.1 = f32[4,512,1024]{2,1,0:T(8,128)} custom-call(s32[8]{0:T(128)} %compare_select_fusion.2.pos, s32[4]{0:T(128)} %live.3, s32[4,32]{1,0:T(4,128)} %quarters.9, f32[2048,1024]{1,0:T(8,128)} %bitcast.106, bf16[2048,384]{1,0:T(8,128)(2,1)} %get-tuple-element.34.brow3, bf16[384,1024]{1,0:T(8,128)(2,1)} %get-tuple-element.35.bcol3), custom_call_target="tpu_custom_call" | custom-call | flops 1000000 | bytes 35000000 | tf_op jit(solution)/shard_map/outgoing/pallas_call | solution.py:449
  118.6 9.2 %collective-permute-done.12 = f32[512,384]{0,1:T(8,128)} collective-permute-done((f32[512,384]{0,1:T(8,128)}, f32[512,384]{0,1:T(8,128)}, u32[]{:S(2)}, u32[]{:S(2)}) %collective-permute-start.12) | collective-permute-done | bytes 786464 | tf_op jit(solution)/shard_map/ppermute | solution.py:365
  127.8 12.7 %collective-permute-done.11 = f32[512,384]{0,1:T(8,128)S(1)} collective-permute-done((f32[512,384]{0,1:T(8,128)}, f32[512,384]{0,1:T(8,128)S(1)}, u32[]{:S(2)}, u32[]{:S(2)}) %collective-permute-start.11) | collective-permute-done | bytes 786464 | tf_op jit(solution)/shard_map/ppermute | solution.py:365
  140.5 1.2 all-to-all-done.1.refs_1_
  141.7 5.6 %all-to-all-start.2 = ((f32[4,512,1024]{2,1,0:T(8,128)}), f32[4,512,1024]{2,1,0:T(8,128)}, u32[]{:S(2)}, u32[]{:S(2)}) async-start(f32[4,512,1024]{2,1,0:T(8,128)} %outgoing.1), calls=%async_computation.2 | async-start | bytes 16777216 | tf_op jit(solution)/shard_map/all_to_all | solution.py:467
  148.5 9.2 %collective-permute-start.18 = (f32[128,1024]{1,0:T(8,128)S(1)}, f32[128,1024]{1,0:T(8,128)S(1)}, u32[]{:S(2)}, u32[]{:S(2)}) collective-permute-start(f32[128,1024]{1,0:T(8,128)S(1)} %get-tuple-element.71), channel_id=1, source_target_pairs={{0,4},{4,0},{1,5},{5,1},{2,6},{6,2},{3,7},{7,3},{8,12},{12,8},{9,1... | collective-permute-start | bytes 1572872 | tf_op jit(solution)/shard_map/ppermute | solution.py:365
  157.8 1.9 collective-permute-start.16
  160.0 10.4 %collective-permute-done.18.refs_9_ = f32[128,1024]{1,0:T(8,128)S(1)} collective-permute-done((f32[128,1024]{1,0:T(8,128)S(1)}, f32[128,1024]{1,0:T(8,128)S(1)}, u32[]{:S(2)}, u32[]{:S(2)}) %collective-permute-start.18) | collective-permute-done | bytes 524320 | tf_op jit(solution)/shard_map/ppermute | solution.py:365
  170.5 11.2 %collective-permute-done.17.refs_8_ = f32[128,1024]{1,0:T(8,128)S(1)} collective-permute-done((f32[128,1024]{1,0:T(8,128)S(1)}, f32[128,1024]{1,0:T(8,128)S(1)}, u32[]{:S(2)}, u32[]{:S(2)}) %collective-permute-start.17) | collective-permute-done | bytes 524320 | tf_op jit(solution)/shard_map/ppermute | solution.py:365
  181.7 11.2 %collective-permute-done.16.refs_7_ = f32[128,1024]{1,0:T(8,128)S(1)} collective-permute-done((f32[128,1024]{1,0:T(8,128)S(1)}, f32[128,1024]{1,0:T(8,128)S(1)}, u32[]{:S(2)}, u32[]{:S(2)}) %collective-permute-start.16) | collective-permute-done | bytes 524320 | tf_op jit(solution)/shard_map/ppermute | solution.py:365
  192.9 9.7 %collective-permute-done.15.refs_6_ = f32[128,1024]{1,0:T(8,128)S(1)} collective-permute-done((f32[128,1024]{1,0:T(8,128)S(1)}, f32[128,1024]{1,0:T(8,128)S(1)}, u32[]{:S(2)}, u32[]{:S(2)}) %collective-permute-start.15) | collective-permute-done | bytes 524320 | tf_op jit(solution)/shard_map/ppermute | solution.py:365
  203.4 6.1 %collective-permute-start.19 = (f32[384,384]{0,1:T(8,128)S(1)}, f32[384,384]{0,1:T(8,128)S(1)}, u32[]{:S(2)}, u32[]{:S(2)}) collective-permute-start(f32[384,384]{0,1:T(8,128)S(1)} %fusion), channel_id=1, source_target_pairs={{0,2},{4,6},{8,10},{12,14},{16,18},{20,22},{24,26},{28,30}} | collective-permute-start | bytes 1769480 | tf_op jit(solution)/shard_map/ppermute | solution.py:358
  209.6 1.8 collective-permute-start.14
  211.7 5.3 %collective-permute-done.19 = f32[384,384]{0,1:T(8,128)S(1)} collective-permute-done((f32[384,384]{0,1:T(8,128)S(1)}, f32[384,384]{0,1:T(8,128)S(1)}, u32[]{:S(2)}, u32[]{:S(2)}) %collective-permute-start.19) | collective-permute-done | bytes 589856 | tf_op jit(solution)/shard_map/ppermute | solution.py:358
  216.9 0.9 broadcast_select_fusion.5
  217.8 2.1 collective-permute-start.20
  219.9 2.4 copy.7.refs_0_
  222.3 8.1 %collective-permute-done.14 = f32[512,384]{0,1:T(8,128)} collective-permute-done((f32[512,384]{0,1:T(8,128)}, f32[512,384]{0,1:T(8,128)}, u32[]{:S(2)}, u32[]{:S(2)}) %collective-permute-start.14) | collective-permute-done | bytes 786464 | tf_op jit(solution)/shard_map/ppermute | solution.py:365
  230.4 2.3 copy.11.refs_5_
  232.6 6.8 %collective-permute-done.13 = f32[512,384]{0,1:T(8,128)} collective-permute-done((f32[512,384]{0,1:T(8,128)}, f32[512,384]{0,1:T(8,128)}, u32[]{:S(2)}, u32[]{:S(2)}) %collective-permute-start.13) | collective-permute-done | bytes 786464 | tf_op jit(solution)/shard_map/ppermute | solution.py:365
  239.4 2.4 copy.10.refs_4_
  241.8 1.2 copy.8.refs_2_
  243.0 2.3 copy.9.refs_3_
  245.3 6.6 %mine.1 = f32[384,1024]{1,0:T(8,128)} custom-call(s32[8]{0:T(128)} %compare_select_fusion.2.pos, s32[4,32]{1,0:T(4,128)} %quarters.9, f32[4,512,384]{2,1,0:T(8,128)} %copy.7.refs_0_, f32[4,128,1024]{2,1,0:T(8,128)} %copy-done, f32[512,384]{1,0:T(8,128)} %copy.8.refs_2_, f32[512,384]{1,0:T(8,128)} %copy.9.refs_3_, f32[512,384]{1,0:T(8,128)} %copy.10.refs_4_, ...), custom_call_target="tpu_custom_call" | custom-call | flops 1000000 | bytes 21000000 | tf_op jit(solution)/shard_map/mine/pallas_call | solution.py:500
  251.9 1.3 broadcast_select_fusion.6
  253.2 7.1 %collective-permute-start.21 = (f32[384,1024]{1,0:T(8,128)}, f32[384,1024]{1,0:T(8,128)}, u32[]{:S(2)}, u32[]{:S(2)}) collective-permute-start(f32[384,1024]{1,0:T(8,128)} %mine.1), channel_id=1, source_target_pairs={{0,2},{1,3},{6,4},{7,5},{8,10},{9,11},{14,12},{15,13},{16,18},{17,... | collective-permute-start | bytes 4718600 | tf_op jit(solution)/shard_map/ppermute | solution.py:532
  260.3 1.1 copy.12.head
  261.4 26.1 %head.1.inverse = f32[384,384]{1,0:T(8,128)} custom-call(f32[384,384]{1,0:T(8,128)} %copy.12.head), custom_call_target="tpu_custom_call" | custom-call | flops 1000000 | bytes 87500000 | tf_op jit(solution)/shard_map/head/pallas_call | solution.py:511
  287.5 2.7 collective-permute-done.21
  290.6 19.8 %columns.1.lc3 = bf16[1152,4096]{1,0:T(8,128)(2,1)} custom-call(s32[8]{0:T(128)} %compare_select_fusion.2.pos, s32[4,32]{1,0:T(4,128)} %quarters.9, f32[384,384]{1,0:T(8,128)} %head.1.inverse, f32[4,512,384]{2,1,0:T(8,128)} %copy.7.refs_0_, f32[4,128,1024]{2,1,0:T(8,128)} %copy-done, f32[512,384]{1,0:T(8,128)} %copy.8.refs_2_, f32[512,384]{1,0:T(8,128)} %copy.9.refs_3_, ...), custom_call_target="tpu_custom_call" | custom-call | flops 1000000 | bytes 80500000 | tf_op jit(solution)/shard_map/columns/pallas_call | solution.py:549
  310.7 2.0 pad_maximum_fusion.across
  312.7 10.7 %rows.1 = (f32[2048,384]{1,0:T(8,128)}, bf16[2048,1152]{1,0:T(8,128)(2,1)}) custom-call(s32[8]{0:T(128)} %compare_select_fusion.2.pos, f32[384,384]{1,0:T(8,128)} %head.1.inverse, f32[384,2048]{1,0:T(8,128)} %pad_maximum_fusion.across), custom_call_target="tpu_custom_call" | custom-call | flops 1000000 | bytes 42000000 | tf_op jit(solution)/shard_map/rows/pallas_call | solution.py:562
  323.4 6.5 %all-to-all-done.2.incoming = f32[4,512,1024]{2,1,0:T(8,128)} async-done(((f32[4,512,1024]{2,1,0:T(8,128)}), f32[4,512,1024]{2,1,0:T(8,128)}, u32[]{:S(2)}, u32[]{:S(2)}) %all-to-all-start.2) | async-done | bytes 8388640 | tf_op jit(solution)/shard_map/all_to_all | solution.py:467
  329.9 47.4 %final.1 = f32[2048,32,128]{2,1,0:T(8,128)} custom-call(s32[8]{0:T(128)} %compare_select_fusion.2.pos, s32[4,32]{1,0:T(4,128)} %quarters.9, f32[4,512,1024]{2,1,0:T(8,128)} %all-to-all-done.2.incoming, f32[2048,384]{1,0:T(8,128)} %get-tuple-element.51.lr, bf16[2048,1152]{1,0:T(8,128)(2,1)} %get-tuple-element.52.lr3, bf16[1152,4096]{1,0:T(8,128)(2,1)} %columns.1.lc3, ...), custom_call_target="tpu_custom_call" | custom-call | flops 1000000 | bytes 175000000 | tf_op jit(solution)/shard_map/final/pallas_call | solution.py:579
  (68 shorter events, 5.8 us)
Async XLA Ops:
  5.1 15.6 %collective-permute-start.2 = (f32[512,384]{1,0:T(8,128)}, f32[512,384]{1,0:T(8,128)S(1)}, u32[]{:S(2)}, u32[]{:S(2)}) collective-permute-start(f32[512,384]{1,0:T(8,128)} %get-tuple-element.31), channel_id=1, source_target_pairs={{0,1},{4,3},{8,9},{12,11},{16,17},{20,19},{24,25},{28,27}} | collective-permute-start | bytes 2359304 | tf_op jit(solution)/shard_map/ppermute | solution.py:419
  7.5 13.2 %collective-permute-start.3 = (f32[512,384]{1,0:T(8,128)}, f32[512,384]{1,0:T(8,128)S(1)}, u32[]{:S(2)}, u32[]{:S(2)}) collective-permute-start(f32[512,384]{1,0:T(8,128)} %get-tuple-element.32), channel_id=1, source_target_pairs={{0,5},{4,7},{8,13},{12,15},{16,21},{20,23},{24,29},{28,31}} | collective-permute-start | bytes 2359304 | tf_op jit(solution)/shard_map/ppermute | solution.py:419
  15.3 5.4 %collective-permute-start = (f32[512,384]{1,0:T(8,128)}, f32[512,384]{1,0:T(8,128)S(1)}, u32[]{:S(2)}, u32[]{:S(2)}) collective-permute-start(f32[512,384]{1,0:T(8,128)} %get-tuple-element.29), channel_id=1, source_target_pairs={{0,0},{4,2},{8,8},{12,10},{16,16},{20,18},{24,24},{28,26}} | collective-permute-start | bytes 2359304 | tf_op jit(solution)/shard_map/ppermute | solution.py:419
  17.1 13.4 %collective-permute-start.1 = (f32[512,384]{1,0:T(8,128)}, f32[512,384]{1,0:T(8,128)S(1)}, u32[]{:S(2)}, u32[]{:S(2)}) collective-permute-start(f32[512,384]{1,0:T(8,128)} %get-tuple-element.30), channel_id=1, source_target_pairs={{0,4},{4,6},{8,12},{12,14},{16,20},{20,22},{24,28},{28,30}} | collective-permute-start | bytes 2359304 | tf_op jit(solution)/shard_map/ppermute | solution.py:419
  32.9 60.2 %all-to-all-start = ((f32[4,512,384]{1,2,0:T(8,128)}), f32[4,512,384]{1,2,0:T(8,128)S(1)}, u32[]{:S(2)}, u32[]{:S(2)}) async-start(f32[4,512,384]{1,2,0:T(8,128)} %broadcast_in_dim.179), calls=%async_computation | async-start | bytes 6291456 | tf_op jit(solution)/shard_map/all_to_all | solution.py:369
  40.1 15.0 %collective-permute-start.7 = (f32[2048,128]{1,0:T(8,128)}, f32[2048,128]{1,0:T(8,128)}, u32[]{:S(2)}, u32[]{:S(2)}) collective-permute-start(f32[2048,128]{1,0:T(8,128)} %slice.89), channel_id=1, source_target_pairs={{0,2},{4,6},{8,10},{12,14},{16,18},{20,22},{24,26},{28,30}} | collective-permute-start | bytes 3145736 | tf_op jit(solution)/shard_map/ppermute | solution.py:358
  44.4 15.3 %collective-permute-start.4 = (f32[384,128]{1,0:T(8,128)S(1)}, f32[384,128]{1,0:T(8,128)S(1)}, u32[]{:S(2)}, u32[]{:S(2)}) collective-permute-start(f32[384,128]{1,0:T(8,128)S(1)} %slice.88), channel_id=1, source_target_pairs={{0,2},{4,6},{8,10},{12,14},{16,18},{20,22},{24,26},{28,30}} | collective-permute-start | bytes 589832 | tf_op jit(solution)/shard_map/ppermute | solution.py:358
  48.0 18.9 %collective-permute-start.10 = (f32[128,1024]{1,0:T(8,128)}, f32[128,1024]{1,0:T(8,128)}, u32[]{:S(2)}, u32[]{:S(2)}) collective-permute-start(f32[128,1024]{1,0:T(8,128)} %get-tuple-element.63), channel_id=1, source_target_pairs={{0,4},{1,5},{2,6},{3,7},{8,12},{9,13},{10,14},{11,15},{16,20},{17,... | collective-permute-start | bytes 1572872 | tf_op jit(solution)/shard_map/ppermute | solution.py:428
  52.6 14.3 %collective-permute-start.9 = (f32[128,1024]{1,0:T(8,128)}, f32[128,1024]{1,0:T(8,128)}, u32[]{:S(2)}, u32[]{:S(2)}) collective-permute-start(f32[128,1024]{1,0:T(8,128)} %get-tuple-element.64), channel_id=1, source_target_pairs={{0,4},{1,5},{2,6},{3,7},{8,12},{9,13},{10,14},{11,15},{16,20},{17,... | collective-permute-start | bytes 1572872 | tf_op jit(solution)/shard_map/ppermute | solution.py:358
  57.4 14.8 %collective-permute-start.8 = (f32[2048,128]{1,0:T(8,128)}, f32[2048,128]{1,0:T(8,128)}, u32[]{:S(2)}, u32[]{:S(2)}) collective-permute-start(f32[2048,128]{1,0:T(8,128)} %broadcast_select_fusion.3), channel_id=1, source_target_pairs={{0,1},{2,3},{4,5},{6,7},{8,9},{10,11},{12,13},{14,15},{16,17},{18,... | collective-permute-start | bytes 3145736 | tf_op jit(solution)/shard_map/ppermute | solution.py:358
  60.7 2.4 collective-permute-start.5
  63.0 8.5 %collective-permute-start.6 = (f32[384,128]{1,0:T(8,128)S(1)}, f32[384,128]{1,0:T(8,128)S(1)}, u32[]{:S(2)}, u32[]{:S(2)}) collective-permute-start(f32[384,128]{1,0:T(8,128)S(1)} %broadcast_select_fusion.9), channel_id=1, source_target_pairs={{0,4},{1,5},{2,6},{3,7},{8,12},{9,13},{10,14},{11,15},{16,20},{17,... | collective-permute-start | bytes 589832 | tf_op jit(solution)/shard_map/ppermute | solution.py:358
  93.2 1.6 copy-start.1
  94.8 46.8 %all-to-all-start.1 = ((f32[4,128,1024]{2,1,0:T(8,128)}), f32[4,128,1024]{2,1,0:T(8,128)S(1)}, u32[]{:S(2)}, u32[]{:S(2)}) async-start(f32[4,128,1024]{2,1,0:T(8,128)} %get-tuple-element.41), calls=%async_computation.1 | async-start | bytes 4194304 | tf_op jit(solution)/shard_map/all_to_all | solution.py:462
  102.0 25.9 %collective-permute-start.12 = (f32[512,384]{0,1:T(8,128)}, f32[512,384]{0,1:T(8,128)}, u32[]{:S(2)}, u32[]{:S(2)}) collective-permute-start(f32[512,384]{0,1:T(8,128)} %get-tuple-element.69), channel_id=1, source_target_pairs={{0,4},{4,0},{1,5},{5,1},{2,6},{6,2},{3,7},{7,3},{8,12},{12,8},{9,1... | collective-permute-start | bytes 2359304 | tf_op jit(solution)/shard_map/ppermute | solution.py:365
  109.1 31.4 %collective-permute-start.11 = (f32[512,384]{0,1:T(8,128)}, f32[512,384]{0,1:T(8,128)S(1)}, u32[]{:S(2)}, u32[]{:S(2)}) collective-permute-start(f32[512,384]{0,1:T(8,128)} %get-tuple-element.70), channel_id=1, source_target_pairs={{0,4},{4,0},{1,5},{5,1},{2,6},{6,2},{3,7},{7,3},{8,12},{12,8},{9,1... | collective-permute-start | bytes 2359304 | tf_op jit(solution)/shard_map/ppermute | solution.py:365
  118.6 28.7 %copy-start.11 = (s32[4,32]{1,0:T(4,128)S(1)}, s32[4,32]{1,0:T(4,128)}, u32[]{:S(2)}) copy-start(s32[4,32]{1,0:T(4,128)} %quarters.9) | copy-start | bytes 1540
  140.5 1.2 copy-start.8
  141.7 6.6 %copy-start = (f32[4,128,1024]{2,1,0:T(8,128)}, f32[4,128,1024]{2,1,0:T(8,128)S(1)}, u32[]{:S(2)}) copy-start(f32[4,128,1024]{2,1,0:T(8,128)S(1)} %all-to-all-done.1.refs_1_) | copy-start | bytes 6291460
  141.7 188.2 %all-to-all-start.2 = ((f32[4,512,1024]{2,1,0:T(8,128)}), f32[4,512,1024]{2,1,0:T(8,128)}, u32[]{:S(2)}, u32[]{:S(2)}) async-start(f32[4,512,1024]{2,1,0:T(8,128)} %outgoing.1), calls=%async_computation.2 | async-start | bytes 16777216 | tf_op jit(solution)/shard_map/all_to_all | solution.py:467
  148.5 54.6 %copy-start.2 = (f32[4,512,384]{1,2,0:T(8,128)S(1)}, f32[4,512,384]{1,2,0:T(8,128)}, u32[]{:S(2)}) copy-start(f32[4,512,384]{1,2,0:T(8,128)} %copy-done.1) | copy-start | bytes 9437188
  148.5 54.6 %copy-start.9 = (f32[512,384]{0,1:T(8,128)S(1)}, f32[512,384]{0,1:T(8,128)}, u32[]{:S(2)}) copy-start(f32[512,384]{0,1:T(8,128)} %copy-done.8) | copy-start | bytes 2359300
  148.5 22.0 %collective-permute-start.18 = (f32[128,1024]{1,0:T(8,128)S(1)}, f32[128,1024]{1,0:T(8,128)S(1)}, u32[]{:S(2)}, u32[]{:S(2)}) collective-permute-start(f32[128,1024]{1,0:T(8,128)S(1)} %get-tuple-element.71), channel_id=1, source_target_pairs={{0,4},{4,0},{1,5},{5,1},{2,6},{6,2},{3,7},{7,3},{8,12},{12,8},{9,1... | collective-permute-start | bytes 1572872 | tf_op jit(solution)/shard_map/ppermute | solution.py:365
  157.7 24.0 %collective-permute-start.17 = (f32[128,1024]{1,0:T(8,128)S(1)}, f32[128,1024]{1,0:T(8,128)S(1)}, u32[]{:S(2)}, u32[]{:S(2)}) collective-permute-start(f32[128,1024]{1,0:T(8,128)S(1)} %get-tuple-element.72), channel_id=1, source_target_pairs={{0,4},{4,0},{1,5},{5,1},{2,6},{6,2},{3,7},{7,3},{8,12},{12,8},{9,1... | collective-permute-start | bytes 1572872 | tf_op jit(solution)/shard_map/ppermute | solution.py:365
  157.8 35.2 %collective-permute-start.16 = (f32[128,1024]{1,0:T(8,128)S(1)}, f32[128,1024]{1,0:T(8,128)S(1)}, u32[]{:S(2)}, u32[]{:S(2)}) collective-permute-start(f32[128,1024]{1,0:T(8,128)S(1)} %get-tuple-element.73), channel_id=1, source_target_pairs={{0,4},{4,0},{1,5},{5,1},{2,6},{6,2},{3,7},{7,3},{8,12},{12,8},{9,1... | collective-permute-start | bytes 1572872 | tf_op jit(solution)/shard_map/ppermute | solution.py:365
  159.7 42.9 %collective-permute-start.15 = (f32[128,1024]{1,0:T(8,128)S(1)}, f32[128,1024]{1,0:T(8,128)S(1)}, u32[]{:S(2)}, u32[]{:S(2)}) collective-permute-start(f32[128,1024]{1,0:T(8,128)S(1)} %get-tuple-element.74), channel_id=1, source_target_pairs={{0,4},{4,0},{1,5},{5,1},{2,6},{6,2},{3,7},{7,3},{8,12},{12,8},{9,1... | collective-permute-start | bytes 1572872 | tf_op jit(solution)/shard_map/ppermute | solution.py:365
  170.5 32.8 %copy-start.4 = (f32[128,1024]{1,0:T(8,128)}, f32[128,1024]{1,0:T(8,128)S(1)}, u32[]{:S(2)}) copy-start(f32[128,1024]{1,0:T(8,128)S(1)} %collective-permute-done.18.refs_9_) | copy-start | bytes 1572868
  181.7 21.5 %copy-start.5 = (f32[128,1024]{1,0:T(8,128)}, f32[128,1024]{1,0:T(8,128)S(1)}, u32[]{:S(2)}) copy-start(f32[128,1024]{1,0:T(8,128)S(1)} %collective-permute-done.17.refs_8_) | copy-start | bytes 1572868
  192.9 10.3 %copy-start.6 = (f32[128,1024]{1,0:T(8,128)}, f32[128,1024]{1,0:T(8,128)S(1)}, u32[]{:S(2)}) copy-start(f32[128,1024]{1,0:T(8,128)S(1)} %collective-permute-done.16.refs_7_) | copy-start | bytes 1572868
  202.6 0.8 copy-start.7
  203.4 13.5 %collective-permute-start.19 = (f32[384,384]{0,1:T(8,128)S(1)}, f32[384,384]{0,1:T(8,128)S(1)}, u32[]{:S(2)}, u32[]{:S(2)}) collective-permute-start(f32[384,384]{0,1:T(8,128)S(1)} %fusion), channel_id=1, source_target_pairs={{0,2},{4,6},{8,10},{12,14},{16,18},{20,22},{24,26},{28,30}} | collective-permute-start | bytes 1769480 | tf_op jit(solution)/shard_map/ppermute | solution.py:358
  209.6 20.8 %collective-permute-start.14 = (f32[512,384]{0,1:T(8,128)}, f32[512,384]{0,1:T(8,128)}, u32[]{:S(2)}, u32[]{:S(2)}) collective-permute-start(f32[512,384]{0,1:T(8,128)} %get-tuple-element.67), channel_id=1, source_target_pairs={{0,4},{4,0},{1,5},{5,1},{2,6},{6,2},{3,7},{7,3},{8,12},{12,8},{9,1... | collective-permute-start | bytes 2359304 | tf_op jit(solution)/shard_map/ppermute | solution.py:365
  211.4 28.1 %collective-permute-start.13 = (f32[512,384]{0,1:T(8,128)}, f32[512,384]{0,1:T(8,128)}, u32[]{:S(2)}, u32[]{:S(2)}) collective-permute-start(f32[512,384]{0,1:T(8,128)} %get-tuple-element.68), channel_id=1, source_target_pairs={{0,4},{4,0},{1,5},{5,1},{2,6},{6,2},{3,7},{7,3},{8,12},{12,8},{9,1... | collective-permute-start | bytes 2359304 | tf_op jit(solution)/shard_map/ppermute | solution.py:365
  217.8 34.1 %collective-permute-start.20 = (f32[384,384]{0,1:T(8,128)}, f32[384,384]{0,1:T(8,128)}, u32[]{:S(2)}, u32[]{:S(2)}) collective-permute-start(f32[384,384]{0,1:T(8,128)} %broadcast_select_fusion.5), channel_id=1, source_target_pairs={{0,1},{2,3},{4,5},{6,7},{8,9},{10,11},{12,13},{14,15},{16,17},{18,... | collective-permute-start | bytes 1769480 | tf_op jit(solution)/shard_map/ppermute | solution.py:358
  222.3 19.5 %copy-start.10 = (f32[512,384]{0,1:T(8,128)S(1)}, f32[512,384]{0,1:T(8,128)}, u32[]{:S(2)}) copy-start(f32[512,384]{0,1:T(8,128)} %copy-done.8) | copy-start | bytes 2359300
  251.9 38.3 %copy-start.3 = (f32[384,1024]{1,0:T(8,128)S(1)}, f32[384,1024]{1,0:T(8,128)}, u32[]{:S(2)}) copy-start(f32[384,1024]{1,0:T(8,128)} %mine.1) | copy-start | bytes 4718596
  253.2 37.0 %collective-permute-start.21 = (f32[384,1024]{1,0:T(8,128)}, f32[384,1024]{1,0:T(8,128)}, u32[]{:S(2)}, u32[]{:S(2)}) collective-permute-start(f32[384,1024]{1,0:T(8,128)} %mine.1), channel_id=1, source_target_pairs={{0,2},{1,3},{6,4},{7,5},{8,10},{9,11},{14,12},{15,13},{16,18},{17,... | collective-permute-start | bytes 4718600 | tf_op jit(solution)/shard_map/ppermute | solution.py:532
  290.5 19.9 %collective-permute-start.22 = (f32[384,1024]{1,0:T(8,128)S(1)}, f32[384,1024]{1,0:T(8,128)S(1)}, u32[]{:S(2)}, u32[]{:S(2)}) collective-permute-start(f32[384,1024]{1,0:T(8,128)S(1)} %broadcast_select_fusion.1), channel_id=1, source_target_pairs={{0,1},{1,0},{2,3},{3,2},{4,5},{5,4},{6,7},{7,6},{8,9},{9,8},{10,11... | collective-permute-start | bytes 4718600 | tf_op jit(solution)/shard_map/ppermute | solution.py:540
